TPU v7x, 32 devices: a whole 2x2x4 slice. The times are simulated.
32 devices in a mesh: img: 8 (over z, x), band: 2 (over y), head: 2 (over core).
Axes of the slice: x: 2, y: 2, z: 4, core: 2. Of those that a mesh axis runs over, the one named last changes fastest.
Arguments:
- tokens: bfloat16 [8, 16, 16, 1152], P('img', 'band'), may hold values from -6 to 6
- timesteps: int32 [8], P('img'), may hold values from 0 to 999
- first_gain: float32 [1152], replicated, may hold values from 0.5 to 1.5
- first_shift: float32 [1152], replicated, may hold values from -3 to 3
- project_in: bfloat16 [1152, 3, 1152], P(None, None, 'head'), may hold values from -0.1875 to 0.1875
- time_weight: bfloat16 [1152, 2, 1152], P(None, None, 'head'), may hold values from -0.1875 to 0.1875
- bias_table: float32 [16, 25], P('head'), may hold values from -4 to 4
- bias_index: int32 [25], replicated, may hold values from 0 to 24, each once
- project_out: bfloat16 [1152, 1152], P('head'), may hold values from -0.875 to 0.875
- out_shift: float32 [1152], replicated, may hold values from -3 to 3
- second_gain: float32 [1152], replicated, may hold values from 0.5 to 1.5
- second_shift: float32 [1152], replicated, may hold values from -3 to 3
- up_weight: bfloat16 [1152, 4608], P(None, 'head'), may hold values from -0.1875 to 0.1875
- up_shift: float32 [4608], P('head'), may hold values from -3 to 3
- down_weight: bfloat16 [4608, 1152], P('head'), may hold values from -0.09375 to 0.09375
- down_shift: float32 [1152], replicated, may hold values from -3 to 3
- cotangent: bfloat16 [8, 16, 16, 1152], P('img', 'band'), may hold values from -6 to 6
Outputs:
- output: bfloat16 [8, 16, 16, 1152], P('img', 'band')
- tokens_grad: float32 [8, 16, 16, 1152], P('img', 'band')
- first_gain_grad: float32 [1152], replicated
- first_shift_grad: float32 [1152], replicated
- project_in_grad: float32 [1152, 3, 1152], P(('img', 'band'), None, 'head')
- time_weight_grad: float32 [1152, 2, 1152], P(('img', 'band'), None, 'head')
- bias_table_grad: float32 [16, 25], P('head')
- project_out_grad: float32 [1152, 1152], P('head', ('img', 'band'))
- out_shift_grad: float32 [1152], replicated
- second_gain_grad: float32 [1152], replicated
- second_shift_grad: float32 [1152], replicated
- up_weight_grad: float32 [1152, 4608], P(('img', 'band'), 'head')
- up_shift_grad: float32 [4608], P('head')
- down_weight_grad: float32 [4608, 1152], P('head', ('img', 'band'))
- down_shift_grad: float32 [1152], replicated
Inputs may be any that keep to these rules, and one draw needn't show every extreme that they name: `bias_index`: each entry of the table appears exactly once.
All inputs are finite; a program needn't handle non-finite values.
Results may differ from a plain program's by a relative error of at most 0.014.
Values may be sent and summed in bfloat16 or wider, within the bound.
A program may use at most 256 MiB of HBM per device.

v0:
```python
import math

import jax
import jax.numpy as jnp
from jax import lax
from jax.sharding import PartitionSpec as P

HD = 72
ROWS = 16
COLS = 16
WIN = 5


epsilon = 1e-05
highest = lax.Precision.HIGHEST
masked_score = -1000000000.0


def padded_2(cells, sides, width):
    for axis, dim in sides:
        count = lax.axis_size(axis)
        ends = count - 1
        head = lax.slice_in_dim(cells, 0, width, axis=dim)
        tail = lax.slice_in_dim(cells, cells.shape[dim] - width, cells.shape[dim], axis=dim)
        cells = jnp.concatenate(
            [
                lax.ppermute(tail, axis, [(i, (i + 1) % count) for i in range(ends)]),
                cells,
                lax.ppermute(head, axis, [((i + 1) % count, i) for i in range(ends)]),
            ],
            axis=dim,
        )
    return cells


def from_behind(block, axis, distance):
    devices = range(lax.axis_size(axis))
    route = [(i - distance, i) for i in devices if i - distance in devices]
    return lax.ppermute(block, axis, route)


def layer_norm(values, gain, shift):
    center = values - jnp.mean(values, axis=-1, keepdims=True)
    spread = jnp.mean(center * center, axis=-1, keepdims=True)
    return center * lax.rsqrt(spread + epsilon) * gain + shift


def gelu_tanh(values):
    return jax.nn.gelu(values, approximate=True)


def time_features(timesteps, width):
    half = width // 2
    freqs = jnp.exp(jnp.arange(half, dtype=jnp.float32) * (-math.log(10000.0) / half))
    angles = timesteps.astype(jnp.float32)[:, None] * freqs[None, :]
    return jnp.concatenate([jnp.cos(angles), jnp.sin(angles)], axis=1)


def window_valid(row_start, row_count, column_count):
    reach = WIN // 2
    global_rows = row_start + jnp.arange(row_count, dtype=jnp.int32)
    columns = jnp.arange(column_count, dtype=jnp.int32)
    masks = []
    for tap in range(WIN * WIN):
        row_step = tap // WIN - reach
        col_step = tap % WIN - reach
        row_ok = (global_rows + row_step >= 0) & (global_rows + row_step < ROWS)
        col_ok = (columns + col_step >= 0) & (columns + col_step < COLS)
        masks.append(row_ok[:, None] & col_ok[None, :])
    return jnp.stack(masks, axis=-1)


def on_device(
    tokens,
    timesteps,
    first_gain,
    first_shift,
    project_in,
    time_weight,
    bias_table,
    bias_index,
    project_out,
    out_shift,
    second_gain,
    second_shift,
    up_weight,
    up_shift,
    down_weight,
    down_shift,
    cotangent,
):
    batch, band_rows, column_count, width = tokens.shape
    local_width = project_in.shape[2]
    local_heads = bias_table.shape[0]
    reach = WIN // 2
    taps = WIN * WIN
    score_scale = HD ** (-0.5)
    valid = window_valid(lax.axis_index("band") * band_rows, band_rows, column_count)
    selector = (bias_index[:, None] == jnp.arange(taps, dtype=jnp.int32)[None, :]).astype(
        jnp.float32
    )
    tap_bias = jnp.dot(bias_table, jnp.transpose(selector), precision=highest)

    def heads_view(values):
        return values.reshape(batch, band_rows, column_count, local_heads, HD)

    def tap_view(padded, tap):
        row_at = tap // WIN
        col_at = tap % WIN
        return heads_view(
            padded[:, row_at : row_at + band_rows, col_at : col_at + column_count]
        ).astype(jnp.float32)

    inputs = tokens.astype(jnp.float32)
    first_norm, first_pull = jax.vjp(layer_norm, inputs, first_gain, first_shift)
    first_low = first_norm.astype(jnp.bfloat16)
    mixed = jnp.einsum("brcd,dke->brcke", first_low, project_in, preferred_element_type=jnp.float32)
    time_low = time_features(timesteps, width).astype(jnp.bfloat16)
    time_proj = jnp.einsum("bd,dke->bke", time_low, time_weight, preferred_element_type=jnp.float32)
    query_low = (mixed[..., 0, :] + time_proj[:, None, None, 0, :]).astype(jnp.bfloat16)
    key_low = mixed[..., 1, :].astype(jnp.bfloat16)
    value_low = (mixed[..., 2, :] + time_proj[:, None, None, 1, :]).astype(jnp.bfloat16)
    pair = jnp.stack([key_low, value_low], axis=3)
    extended = padded_2(pair, (("band", 1),), reach)
    extended = jnp.pad(extended, ((0, 0), (0, 0), (reach, reach), (0, 0), (0, 0)))
    key_padded = extended[..., 0, :]
    value_padded = extended[..., 1, :]
    query_heads = heads_view(query_low.astype(jnp.float32))

    def tap_scores(tap):
        raw = (
            jnp.sum(query_heads * tap_view(key_padded, tap), axis=-1) * score_scale
            + tap_bias[:, tap]
        )
        return jnp.where(valid[None, :, :, tap, None], raw, masked_score)

    scores = jnp.stack([tap_scores(tap) for tap in range(taps)], axis=-1)
    top = jnp.max(scores, axis=-1, keepdims=True)
    weights = jnp.exp(scores - top)
    total = jnp.sum(weights, axis=-1, keepdims=True)
    probs = weights / total
    log_total = (top + jnp.log(total))[..., 0]
    attended_heads = jnp.zeros(query_heads.shape, jnp.float32)
    for tap in range(taps):
        attended_heads = attended_heads + probs[..., tap, None] * tap_view(value_padded, tap)
    attended_low = attended_heads.reshape(batch, band_rows, column_count, local_width).astype(
        jnp.bfloat16
    )
    projected = jnp.einsum(
        "brce,ed->brcd", attended_low, project_out, preferred_element_type=jnp.float32
    )
    projected = lax.psum(projected, "head")
    resid = inputs + projected + out_shift
    second_norm, second_pull = jax.vjp(layer_norm, resid, second_gain, second_shift)
    second_low = second_norm.astype(jnp.bfloat16)
    upper = (
        jnp.einsum("brcd,df->brcf", second_low, up_weight, preferred_element_type=jnp.float32)
        + up_shift
    )
    active, gelu_pull = jax.vjp(gelu_tanh, upper)
    active_low = active.astype(jnp.bfloat16)
    lowered = jnp.einsum(
        "brcf,fd->brcd", active_low, down_weight, preferred_element_type=jnp.float32
    )
    lowered = lax.psum(lowered.astype(jnp.bfloat16), "head").astype(jnp.float32)
    output = (resid + lowered + down_shift).astype(jnp.bfloat16)
    cot_full = cotangent.astype(jnp.float32)
    down_shift_grad = jnp.sum(cot_full, axis=(0, 1, 2))
    down_weight_grad = jnp.einsum(
        "brcf,brcd->fd", active_low, cotangent, preferred_element_type=jnp.float32
    )
    active_grad = jnp.einsum(
        "brcd,fd->brcf", cotangent, down_weight, preferred_element_type=jnp.float32
    )
    (upper_grad,) = gelu_pull(active_grad)
    up_shift_grad = jnp.sum(upper_grad, axis=(0, 1, 2))
    upper_low = upper_grad.astype(jnp.bfloat16)
    up_weight_grad = jnp.einsum(
        "brcd,brcf->df", second_low, upper_low, preferred_element_type=jnp.float32
    )
    second_back = jnp.einsum(
        "brcf,df->brcd", upper_low, up_weight, preferred_element_type=jnp.float32
    )
    second_back = lax.psum(second_back.astype(jnp.bfloat16), "head").astype(jnp.float32)
    resid_part, second_gain_grad, second_shift_grad = second_pull(second_back)
    resid_grad = cot_full + resid_part
    out_shift_grad = jnp.sum(resid_grad, axis=(0, 1, 2))
    resid_low = resid_grad.astype(jnp.bfloat16)
    project_out_grad = jnp.einsum(
        "brce,brcd->ed", attended_low, resid_low, preferred_element_type=jnp.float32
    )
    attended_grad = heads_view(
        jnp.einsum("brcd,ed->brce", resid_low, project_out, preferred_element_type=jnp.float32)
    )
    delta = jnp.sum(attended_grad * attended_heads, axis=-1)
    query_grad = jnp.zeros(query_heads.shape, jnp.float32)
    key_pad_grad = jnp.zeros(key_padded.shape, jnp.float32)
    value_pad_grad = jnp.zeros(value_padded.shape, jnp.float32)
    bias_columns = []
    for tap in range(taps):
        row_at = tap // WIN
        col_at = tap % WIN
        key_tap = tap_view(key_padded, tap)
        prob = jnp.exp(tap_scores(tap) - log_total)
        prob_grad = jnp.sum(attended_grad * tap_view(value_padded, tap), axis=-1)
        score_grad = prob * (prob_grad - delta)
        bias_columns.append(jnp.sum(score_grad, axis=(0, 1, 2)))
        score_grad = score_grad * score_scale
        query_grad = query_grad + score_grad[..., None] * key_tap
        key_term = (score_grad[..., None] * query_heads).reshape(
            batch, band_rows, column_count, local_width
        )
        value_term = (prob[..., None] * attended_grad).reshape(
            batch, band_rows, column_count, local_width
        )
        key_pad_grad = key_pad_grad.at[
            :, row_at : row_at + band_rows, col_at : col_at + column_count
        ].add(key_term)
        value_pad_grad = value_pad_grad.at[
            :, row_at : row_at + band_rows, col_at : col_at + column_count
        ].add(value_term)
    bias_grad = jnp.stack(bias_columns, axis=1)
    bias_table_grad = jnp.dot(bias_grad, selector, precision=highest)
    pair_grad = jnp.stack([key_pad_grad, value_pad_grad], axis=3)[
        :, :, reach : reach + column_count
    ]
    from_below = from_behind(pair_grad[:, :reach].astype(jnp.bfloat16), "band", -1).astype(
        jnp.float32
    )
    from_above = from_behind(
        pair_grad[:, reach + band_rows :].astype(jnp.bfloat16), "band", 1
    ).astype(jnp.float32)
    own_grad = pair_grad[:, reach : reach + band_rows]
    own_grad = own_grad.at[:, band_rows - reach :].add(from_below)
    own_grad = own_grad.at[:, :reach].add(from_above)
    query_low_grad = query_grad.reshape(batch, band_rows, column_count, local_width).astype(
        jnp.bfloat16
    )
    key_low_grad = own_grad[..., 0, :].astype(jnp.bfloat16)
    value_low_grad = own_grad[..., 1, :].astype(jnp.bfloat16)
    time_sums = jnp.stack(
        [
            jnp.sum(query_low_grad.astype(jnp.float32), axis=(1, 2)),
            jnp.sum(value_low_grad.astype(jnp.float32), axis=(1, 2)),
        ],
        axis=1,
    )
    time_weight_grad = jnp.einsum(
        "bd,bke->dke", time_low.astype(jnp.float32), time_sums, precision=highest
    )
    stacked_grad = jnp.stack([query_low_grad, key_low_grad, value_low_grad], axis=3)
    project_in_grad = jnp.einsum(
        "brcd,brcke->dke", first_low, stacked_grad, preferred_element_type=jnp.float32
    )
    first_back = jnp.einsum(
        "brcke,dke->brcd", stacked_grad, project_in, preferred_element_type=jnp.float32
    )
    first_back = lax.psum(first_back.astype(jnp.bfloat16), "head").astype(jnp.float32)
    input_part, first_gain_grad, first_shift_grad = first_pull(first_back)
    tokens_grad = resid_grad + input_part
    project_in_share, time_weight_share, project_out_share, up_weight_share, down_weight_share = (
        lax.psum_scatter(project_in_grad, ("img", "band"), scatter_dimension=0, tiled=True),
        lax.psum_scatter(time_weight_grad, ("img", "band"), scatter_dimension=0, tiled=True),
        lax.psum_scatter(project_out_grad, ("img", "band"), scatter_dimension=1, tiled=True),
        lax.psum_scatter(up_weight_grad, ("img", "band"), scatter_dimension=0, tiled=True),
        lax.psum_scatter(down_weight_grad, ("img", "band"), scatter_dimension=1, tiled=True),
    )
    sums = lax.psum(
        (
            first_gain_grad,
            first_shift_grad,
            bias_table_grad,
            out_shift_grad,
            second_gain_grad,
            second_shift_grad,
            up_shift_grad,
            down_shift_grad,
        ),
        ("img", "band"),
    )
    return (
        output,
        tokens_grad,
        sums[0],
        sums[1],
        project_in_share,
        time_weight_share,
        sums[2],
        project_out_share,
        sums[3],
        sums[4],
        sums[5],
        up_weight_share,
        sums[6],
        down_weight_share,
        sums[7],
    )


def solution(mesh):
    return jax.shard_map(
        on_device,
        mesh=mesh,
        in_specs=(
            P("img", "band", None, None),
            P("img"),
            P(),
            P(),
            P(None, None, "head"),
            P(None, None, "head"),
            P("head", None),
            P(),
            P("head", None),
            P(),
            P(),
            P(),
            P(None, "head"),
            P("head"),
            P("head", None),
            P(),
            P("img", "band", None, None),
        ),
        out_specs=(
            P("img", "band", None, None),
            P("img", "band", None, None),
            P(),
            P(),
            P(("img", "band"), None, "head"),
            P(("img", "band"), None, "head"),
            P("head", None),
            P("head", ("img", "band")),
            P(),
            P(),
            P(),
            P(("img", "band"), "head"),
            P("head"),
            P("head", ("img", "band")),
            P(),
        ),
        check_vma=False,
    )
```

profile of v0, /device:TPU:0, one launch (start us, length us, event | category | flops | bytes accessed | tf_op | source)
XLA Modules:
  0.0 1525.0 jit_solution(417973600825948013)
XLA Ops:
  17.7 4.9 collective-permute-start
  77.5 6.5 fusion.98
  119.6 4.2 add_convert_fusion.4
  175.1 5.3 fusion.224
  183.1 4.3 fusion.27
  187.4 15.6 %all-reduce.14.cloned.1.call-done = bf16[1,8,16,1152]{3,2,1,0:T(8,128)(2,1)} async-done(((bf16[1,8,16,1152]{3,2,1,0:T(8,128)(2,1)}), bf16[1,8,16,1152]{3,2,1,0:T(8,128)(2,1)}) %all-reduce.14.cloned.1.call-update) | async-done | bytes 294928 | tf_op jit(solution)/shard_map/psum | solution.py:184
  213.9 8.9 multiply_reduce_fusion.25
  244.4 6.0 scatter-add.175
  252.2 5.4 scatter-add.176
  263.3 6.0 scatter-add.179
  276.9 6.0 scatter-add.180
  311.8 4.4 scatter-add.184
  318.0 4.8 scatter-add.185
  324.6 4.4 scatter-add.186
  330.7 4.4 scatter-add.189
  347.0 4.2 scatter-add.194
  441.0 4.8 convert_reduce_fusion.5
  455.0 5.6 scatter-add.216
  462.4 5.6 scatter-add.219
  472.2 5.5 scatter-add.220
  482.1 5.6 scatter-add.221
  595.2 4.6 collective-permute-start.3
  603.6 5.4 broadcast_multiply_fusion
  613.0 5.5 convolution_bitcast_fusion.2
  619.6 5.7 convolution_bitcast_fusion.1
  626.6 5.4 convolution_bitcast_fusion
  639.1 81.3 %all-reduce.5 = (f32[1152]{0:T(1024)}, f32[1152]{0:T(1024)}, f32[8,25]{1,0:T(8,128)}, f32[1152]{0:T(1024)}, f32[1152]{0:T(1024)}, /*index=5*/f32[1152]{0:T(1024)}, f32[2304]{0:T(1024)}, f32[1152]{0:T(1024)}) all-reduce(f32[1152]{0:T(1024)S(1)} %get-tuple-element.641, ...), channel_id=1, replica_groups=mesh['img'=8,'band'=2,'head'=2] {'img','band'}, use_global_device_ids=true, to_apply=%region_68.69 | all-reduce | flops 9416 | bytes 75328 | tf_op jit(solution)/shard_map/psum | solution.py:268
  724.6 110.8 %all-reduce.16.cloned.1.call-done = f32[1152,2,576]{2,1,0:T(2,128)} async-done(((f32[1152,2,576]{2,1,0:T(2,128)}), f32[1152,2,576]{2,1,0:T(2,128)}) %all-reduce.16.cloned.1.call-update) | async-done | bytes 5308432
  837.2 132.7 %reduce-scatter.13.cloned.1.call-done = f32[576,72]{0,1:T(8,128)} async-done(((f32[576,1152]{0,1:T(8,128)}), f32[576,72]{0,1:T(8,128)}) %reduce-scatter.13.cloned.1.call-update) | async-done | bytes 165904
  969.9 172.4 %reduce-scatter.7.cloned.1.call-done = f32[72,3,576]{2,0,1:T(8,128)} async-done(((f32[1152,3,576]{2,0,1:T(8,128)}), f32[72,3,576]{2,0,1:T(8,128)}) %reduce-scatter.7.cloned.1.call-update) | async-done | bytes 497680 | tf_op jit(solution)/shard_map/reduce_scatter | solution.py:262
  1142.3 186.7 %reduce-scatter.9.cloned.1.call-done = f32[72,2304]{1,0:T(8,128)} async-done(((f32[1152,2304]{1,0:T(8,128)}), f32[72,2304]{1,0:T(8,128)}) %reduce-scatter.9.cloned.1.call-update) | async-done | bytes 663568 | tf_op jit(solution)/shard_map/reduce_scatter | solution.py:265
  1329.0 188.8 %reduce-scatter.11.cloned.1.call-done = f32[2304,72]{0,1:T(8,128)} async-done(((f32[2304,1152]{0,1:T(8,128)}), f32[2304,72]{0,1:T(8,128)}) %reduce-scatter.11.cloned.1.call-update) | async-done | bytes 663568 | tf_op jit(solution)/shard_map/reduce_scatter | solution.py:266
  (1078 shorter events, 482.1 us)
Async XLA Ops:
  7.2 162.7 %all-reduce.12.cloned.1.call-start = ((), (), s32[]{:S(2)}) async-start(), calls=%async_computation.4 | async-start | bytes 1179648 | tf_op jit(solution)/shard_map/psum | solution.py:152
  16.2 13.8 copy-start.39
  16.4 13.6 collective-permute-start.1
  17.7 12.3 collective-permute-start
  29.3 59.8 %copy-start.212 = (pred[8,16]{1,0:T(8,128)(4,1)}, pred[8,16]{1,0:T(8,128)(4,1)S(1)}, u32[]{:S(2)}) copy-start(pred[8,16]{1,0:T(8,128)(4,1)S(1)} %get-tuple-element.918) | copy-start | bytes 388
  29.3 59.8 %copy-start.214 = (pred[8,16]{1,0:T(8,128)(4,1)}, pred[8,16]{1,0:T(8,128)(4,1)S(1)}, u32[]{:S(2)}) copy-start(pred[8,16]{1,0:T(8,128)(4,1)S(1)} %get-tuple-element.922) | copy-start | bytes 388
  29.3 59.8 %copy-start.216 = (pred[8,16]{1,0:T(8,128)(4,1)}, pred[8,16]{1,0:T(8,128)(4,1)S(1)}, u32[]{:S(2)}) copy-start(pred[8,16]{1,0:T(8,128)(4,1)S(1)} %get-tuple-element.923) | copy-start | bytes 388
  29.4 61.2 %copy-start.210 = (pred[8,16]{1,0:T(8,128)(4,1)}, pred[8,16]{1,0:T(8,128)(4,1)S(1)}, u32[]{:S(2)}) copy-start(pred[8,16]{1,0:T(8,128)(4,1)S(1)} %get-tuple-element.917) | copy-start | bytes 388
  91.7 14.4 copy-start.120
  91.8 15.5 %copy-start.121 = (f32[8,16,8]{2,1,0:T(8,128)}, f32[8,16,8]{2,1,0:T(8,128)S(1)}, u32[]{:S(2)}) copy-start(f32[8,16,8]{2,1,0:T(8,128)S(1)} %get-tuple-element.813) | copy-start | bytes 12292
  91.8 16.6 %copy-start.122 = (f32[8,16,8]{2,1,0:T(8,128)}, f32[8,16,8]{2,1,0:T(8,128)S(1)}, u32[]{:S(2)}) copy-start(f32[8,16,8]{2,1,0:T(8,128)S(1)} %get-tuple-element.814) | copy-start | bytes 12292
  91.8 17.7 %copy-start.123 = (f32[8,16,8]{2,1,0:T(8,128)}, f32[8,16,8]{2,1,0:T(8,128)S(1)}, u32[]{:S(2)}) copy-start(f32[8,16,8]{2,1,0:T(8,128)S(1)} %get-tuple-element.815) | copy-start | bytes 12292
  91.8 18.8 %copy-start.124 = (f32[8,16,8]{2,1,0:T(8,128)}, f32[8,16,8]{2,1,0:T(8,128)S(1)}, u32[]{:S(2)}) copy-start(f32[8,16,8]{2,1,0:T(8,128)S(1)} %get-tuple-element.816) | copy-start | bytes 12292
  91.8 26.7 %copy-start.99 = (f32[8,16,8]{2,1,0:T(8,128)}, f32[8,16,8]{2,1,0:T(8,128)S(1)}, u32[]{:S(2)}) copy-start(f32[8,16,8]{2,1,0:T(8,128)S(1)} %get-tuple-element.798) | copy-start | bytes 12292
  91.8 19.9 %copy-start.126 = (f32[8,16,8]{2,1,0:T(8,128)}, f32[8,16,8]{2,1,0:T(8,128)S(1)}, u32[]{:S(2)}) copy-start(f32[8,16,8]{2,1,0:T(8,128)S(1)} %get-tuple-element.818) | copy-start | bytes 12292
  91.8 21.0 %copy-start.127 = (f32[8,16,8]{2,1,0:T(8,128)}, f32[8,16,8]{2,1,0:T(8,128)S(1)}, u32[]{:S(2)}) copy-start(f32[8,16,8]{2,1,0:T(8,128)S(1)} %get-tuple-element.819) | copy-start | bytes 12292
  91.9 22.2 %copy-start.128 = (f32[8,16,8]{2,1,0:T(8,128)}, f32[8,16,8]{2,1,0:T(8,128)S(1)}, u32[]{:S(2)}) copy-start(f32[8,16,8]{2,1,0:T(8,128)S(1)} %get-tuple-element.820) | copy-start | bytes 12292
  91.9 23.3 %copy-start.129 = (f32[8,16,8]{2,1,0:T(8,128)}, f32[8,16,8]{2,1,0:T(8,128)S(1)}, u32[]{:S(2)}) copy-start(f32[8,16,8]{2,1,0:T(8,128)S(1)} %get-tuple-element.821) | copy-start | bytes 12292
  91.9 24.4 %copy-start.130 = (f32[8,16,8]{2,1,0:T(8,128)}, f32[8,16,8]{2,1,0:T(8,128)S(1)}, u32[]{:S(2)}) copy-start(f32[8,16,8]{2,1,0:T(8,128)S(1)} %get-tuple-element.822) | copy-start | bytes 12292
  91.9 25.5 %copy-start.125 = (f32[8,16,8]{2,1,0:T(8,128)}, f32[8,16,8]{2,1,0:T(8,128)S(1)}, u32[]{:S(2)}) copy-start(f32[8,16,8]{2,1,0:T(8,128)S(1)} %get-tuple-element.817) | copy-start | bytes 12292
  125.1 77.9 %all-reduce.14.cloned.1.call-start = ((), (), s32[]{:S(2)}) async-start(), calls=%async_computation.5 | async-start | bytes 589824 | tf_op jit(solution)/shard_map/psum | solution.py:184
  183.0 453.4 %all-reduce.18.cloned.1.call-start = ((), (), s32[]{:S(2)}) async-start(), calls=%async_computation.11 | async-start | bytes 1179648 | tf_op jit(solution)/shard_map/psum | solution.py:165
  187.4 21.3 %copy-start.8 = (bf16[576,1152]{1,0:T(8,128)(2,1)S(1)}, bf16[576,1152]{1,0:T(8,128)(2,1)}, u32[]{:S(2)}) copy-start(bf16[576,1152]{1,0:T(8,128)(2,1)} %param.129) | copy-start | bytes 3981316
  453.8 14.2 copy-start.181
  593.9 6.5 collective-permute-start.2
  595.2 6.6 collective-permute-start.3
  603.5 231.9 %all-reduce.16.cloned.1.call-start = ((), (), s32[]{:S(2)}) async-start(), calls=%async_computation.9 | async-start | bytes 11796480
  609.1 360.8 %reduce-scatter.13.cloned.1.call-start = ((), (), s32[]{:S(2)}) async-start(), calls=%async_computation.10 | async-start | bytes 3133440
  612.4 529.9 %reduce-scatter.7.cloned.1.call-start = ((), (), s32[]{:S(2)}) async-start(), calls=%async_computation.6 | async-start | bytes 9400320 | tf_op jit(solution)/shard_map/reduce_scatter | solution.py:262
  618.6 710.4 %reduce-scatter.9.cloned.1.call-start = ((), (), s32[]{:S(2)}) async-start(), calls=%async_computation.7 | async-start | bytes 11280384 | tf_op jit(solution)/shard_map/reduce_scatter | solution.py:265
  625.3 892.4 %reduce-scatter.11.cloned.1.call-start = ((), (), s32[]{:S(2)}) async-start(), calls=%async_computation.8 | async-start | bytes 11280384 | tf_op jit(solution)/shard_map/reduce_scatter | solution.py:266
  720.4 797.4 %copy-start.1 = (bf16[1152,2,576]{0,2,1:T(8,128)(2,1)S(1)}, bf16[1152,2,576]{0,2,1:T(8,128)(2,1)}, u32[]{:S(2)}) copy-start(bf16[1152,2,576]{0,2,1:T(8,128)(2,1)} %param.126) | copy-start | bytes 7962628
  (297 other events, 1315.0 us)
Sparse Core Ops, SparseCore 0:
  125.2 20.2 all-reduce.11
  183.1 19.8 all-reduce.13
  603.7 20.9 all-reduce.17
  630.8 204.5 all-reduce.15
  840.9 128.9 reduce-scatter.12
  976.0 166.2 reduce-scatter.6
  1148.7 180.2 reduce-scatter.8
  1336.4 181.3 reduce-scatter.10
where the time goes:
time: 1540 us; the launch traced here: 1530 us
  waiting for transfers between devices  809 us (53%)
  local copies, waits for them, and re-layouts  423 us (27%)
  other arithmetic  135 us (9%)
  blocking collectives  81.3 us (5%)
  matrix products  42.8 us (3%)
  between operations  21.3 us (1%)
    unnamed x10, waiting for transfers between devices  244 us
    reduce_scatter x1, waiting for transfers between devices, on_device(): lax.psum_scatter(down_weight_grad, ('img', 'band'), scatter_dimension=1,...  189 us
    reduce_scatter x1, waiting for transfers between devices, on_device(): lax.psum_scatter(up_weight_grad, ('img', 'band'), scatter_dimension=0, ti...  187 us
    reduce_scatter x1, waiting for transfers between devices, on_device(): lax.psum_scatter(project_in_grad, ('img', 'band'), scatter_dimension=0, t...  172 us
    scatter-add x21, local copies, waits for them, and re-layouts, on_device(): key_pad_grad = key_pad_grad.at[:, row_at:row_at + band_rows, col_at:col_a...  89.6 us
    convert_element_type x50, local copies, waits for them, and re-layouts, tap_view(): return heads_view(padded[:, row_at:row_at + band_rows, col_at:col_at + co...  84.6 us
    psum x1, blocking collectives, on_device(): lax.psum((first_gain_grad, first_shift_grad, bias_table_grad, out_shift_g...  81.3 us
    scatter-add x21, local copies, waits for them, and re-layouts, on_device(): value_pad_grad = value_pad_grad.at[:, row_at:row_at + band_rows, col_at:c...  78.6 us
  transfers between devices with their start and end apart: 12, of which 8 were waited for; matrix products, arithmetic and copies ran while one was open for 6% of the time, Pallas kernels for 0%

commit v1 on v0

v1 whole, which is shorter than its diff:
```python
import functools
import math

import jax
import jax.numpy as jnp
from jax import lax
from jax.experimental import pallas as pl
from jax.experimental.pallas import tpu as pltpu
from jax.sharding import PartitionSpec as P

HD = 72
ROWS = 16
COLS = 16
WIN = 5
REACH = WIN // 2
TAPS = WIN * WIN
HALO = REACH * COLS
KEYS = 256

EPSILON = 1e-05
MASKED = -1000000000.0
HIGHEST = lax.Precision.HIGHEST
MESH = pl.DeviceIdType.MESH
BF16 = jnp.bfloat16
F32 = jnp.float32
GELU_A = math.sqrt(2.0 / math.pi)
GELU_B = 0.044715


def dot_nn(a, b):
    return lax.dot_general(a, b, (((1,), (0,)), ((), ())), preferred_element_type=F32)


def dot_nt(a, b):
    return lax.dot_general(a, b, (((1,), (1,)), ((), ())), preferred_element_type=F32)


def dot_tn(a, b):
    return lax.dot_general(a, b, (((0,), (0,)), ((), ())), preferred_element_type=F32)


def normed(values):
    center = values - jnp.mean(values, axis=-1, keepdims=True)
    inv = lax.rsqrt(jnp.mean(center * center, axis=-1, keepdims=True) + EPSILON)
    return center * inv, inv


def normed_back(unit, inv, gain, grad):
    unit_grad = grad * gain
    return inv * (
        unit_grad
        - jnp.mean(unit_grad, axis=-1, keepdims=True)
        - unit * jnp.mean(unit_grad * unit, axis=-1, keepdims=True)
    )


def gelu_pair(u):
    square = u * u
    t = jnp.tanh(GELU_A * u * (1.0 + GELU_B * square))
    half = 0.5 * (1.0 + t)
    slope = half + (0.5 * GELU_A) * u * (1.0 - t * t) * (1.0 + (3.0 * GELU_B) * square)
    return u * half, slope


def column_sum(values):
    return jnp.sum(values, axis=0, keepdims=True)


def head_window(head, width):
    first = head * HD // 128 * 128
    last = min(-(-(head + 1) * HD // 128) * 128, width)
    return first, last


def main_kernel(
    tokens,
    cotangent,
    time_low,
    first_gain,
    first_shift,
    out_shift,
    second_gain,
    second_shift,
    up_shift,
    down_shift,
    bias_table,
    bias_index,
    in_hbm,
    time_hbm,
    out_hbm,
    up_hbm,
    down_hbm,
    output,
    tokens_grad,
    first_low,
    second_low,
    active_low,
    upper_low,
    attended_low,
    resid_low,
    mixed_grad,
    small_sums,
    bias_grad,
    in_w,
    time_w,
    out_w,
    up_w,
    down_w,
    halo_tokens,
    rows_low,
    query,
    keys,
    values,
    prob,
    key_grad,
    value_grad,
    attended_grad,
    query_grad,
    attended,
    resid,
    part_own,
    part_other,
    down_own,
    down_other,
    second_own,
    second_other,
    first_own,
    first_other,
    halo_own,
    halo_other,
    bias_tiles,
    weight_sems,
    send_sems,
    recv_sems,
):
    count = tokens.shape[0]
    local = query.shape[1]
    heads = bias_table.shape[0]
    hidden = up_shift.shape[1]
    scale = HD ** (-0.5)
    image = lax.axis_index("img")
    band = lax.axis_index("band")
    head_half = lax.axis_index("head")
    sibling = (image, band, 1 - head_half)
    beside = (image, 1 - band, head_half)

    weight_copies = [
        pltpu.make_async_copy(src, dst, weight_sems.at[i])
        for i, (src, dst) in enumerate(
            (
                (in_hbm, in_w),
                (time_hbm, time_w),
                (out_hbm, out_w),
                (up_hbm, up_w),
                (down_hbm, down_w),
            )
        )
    ]
    for copy in weight_copies:
        copy.start()

    barrier = pltpu.get_barrier_semaphore()
    for other in (sibling, beside):
        pl.semaphore_signal(barrier, inc=1, device_id=other, device_id_type=MESH)
    pl.semaphore_wait(barrier, 2)

    def remote(index, source, target, device):
        return pltpu.make_async_remote_copy(
            src_ref=source,
            dst_ref=target,
            send_sem=send_sems.at[index],
            recv_sem=recv_sems.at[index],
            device_id=device,
            device_id_type=MESH,
        )

    edge = pl.multiple_of((1 - band) * (count - HALO), HALO)
    token_copy = remote(0, tokens.at[pl.ds(edge, HALO)], halo_tokens, beside)
    token_copy.start()

    gain_1 = first_gain[...]
    shift_1 = first_shift[...]
    unit, _ = normed(tokens[...].astype(F32))
    own_low = (unit * gain_1 + shift_1).astype(BF16)
    first_low[...] = own_low
    rows_low[pl.ds(0, count)] = own_low
    token_copy.wait()
    unit, _ = normed(halo_tokens[...].astype(F32))
    rows_low[pl.ds(count, HALO)] = (unit * gain_1 + shift_1).astype(BF16)

    weight_copies[1].wait()
    time_proj = dot_nt(jnp.broadcast_to(time_low[...], (8, time_low.shape[1])), time_w[...])[0:1]
    weight_copies[0].wait()
    rows = rows_low[...]
    query[...] = (dot_nt(rows[:count], in_w[0:local]) + time_proj[:, :local]).astype(BF16)
    halo_at = pl.multiple_of((1 - band) * (count + HALO), HALO)
    blank_at = pl.multiple_of(band * (count + HALO), HALO)
    zero_rows = jnp.zeros((HALO, local), BF16)
    zero_tail = jnp.zeros((KEYS - count - 2 * HALO, local), BF16)
    for kept, projected in (
        (keys, dot_nt(rows, in_w[local : 2 * local])),
        (values, dot_nt(rows, in_w[2 * local : 3 * local]) + time_proj[:, local:]),
    ):
        projected = projected.astype(BF16)
        kept[pl.ds(HALO, count)] = projected[:count]
        kept[pl.ds(halo_at, HALO)] = projected[count:]
        kept[pl.ds(blank_at, HALO)] = zero_rows
        kept[pl.ds(count + 2 * HALO, KEYS - count - 2 * HALO)] = zero_tail

    lane = lax.broadcasted_iota(jnp.int32, (COLS, 128), 1)
    row = lax.broadcasted_iota(jnp.int32, (COLS, 128), 0)
    col_step = lane % COLS - row
    row_step = lane // COLS
    inside = (col_step >= -REACH) & (col_step <= REACH) & (row_step < WIN)
    tap_of = jnp.where(inside, row_step * WIN + col_step + REACH, -1)
    key_lane = lax.broadcasted_iota(jnp.int32, (1, KEYS), 1)
    absent = jnp.where(key_lane < HALO, 1 - band, 0) + jnp.where(
        (key_lane >= count + HALO) & (key_lane < count + 2 * HALO), band, 0
    )
    absent = absent.astype(F32) * MASKED
    masked_half = jnp.full((COLS, 128), MASKED, F32)
    bands_here = count // COLS

    def in_head(head, shape):
        first, _ = head_window(head, local)
        at = lax.broadcasted_iota(jnp.int32, shape, 1) + first
        return (at >= head * HD) & (at < (head + 1) * HD)

    attended[...] = jnp.zeros(attended.shape, F32)
    for head in range(heads):
        first, last = head_window(head, local)
        width = last - first
        own = in_head(head, (count, width))
        tile = jnp.full((COLS, 128), MASKED, F32)
        for tap in range(TAPS):
            tile = jnp.where(tap_of == tap, bias_table[head, bias_index[tap]], tile)
        tile = jnp.concatenate([tile, masked_half], axis=1)
        bias = jnp.concatenate(
            [tile] + [pltpu.roll(tile, COLS * r, 1) for r in range(1, bands_here)], axis=0
        )
        queries = jnp.where(own, query[:, first:last], jnp.zeros((), BF16))
        scores = dot_nt(queries, keys[:, first:last]) * scale + (bias + absent)
        top = jnp.max(scores, axis=-1, keepdims=True)
        weights = jnp.exp(scores - top)
        weights = weights * (1.0 / jnp.sum(weights, axis=-1, keepdims=True))
        prob[head] = weights
        mixed = dot_nn(weights.astype(BF16), values[:, first:last])
        attended[:, first:last] += jnp.where(own, mixed, 0.0)

    low = attended[...].astype(BF16)
    attended_low[...] = low
    weight_copies[2].wait()
    part_own[...] = dot_nn(low, out_w[...])
    part_copy = remote(1, part_own, part_other, sibling)
    part_copy.start()
    part_copy.wait()
    after = tokens[...].astype(F32) + (part_own[...] + part_other[...]) + out_shift[...]
    resid[...] = after
    unit, _ = normed(after)
    low = (unit * second_gain[...] + second_shift[...]).astype(BF16)
    second_low[...] = low

    weight_copies[3].wait()
    weight_copies[4].wait()
    step = 768
    down_sum = None
    second_sum = None
    for at in range(0, hidden, step):
        piece = slice(at, at + step)
        upper = dot_nn(second_low[...], up_w[:, piece]) + up_shift[:, piece]
        active, slope = gelu_pair(upper)
        active = active.astype(BF16)
        active_low[:, piece] = active
        term = dot_nn(active, down_w[piece])
        down_sum = term if down_sum is None else down_sum + term
        grad = dot_nt(cotangent[...], down_w[piece]) * slope
        upper_sum = column_sum(grad)
        if at + step <= 1152:
            small_sums[6:7, at : at + step] = upper_sum
        elif at >= 1152:
            small_sums[7:8, at - 1152 : at + step - 1152] = upper_sum
        else:
            small_sums[6:7, at:1152] = upper_sum[:, : 1152 - at]
            small_sums[7:8, 0 : at + step - 1152] = upper_sum[:, 1152 - at :]
        grad = grad.astype(BF16)
        upper_low[:, piece] = grad
        term = dot_nt(grad, up_w[:, piece])
        second_sum = term if second_sum is None else second_sum + term
    second_own[...] = second_sum.astype(BF16)
    second_copy = remote(2, second_own, second_other, sibling)
    second_copy.start()
    down_own[...] = down_sum.astype(BF16)
    down_copy = remote(3, down_own, down_other, sibling)
    down_copy.start()
    cot = cotangent[...].astype(F32)
    small_sums[5:6] = column_sum(cot)
    second_copy.wait()
    back = second_own[...].astype(F32) + second_other[...].astype(F32)
    unit, inv = normed(resid[...])
    small_sums[3:4] = column_sum(back * unit)
    small_sums[4:5] = column_sum(back)
    grad = cot + normed_back(unit, inv, second_gain[...], back)
    tokens_grad[...] = grad
    small_sums[2:3] = column_sum(grad)
    low = grad.astype(BF16)
    resid_low[...] = low
    attended_grad[...] = dot_nt(low, out_w[...]).astype(BF16)

    query_grad[...] = jnp.zeros(query_grad.shape, F32)
    key_grad[...] = jnp.zeros(key_grad.shape, F32)
    value_grad[...] = jnp.zeros(value_grad.shape, F32)
    for head in range(heads):
        first, last = head_window(head, local)
        width = last - first
        own = in_head(head, (count, width))
        nothing = jnp.zeros((), BF16)
        queries = jnp.where(own, query[:, first:last], nothing)
        grads = jnp.where(own, attended_grad[:, first:last], nothing)
        weights = prob[head]
        prob_grad = dot_nt(grads, values[:, first:last])
        value_grad[:, first:last] += dot_tn(weights.astype(BF16), grads)
        product = weights * prob_grad
        score_grad = product - weights * jnp.sum(product, axis=-1, keepdims=True)
        tile = score_grad[0:COLS]
        for r in range(1, bands_here):
            tile = tile + pltpu.roll(score_grad[r * COLS : (r + 1) * COLS], KEYS - COLS * r, 1)
        bias_tiles[head] = tile[:, :128]
        low = (score_grad * scale).astype(BF16)
        query_grad[:, first:last] += jnp.where(own, dot_nn(low, keys[:, first:last]), 0.0)
        key_grad[:, first:last] += dot_tn(low, queries)

    halo_own[:, :local] = key_grad[pl.ds(halo_at, HALO)].astype(BF16)
    halo_own[:, local:] = value_grad[pl.ds(halo_at, HALO)].astype(BF16)
    halo_copy = remote(4, halo_own, halo_other, beside)
    halo_copy.start()

    low = query_grad[...].astype(BF16)
    mixed_grad[:, :local] = low
    small_sums[8:9, :local] = column_sum(low.astype(F32))
    out_lane = lax.broadcasted_iota(jnp.int32, (heads, 128), 1)
    table_grad = jnp.zeros((heads, 128), F32)
    for dc in range(WIN):
        diagonal = inside & (col_step == dc - REACH)
        sums = jnp.sum(jnp.where(diagonal[None], bias_tiles[...], 0.0), axis=1)
        for dr in range(WIN):
            group = (out_lane >= dr * COLS) & (out_lane < (dr + 1) * COLS)
            total = jnp.sum(jnp.where(group, sums, 0.0), axis=-1, keepdims=True)
            table_grad = jnp.where(out_lane == bias_index[dr * WIN + dc], total, table_grad)
    bias_grad[...] = table_grad
    down_copy.wait()
    lowered = down_own[...].astype(F32) + down_other[...].astype(F32)
    output[...] = (resid[...] + lowered + down_shift[...]).astype(BF16)

    halo_copy.wait()
    edge_at = pl.multiple_of(HALO + edge, HALO)
    arrived = halo_other[...].astype(F32)
    key_grad[pl.ds(edge_at, HALO)] += arrived[:, :local]
    value_grad[pl.ds(edge_at, HALO)] += arrived[:, local:]
    mixed_grad[:, local : 2 * local] = key_grad[pl.ds(HALO, count)].astype(BF16)
    low = value_grad[pl.ds(HALO, count)].astype(BF16)
    mixed_grad[:, 2 * local :] = low
    small_sums[8:9, local:] = column_sum(low.astype(F32))
    small_sums[9:10] = time_low[...].astype(F32)
    small_sums[10:16] = jnp.zeros((6, small_sums.shape[1]), F32)

    first_own[...] = dot_nn(mixed_grad[...], in_w[...]).astype(BF16)
    first_copy = remote(5, first_own, first_other, sibling)
    first_copy.start()
    unit, inv = normed(tokens[...].astype(F32))
    first_copy.wait()
    back = first_own[...].astype(F32) + first_other[...].astype(F32)
    small_sums[0:1] = column_sum(back * unit)
    small_sums[1:2] = column_sum(back)
    tokens_grad[...] += normed_back(unit, inv, first_gain[...], back)


def main_path(tokens, cotangent, time_low, vectors, bias_table, bias_index, weights):
    count, width = tokens.shape
    local = weights[2].shape[0]
    hidden = weights[3].shape[1]
    heads = bias_table.shape[0]
    vmem = pl.BlockSpec(memory_space=pltpu.VMEM)
    smem = pl.BlockSpec(memory_space=pltpu.SMEM)
    anywhere = pl.BlockSpec(memory_space=pl.ANY)
    struct = jax.ShapeDtypeStruct
    outs = (
        struct((count, width), BF16),
        struct((count, width), F32),
        struct((count, width), BF16),
        struct((count, width), BF16),
        struct((count, hidden), BF16),
        struct((count, hidden), BF16),
        struct((count, local), BF16),
        struct((count, width), BF16),
        struct((count, 3 * local), BF16),
        struct((16, width), F32),
        struct((heads, 128), F32),
    )
    scratch = [
        *[pltpu.VMEM(w.shape, BF16) for w in weights],
        pltpu.VMEM((HALO, width), BF16),
        pltpu.VMEM((count + HALO, width), BF16),
        pltpu.VMEM((count, local), BF16),
        pltpu.VMEM((KEYS, local), BF16),
        pltpu.VMEM((KEYS, local), BF16),
        pltpu.VMEM((heads, count, KEYS), F32),
        pltpu.VMEM((KEYS, local), F32),
        pltpu.VMEM((KEYS, local), F32),
        pltpu.VMEM((count, local), BF16),
        pltpu.VMEM((count, local), F32),
        pltpu.VMEM((count, local), F32),
        pltpu.VMEM((count, width), F32),
        pltpu.VMEM((count, width), F32),
        pltpu.VMEM((count, width), F32),
        *[pltpu.VMEM((count, width), BF16) for _ in range(6)],
        pltpu.VMEM((HALO, 2 * local), BF16),
        pltpu.VMEM((HALO, 2 * local), BF16),
        pltpu.VMEM((heads, COLS, 128), F32),
        pltpu.SemaphoreType.DMA((5,)),
        pltpu.SemaphoreType.DMA((6,)),
        pltpu.SemaphoreType.DMA((6,)),
    ]
    return pl.pallas_call(
        main_kernel,
        out_shape=outs,
        in_specs=[vmem] * 10 + [smem] * 2 + [anywhere] * 5,
        out_specs=[vmem] * len(outs),
        scratch_shapes=scratch,
        name="main_path",
        compiler_params=pltpu.CompilerParams(
            collective_id=0, has_side_effects=True, vmem_limit_bytes=60 * 1024 * 1024
        ),
    )(tokens, cotangent, time_low, *vectors, bias_table, bias_index, *weights)


def time_features(timesteps, width):
    half = width // 2
    freqs = jnp.exp(jnp.arange(half, dtype=F32) * (-math.log(10000.0) / half))
    angles = timesteps.astype(F32)[:, None] * freqs[None, :]
    return jnp.concatenate([jnp.cos(angles), jnp.sin(angles)], axis=1)


def on_device(
    tokens,
    timesteps,
    first_gain,
    first_shift,
    project_in,
    time_weight,
    bias_table,
    bias_index,
    project_out,
    out_shift,
    second_gain,
    second_shift,
    up_weight,
    up_shift,
    down_weight,
    down_shift,
    cotangent,
):
    batch, band_rows, columns, width = tokens.shape
    local = project_in.shape[2]
    count = batch * band_rows * columns
    assert batch == 1 and columns == COLS
    time_low = time_features(timesteps, width).astype(BF16)
    in_rows = jnp.transpose(project_in, (1, 2, 0)).reshape(3 * local, width)
    time_rows = jnp.transpose(time_weight, (1, 2, 0)).reshape(2 * local, width)
    vectors = [
        v[None, :]
        for v in (first_gain, first_shift, out_shift, second_gain, second_shift, up_shift, down_shift)
    ]
    (
        output,
        tokens_grad,
        first_low,
        second_low,
        active_low,
        upper_low,
        attended_low,
        resid_low,
        mixed_grad,
        small_sums,
        bias_grad,
    ) = main_path(
        tokens.reshape(count, width),
        cotangent.reshape(count, width),
        time_low,
        vectors,
        bias_table,
        bias_index,
        (in_rows, time_rows, project_out, up_weight, down_weight),
    )
    axes = ("img", "band")
    grads_in = dot_tn(first_low, mixed_grad)
    grads_out = dot_tn(resid_low, attended_low)
    grads_up = dot_tn(second_low, upper_low)
    grads_down = dot_tn(cotangent.reshape(count, width), active_low)
    shares = [
        lax.psum_scatter(g.astype(BF16), axes, scatter_dimension=0, tiled=True).astype(F32)
        for g in (grads_in, grads_out, grads_up, grads_down)
    ]
    times = lax.all_gather(small_sums[8:10], axes, axis=0)
    here = lax.axis_index(axes) * shares[0].shape[0]
    time_cut = lax.dynamic_slice_in_dim(times[:, 1], here, shares[0].shape[0], axis=1)
    time_share = jnp.einsum("nd,nk->dk", time_cut, times[:, 0], precision=HIGHEST)
    sums = lax.psum((small_sums[:8], bias_grad), axes)
    small, bias_total = sums
    rows = shares[0].shape[0]
    return (
        output.reshape(tokens.shape),
        tokens_grad.reshape(tokens.shape),
        small[0],
        small[1],
        shares[0].reshape(rows, 3, local),
        time_share.reshape(rows, 2, local),
        bias_total[:, :TAPS],
        jnp.transpose(shares[1]),
        small[2],
        small[3],
        small[4],
        shares[2],
        small[6:8].reshape(-1)[: up_shift.shape[0]],
        jnp.transpose(shares[3]),
        small[5],
    )


def solution(mesh):
    return jax.shard_map(
        on_device,
        mesh=mesh,
        in_specs=(
            P("img", "band", None, None),
            P("img"),
            P(),
            P(),
            P(None, None, "head"),
            P(None, None, "head"),
            P("head", None),
            P(),
            P("head", None),
            P(),
            P(),
            P(),
            P(None, "head"),
            P("head"),
            P("head", None),
            P(),
            P("img", "band", None, None),
        ),
        out_specs=(
            P("img", "band", None, None),
            P("img", "band", None, None),
            P(),
            P(),
            P(("img", "band"), None, "head"),
            P(("img", "band"), None, "head"),
            P("head", None),
            P("head", ("img", "band")),
            P(),
            P(),
            P(),
            P(("img", "band"), "head"),
            P("head"),
            P("head", ("img", "band")),
            P(),
        ),
        check_vma=False,
    )
```

time: 1540 us -> 615 us (0.40)
  waiting for transfers between devices: 809 us -> 407 us
  local copies, waits for them, and re-layouts: 423 us -> 27.4 us
  other arithmetic: 135 us -> 4.23 us
  blocking collectives: 81.3 us -> 114 us
  Pallas kernels: 0 us -> 32.1 us
  matrix products: 42.8 us -> 15.6 us
    reduce_scatter x3 -> x2, waiting for transfers between devices: 548 us -> 262 us  [on_device(): lax.psum_scatter(g.astype(BF16), axes, scatter_dimension=0, tiled=True)]
    scatter-add x42 -> x0, local copies, waits for them, and re-layouts: 168 us -> none  [the longest x21 89.6 us: on_device(): key_pad_grad = key_pad_grad.at[:, row_at:row_at + band_rows, col_at:col_a...]
    mul x152 -> x0, local copies, waits for them, and re-layouts: 152 us -> none  [the longest x50 70.5 us: on_device(): query_grad = query_grad + score_grad[..., None] * key_tap]
    unnamed x10 -> x6, waiting for transfers between devices: 244 us -> 145 us
    convert_element_type x50 -> x0, local copies, waits for them, and re-layouts: 84.6 us -> none  [tap_view(): return heads_view(padded[:, row_at:row_at + band_rows, col_at:col_at + co...]
    reduce_sum x21 -> x0, other arithmetic: 49.1 us -> none  [the longest x1 8.86 us: on_device(): delta = jnp.sum(attended_grad * attended_heads, axis=-1)]
    all_gather x0 -> x1, blocking collectives: none -> 36.5 us  [on_device(): times = lax.all_gather(small_sums[8:10], axes, axis=0)]
    add x33 -> x0, other arithmetic: 35.2 us -> none  [the longest x16 29.7 us: on_device(): key_pad_grad = key_pad_grad.at[:, row_at:row_at + band_rows, col_at:col_a...]
  transfers between devices with their start and end apart: 12 -> 4, of which waited for: 8 -> 3; matrix products, arithmetic and copies ran while one was open for 6% -> 5% of each run, Pallas kernels for 0% -> 0%
where the time goes in v1:
time: 615 us
  waiting for transfers between devices  407 us (66%)
  blocking collectives  114 us (19%)
  Pallas kernels  32.1 us (5%)
  local copies, waits for them, and re-layouts  27.4 us (4%)
  matrix products  15.6 us (3%)
  between operations  14.6 us (2%)
    reduce_scatter x2, waiting for transfers between devices, on_device(): lax.psum_scatter(g.astype(BF16), axes, scatter_dimension=0, tiled=True)  262 us
    unnamed x6, waiting for transfers between devices  145 us
    psum x1, blocking collectives, on_device(): sums = lax.psum((small_sums[:8], bias_grad), axes)  77 us
    all_gather x1, blocking collectives, on_device(): times = lax.all_gather(small_sums[8:10], axes, axis=0)  36.5 us
    pallas_call x1, Pallas kernels, main_path(): pl.pallas_call(main_kernel, out_shape=outs, in_specs=[vmem] * 10 + [smem]...  32.1 us
    unnamed x25, local copies, waits for them, and re-layouts  15.5 us
    dot_general x4, matrix products, dot_tn(): lax.dot_general(a, b, (((0,), (0,)), ((), ())), preferred_element_type=F32)  15.1 us
  transfers between devices with their start and end apart: 4, of which 3 were waited for; matrix products, arithmetic and copies ran while one was open for 5% of the time, Pallas kernels for 0%

profile of v1, /device:TPU:0, one launch (start us, length us, event | category | flops | bytes accessed | tf_op | source)
XLA Modules:
  0.0 614.6 jit_solution(18193981154190186729)
XLA Ops:
  8.0 1.3 broadcast_in_dim.23.first_gain
  9.2 1.3 broadcast_in_dim.24.first_shift
  10.5 1.3 broadcast_in_dim.25.out_shift
  11.8 1.3 broadcast_in_dim.26.second_gain
  13.1 1.3 broadcast_in_dim.27.second_shift
  14.4 1.3 broadcast_in_dim.29.down_shift
  15.7 1.3 broadcast_in_dim.28.up_shift
  17.0 0.7 pad_maximum_fusion.time_low
  17.7 32.1 %main_path.1 = (bf16[128,1152]{1,0:T(8,128)(2,1)}, f32[128,1152]{1,0:T(8,128)}, bf16[128,1152]{1,0:T(8,128)(2,1)}, bf16[128,1152]{1,0:T(8,128)(2,1)}, bf16[128,2...) custom-call(bf16[128,1152]{1,0:T(8,128)(2,1)} %bitcast.47, ...), custom_call_target="tpu_custom_call" | custom-call | tf_op jit(solution)/shard_map/main_path/pallas_call | solution.py:423
  49.8 2.7 convolution_convert_fusion.3
  52.6 4.5 convolution_convert_fusion.2
  57.2 3.9 fusion
  61.2 8.6 %copy.47 = bf16[1152,2304]{1,0:T(8,128)(2,1)} copy(bf16[1152,2304]{0,1:T(8,128)(2,1)} %fusion) | data formatting | bytes 10616832
  69.8 0.9 copy-done.2
  70.9 3.9 convolution_convert_fusion.1
  74.9 77.0 %all-reduce.1 = (f32[8,1152]{1,0:T(8,128)S(1)}, f32[8,128]{1,0:T(8,128)}) all-reduce(f32[8,1152]{1,0:T(8,128)S(1)} %slice.36, f32[8,128]{1,0:T(8,128)S(1)} %copy-done.7), channel_id=1, replica_groups=mesh['img'=8,'band'=2,'head'=2] {'img','band'}, use_global_device_ids=true, to_apply=%region_0.0 | all-reduce | flops 10240 | bytes 81920 | tf_op jit(solution)/shard_map/psum | solution.py:507
  152.0 0.6 reshape.105
  152.6 36.5 %all-gather.1 = f32[16,2,1152]{2,1,0:T(2,128)S(1)} all-gather(f32[1,2,1152]{2,1,0:T(2,128)S(1)} %slice_bitcast_fusion), channel_id=2, replica_groups=mesh['img'=8,'band'=2,'head'=2] {'img','band'}, dimensions={0}, use_global_device_ids=true | all-gather | bytes 156672 | tf_op jit(solution)/shard_map/all_gather | solution.py:503
  189.4 0.5 fusion.1
  190.0 0.9 copy.45
  190.9 0.7 slice_reduce_fusion
  191.6 1.6 convert_bitcast_fusion.1
  193.1 119.1 %reduce-scatter.9.cloned.1.call-done = bf16[72,1728]{1,0:T(8,128)(2,1)} async-done(((bf16[1152,1728]{1,0:T(8,128)(2,1)}), bf16[72,1728]{1,0:T(8,128)(2,1)}) %reduce-scatter.9.cloned.1.call-update) | async-done | bytes 248848 | tf_op jit(solution)/shard_map/reduce_scatter | solution.py:500
  312.2 1.2 reshape.107
  313.5 0.8 copy.44
  314.3 144.9 %reduce-scatter.13.cloned.1.call-done = bf16[72,2304]{1,0:T(8,128)(2,1)} async-done(((bf16[1152,2304]{1,0:T(8,128)(2,1)}), bf16[72,2304]{1,0:T(8,128)(2,1)}) %reduce-scatter.13.cloned.1.call-update) | async-done | bytes 331792
  459.2 1.3 copy.48
  460.6 1.2 copy.46
  461.7 143.0 %reduce-scatter.11.cloned.1.call-done = bf16[72,2304]{1,0:T(8,128)(2,1)} async-done(((bf16[1152,2304]{1,0:T(8,128)(2,1)}), bf16[72,2304]{1,0:T(8,128)(2,1)}) %reduce-scatter.11.cloned.1.call-update) | async-done | bytes 331792 | tf_op jit(solution)/shard_map/reduce_scatter | solution.py:500
  604.7 1.9 convert_element_type.29
  606.6 0.7 copy.57
  607.3 0.8 copy.58
  (35 shorter events, 0.9 us)
Async XLA Ops:
  7.2 184.4 %reduce-scatter.15.cloned.1.call-start = ((), (), s32[]{:S(2)}) async-start(), calls=%async_computation.7 | async-start | bytes 1566720
  52.6 259.7 %reduce-scatter.9.cloned.1.call-start = ((), (), s32[]{:S(2)}) async-start(), calls=%async_computation.4 | async-start | bytes 4386816 | tf_op jit(solution)/shard_map/reduce_scatter | solution.py:500
  52.6 4.6 copy-start
  52.6 4.6 copy-start.1
  57.2 402.0 %reduce-scatter.13.cloned.1.call-start = ((), (), s32[]{:S(2)}) async-start(), calls=%async_computation.6 | async-start | bytes 5640192
  69.7 1.0 copy-start.2
  69.7 1.2 copy-start.3
  69.8 535.0 %reduce-scatter.11.cloned.1.call-start = ((), (), s32[]{:S(2)}) async-start(), calls=%async_computation.5 | async-start | bytes 5640192 | tf_op jit(solution)/shard_map/reduce_scatter | solution.py:500
  70.9 4.0 copy-start.6
  70.9 4.0 copy-start.7
  74.8 531.7 %copy-start.5 = (bf16[128,1152]{1,0:T(8,128)(2,1)S(1)}, bf16[128,1152]{1,0:T(8,128)(2,1)}, u32[]{:S(2)}) copy-start(bf16[128,1152]{1,0:T(8,128)(2,1)} %get-tuple-element.26) | copy-start | bytes 884740
  189.1 418.2 %copy-start.4 = (f32[128,1152]{1,0:T(8,128)S(1)}, f32[128,1152]{1,0:T(8,128)}, u32[]{:S(2)}) copy-start(f32[128,1152]{1,0:T(8,128)} %get-tuple-element.27) | copy-start | bytes 1769476
Sparse Core Ops, SparseCore 0:
  52.7 118.2 reduce-scatter.14
  176.9 135.2 reduce-scatter.8
  318.3 140.7 reduce-scatter.12
  465.1 139.5 reduce-scatter.10

commit v2 on v1

v2 whole, which is shorter than its diff:
```python
import functools
import math
import types

import jax
import jax.numpy as jnp
from jax import lax
from jax.experimental import pallas as pl
from jax.experimental.pallas import tpu as pltpu
from jax.sharding import PartitionSpec as P

HD = 72
ROWS = 16
COLS = 16
WIN = 5
REACH = WIN // 2
TAPS = WIN * WIN
HALO = REACH * COLS
KEYS = 256

EPSILON = 1e-05
MASKED = -1000000000.0
HIGHEST = lax.Precision.HIGHEST
MESH = pl.DeviceIdType.MESH
BF16 = jnp.bfloat16
F32 = jnp.float32
GELU_A = math.sqrt(2.0 / math.pi)
GELU_B = 0.044715


def dot_nn(a, b):
    return lax.dot_general(a, b, (((1,), (0,)), ((), ())), preferred_element_type=F32)


def dot_nt(a, b):
    return lax.dot_general(a, b, (((1,), (1,)), ((), ())), preferred_element_type=F32)


def dot_tn(a, b):
    return lax.dot_general(a, b, (((0,), (0,)), ((), ())), preferred_element_type=F32)


def normed(values):
    center = values - jnp.mean(values, axis=-1, keepdims=True)
    inv = lax.rsqrt(jnp.mean(center * center, axis=-1, keepdims=True) + EPSILON)
    return center * inv, inv


def normed_back(unit, inv, gain, grad):
    unit_grad = grad * gain
    return inv * (
        unit_grad
        - jnp.mean(unit_grad, axis=-1, keepdims=True)
        - unit * jnp.mean(unit_grad * unit, axis=-1, keepdims=True)
    )


def gelu_pair(u):
    square = u * u
    t = jnp.tanh(GELU_A * u * (1.0 + GELU_B * square))
    half = 0.5 * (1.0 + t)
    slope = half + (0.5 * GELU_A) * u * (1.0 - t * t) * (1.0 + (3.0 * GELU_B) * square)
    return u * half, slope


def column_sum(values):
    return jnp.sum(values, axis=0, keepdims=True)


def head_window(head, width):
    first = head * HD // 128 * 128
    last = min(-(-(head + 1) * HD // 128) * 128, width)
    return first, last


def layer_kernel(names, meshed, *refs):
    r = types.SimpleNamespace(**dict(zip(names, refs, strict=True)))
    count, width = r.tokens.shape
    local = r.query.shape[1]
    heads = r.bias_table.shape[0]
    hidden = r.up_shift.shape[1]
    scale = HD ** (-0.5)
    image = lax.axis_index("img")
    band = lax.axis_index("band")
    half = lax.axis_index("head")
    sibling = (image, band, 1 - half)
    beside = (image, 1 - band, half)
    peers = [sibling, beside]
    if meshed:
        x, z = image % 2, image // 2
        across = z * 2 + 1 - x
        near_z, far_z, third_z = z + 1 - 2 * (z % 2), 3 - z, (z + 2) % 4
        plane = [(across, band, half), beside, (across, 1 - band, half)]
        near, far, third = ((at * 2 + x, band, half) for at in (near_z, far_z, third_z))
        peers = [sibling, *plane, near, far, third]

    weight_copies = [
        pltpu.make_async_copy(source, target, r.weight_sems.at[i])
        for i, (source, target) in enumerate(
            (
                (r.time_hbm, r.time_w),
                (r.in_hbm, r.in_w),
                (r.out_hbm, r.out_w),
                (r.up_hbm, r.up_w),
                (r.down_hbm, r.down_w),
            )
        )
    ]
    for copy in weight_copies:
        copy.start()

    barrier = pltpu.get_barrier_semaphore()
    for other in peers:
        pl.semaphore_signal(barrier, inc=1, device_id=other, device_id_type=MESH)

    def remote(index, source, target, device):
        return pltpu.make_async_remote_copy(
            src_ref=source,
            dst_ref=target,
            send_sem=r.send_sems.at[index],
            recv_sem=r.recv_sems.at[index],
            device_id=device,
            device_id_type=MESH,
        )

    def started(copies):
        for copy in copies:
            copy.start()
        return copies

    def finish(copies):
        for copy in copies:
            copy.wait()

    def spread(index, source, slots):
        return started([remote(index + k, source, slots.at[k], plane[k]) for k in range(3)])

    def spread_rows(index, turned, slots):
        rows = turned.shape[0] // 4
        return started(
            [
                remote(
                    index + k - 1,
                    turned.at[pl.ds(k * rows, rows)],
                    slots.at[:, pl.ds(k * count, count)],
                    plane[k - 1],
                )
                for k in range(1, 4)
            ]
        )

    unit, _ = normed(r.tokens[...].astype(F32))
    own_low = (unit * r.first_gain[...] + r.first_shift[...]).astype(BF16)
    r.first_low[...] = own_low
    r.rows_low[pl.ds(0, count)] = own_low

    pl.semaphore_wait(barrier, len(peers))
    edge = pl.multiple_of((1 - band) * (count - HALO), HALO)
    token_copy = remote(0, r.tokens.at[pl.ds(edge, HALO)], r.halo_tokens, beside)
    token_copy.start()
    if meshed:
        cot_copies = spread(6, r.cotangent, r.cot_all)
        rows4 = width // 4
        owners = rows4 // 4
        place = lax.broadcasted_iota(jnp.int32, (rows4, width), 0)
        place = place + (rows4 - owners) * (place // owners)
        place = lax.broadcasted_iota(jnp.int32, (rows4, width), 1) - place
        for k, spot in enumerate(
            (
                2 * x + band,
                2 * (1 - x) + band,
                2 * x + 1 - band,
                2 * (1 - x) + 1 - band,
            )
        ):
            r.perm[k * rows4 : (k + 1) * rows4] = (place == owners * spot).astype(F32).astype(BF16)
        r.first_turned[...] = dot_nt(r.perm[...], own_low).astype(BF16)
        r.first_all[:, 0:count] = r.first_turned[0:rows4]
        first_copies = spread_rows(9, r.first_turned, r.first_all)

    weight_copies[0].wait()
    time_rows = jnp.broadcast_to(r.time_low[...], (8, width))
    time_proj = dot_nt(time_rows, r.time_w[...])[0:1]
    token_copy.wait()
    unit, _ = normed(r.halo_tokens[...].astype(F32))
    halo_low = (unit * r.first_gain[...] + r.first_shift[...]).astype(BF16)
    r.rows_low[pl.ds(count, HALO)] = halo_low
    weight_copies[1].wait()
    rows = r.rows_low[...]
    r.query[...] = (dot_nt(rows[:count], r.in_w[0:local]) + time_proj[:, :local]).astype(BF16)
    halo_at = pl.multiple_of((1 - band) * (count + HALO), HALO)
    blank_at = pl.multiple_of(band * (count + HALO), HALO)
    tail = KEYS - count - 2 * HALO
    for kept, projected in (
        (r.keys, dot_nt(rows, r.in_w[local : 2 * local])),
        (r.values, dot_nt(rows, r.in_w[2 * local : 3 * local]) + time_proj[:, local:]),
    ):
        projected = projected.astype(BF16)
        kept[pl.ds(HALO, count)] = projected[:count]
        kept[pl.ds(halo_at, HALO)] = projected[count:]
        kept[pl.ds(blank_at, HALO)] = jnp.zeros((HALO, local), BF16)
        kept[pl.ds(count + 2 * HALO, tail)] = jnp.zeros((tail, local), BF16)

    lane = lax.broadcasted_iota(jnp.int32, (COLS, 128), 1)
    row = lax.broadcasted_iota(jnp.int32, (COLS, 128), 0)
    col_step = lane % COLS - row
    row_step = lane // COLS
    inside = (col_step >= -REACH) & (col_step <= REACH) & (row_step < WIN)
    tap_of = jnp.where(inside, row_step * WIN + col_step + REACH, -1)
    key_lane = lax.broadcasted_iota(jnp.int32, (1, KEYS), 1)
    absent = jnp.where(key_lane < HALO, 1 - band, 0) + jnp.where(
        (key_lane >= count + HALO) & (key_lane < count + 2 * HALO), band, 0
    )
    absent = absent.astype(F32) * MASKED
    masked_half = jnp.full((COLS, 128), MASKED, F32)
    bands_here = count // COLS
    nothing = jnp.zeros((), BF16)

    def in_head(head, shape):
        first, _ = head_window(head, local)
        at = lax.broadcasted_iota(jnp.int32, shape, 1) + first
        return (at >= head * HD) & (at < (head + 1) * HD)

    r.attended[...] = jnp.zeros(r.attended.shape, F32)
    for head in range(heads):
        first, last = head_window(head, local)
        own = in_head(head, (count, last - first))
        tile = jnp.full((COLS, 128), MASKED, F32)
        for tap in range(TAPS):
            tile = jnp.where(tap_of == tap, r.bias_table[head, r.bias_index[tap]], tile)
        tile = jnp.concatenate([tile, masked_half], axis=1)
        bias = jnp.concatenate(
            [tile] + [pltpu.roll(tile, COLS * k, 1) for k in range(1, bands_here)], axis=0
        )
        queries = jnp.where(own, r.query[:, first:last], nothing)
        scores = dot_nt(queries, r.keys[:, first:last]) * scale + (bias + absent)
        top = jnp.max(scores, axis=-1, keepdims=True)
        weights = jnp.exp(scores - top)
        weights = weights * (1.0 / jnp.sum(weights, axis=-1, keepdims=True))
        r.prob[head] = weights
        mixed = dot_nn(weights.astype(BF16), r.values[:, first:last])
        r.attended[:, first:last] += jnp.where(own, mixed, 0.0)

    attended_low = r.attended_all.at[0] if meshed else r.attended_low
    attended_low[...] = r.attended[...].astype(BF16)
    weight_copies[2].wait()
    r.part_own[...] = dot_nn(attended_low[...], r.out_w[...])
    part_copy = remote(1, r.part_own, r.part_other, sibling)
    part_copy.start()
    if meshed:
        attended_copies = spread(12, r.attended_all.at[0], r.attended_all.at[pl.ds(1, 3)])
    part_copy.wait()
    after = r.tokens[...].astype(F32) + (r.part_own[...] + r.part_other[...]) + r.out_shift[...]
    r.resid[...] = after
    unit, _ = normed(after)
    r.second_low[...] = (unit * r.second_gain[...] + r.second_shift[...]).astype(BF16)
    if meshed:
        second_copies = spread(15, r.second_low, r.second_all)

    weight_copies[3].wait()
    weight_copies[4].wait()
    step = hidden // 3
    down_sum = None
    second_sum = None
    for at in range(0, hidden, step):
        piece = slice(at, at + step)
        upper = dot_nn(r.second_low[...], r.up_w[:, piece]) + r.up_shift[:, piece]
        active, slope = gelu_pair(upper)
        active = active.astype(BF16)
        r.active_low[:, piece] = active
        term = dot_nn(active, r.down_w[piece])
        down_sum = term if down_sum is None else down_sum + term
        grad = dot_nt(r.cotangent[...], r.down_w[piece]) * slope
        sums = column_sum(grad)
        for line in range(-(-hidden // width)):
            low_at, high_at = max(at, line * width), min(at + step, (line + 1) * width)
            if low_at < high_at:
                r.small_own[6 + line : 7 + line, low_at - line * width : high_at - line * width] = (
                    sums[:, low_at - at : high_at - at]
                )
        grad = grad.astype(BF16)
        r.upper_low[:, piece] = grad
        term = dot_nt(grad, r.up_w[:, piece])
        second_sum = term if second_sum is None else second_sum + term
    r.second_own[...] = second_sum.astype(BF16)
    second_copy = remote(2, r.second_own, r.second_other, sibling)
    second_copy.start()
    r.down_own[...] = down_sum.astype(BF16)
    down_copy = remote(3, r.down_own, r.down_other, sibling)
    down_copy.start()
    cot = r.cotangent[...].astype(F32)
    r.small_own[5:6] = column_sum(cot)
    second_copy.wait()
    back = r.second_own[...].astype(F32) + r.second_other[...].astype(F32)
    unit, inv = normed(r.resid[...])
    r.small_own[3:4] = column_sum(back * unit)
    r.small_own[4:5] = column_sum(back)
    grad = cot + normed_back(unit, inv, r.second_gain[...], back)
    r.tokens_grad[...] = grad
    r.small_own[2:3] = column_sum(grad)
    r.resid_low[...] = grad.astype(BF16)
    r.attended_grad[...] = dot_nt(r.resid_low[...], r.out_w[...]).astype(BF16)
    if meshed:
        r.resid_turned[...] = dot_nt(r.perm[...], r.resid_low[...]).astype(BF16)
        r.resid_all[:, 0:count] = r.resid_turned[0:rows4]
        resid_copies = spread_rows(18, r.resid_turned, r.resid_all)

    r.query_grad[...] = jnp.zeros(r.query_grad.shape, F32)
    r.key_grad[...] = jnp.zeros(r.key_grad.shape, F32)
    r.value_grad[...] = jnp.zeros(r.value_grad.shape, F32)
    for head in range(heads):
        first, last = head_window(head, local)
        own = in_head(head, (count, last - first))
        queries = jnp.where(own, r.query[:, first:last], nothing)
        grads = jnp.where(own, r.attended_grad[:, first:last], nothing)
        weights = r.prob[head]
        prob_grad = dot_nt(grads, r.values[:, first:last])
        r.value_grad[:, first:last] += dot_tn(weights.astype(BF16), grads)
        product = weights * prob_grad
        score_grad = product - weights * jnp.sum(product, axis=-1, keepdims=True)
        tile = score_grad[0:COLS]
        for k in range(1, bands_here):
            tile = tile + pltpu.roll(score_grad[k * COLS : (k + 1) * COLS], KEYS - COLS * k, 1)
        r.bias_tiles[head] = tile[:, :128]
        low = (score_grad * scale).astype(BF16)
        r.query_grad[:, first:last] += jnp.where(own, dot_nn(low, r.keys[:, first:last]), 0.0)
        r.key_grad[:, first:last] += dot_tn(low, queries)

    r.halo_own[:, :local] = r.key_grad[pl.ds(halo_at, HALO)].astype(BF16)
    r.halo_own[:, local:] = r.value_grad[pl.ds(halo_at, HALO)].astype(BF16)
    halo_copy = remote(4, r.halo_own, r.halo_other, beside)
    halo_copy.start()

    query_low = r.query_all.at[0] if meshed else r.query_low
    pair_low = r.pair_all.at[0] if meshed else r.pair_low
    low = r.query_grad[...].astype(BF16)
    query_low[...] = low
    if meshed:
        query_copies = spread(21, r.query_all.at[0], r.query_all.at[pl.ds(1, 3)])
    r.small_own[8:9, :local] = column_sum(low.astype(F32))
    out_lane = lax.broadcasted_iota(jnp.int32, (heads, 128), 1)
    table_grad = jnp.zeros((heads, 128), F32)
    for dc in range(WIN):
        diagonal = inside & (col_step == dc - REACH)
        sums = jnp.sum(jnp.where(diagonal[None], r.bias_tiles[...], 0.0), axis=1)
        for dr in range(WIN):
            group = (out_lane >= dr * COLS) & (out_lane < (dr + 1) * COLS)
            total = jnp.sum(jnp.where(group, sums, 0.0), axis=-1, keepdims=True)
            table_grad = jnp.where(out_lane == r.bias_index[dr * WIN + dc], total, table_grad)
    r.small_own[9:10] = r.time_low[...].astype(F32)
    r.small_own[10:16] = jnp.zeros((6, width), F32)
    for head in range(heads):
        r.small_own[10:11, head * 128 : (head + 1) * 128] = table_grad[head : head + 1]
    down_copy.wait()
    lowered = r.down_own[...].astype(F32) + r.down_other[...].astype(F32)
    r.output[...] = (r.resid[...] + lowered + r.down_shift[...]).astype(BF16)

    halo_copy.wait()
    edge_at = pl.multiple_of(HALO + edge, HALO)
    arrived = r.halo_other[...].astype(F32)
    r.key_grad[pl.ds(edge_at, HALO)] += arrived[:, :local]
    r.value_grad[pl.ds(edge_at, HALO)] += arrived[:, local:]
    pair_low[:, :local] = r.key_grad[pl.ds(HALO, count)].astype(BF16)
    low = r.value_grad[pl.ds(HALO, count)].astype(BF16)
    pair_low[:, local:] = low
    if meshed:
        pair_copies = spread(24, r.pair_all.at[0], r.pair_all.at[pl.ds(1, 3)])
    r.small_own[8:9, local:] = column_sum(low.astype(F32))

    first_sum = dot_nn(query_low[...], r.in_w[0:local])
    first_sum = first_sum + dot_nn(pair_low[...], r.in_w[local:])
    r.first_own[...] = first_sum.astype(BF16)
    first_copy = remote(5, r.first_own, r.first_other, sibling)
    first_copy.start()
    unit, inv = normed(r.tokens[...].astype(F32))
    first_copy.wait()
    back = r.first_own[...].astype(F32) + r.first_other[...].astype(F32)
    r.small_own[0:1] = column_sum(back * unit)
    r.small_own[1:2] = column_sum(back)
    r.tokens_grad[...] += normed_back(unit, inv, r.first_gain[...], back)
    if not meshed:
        return

    small_copies = spread(27, r.small_own, r.small_plane)
    select = r.perm[0:rows4]
    others = 3 * count
    finish(cot_copies)
    cot_others = r.cot_all[...].reshape(others, width)
    r.cot_turned[:, :count] = dot_nt(select, r.cotangent[...]).astype(BF16)
    r.cot_turned[:, count:] = dot_nt(select, cot_others).astype(BF16)
    finish(second_copies)
    second_others = r.second_all[...].reshape(others, width)
    r.second_turned[:, :count] = dot_nt(select, r.second_low[...]).astype(BF16)
    r.second_turned[:, count:] = dot_nt(select, second_others).astype(BF16)

    part = step // 2

    def wide_first(t):
        return [
            remote(36 + 4 * t, r.wide_a.at[t, near_z], r.wide_a_in.at[t, 0], near),
            remote(37 + 4 * t, r.wide_a.at[t, 3 - near_z], r.wide_a_in.at[t, 1], near),
            remote(38 + 4 * t, r.wide_b.at[t, far_z], r.wide_b_in.at[t, 0], far),
            remote(39 + 4 * t, r.wide_b.at[t, far_z + 1 - 2 * (far_z % 2)], r.wide_b_in.at[t, 1], far),
        ]

    def wide_piece(t, carry):
        piece = pl.ds(pl.multiple_of(t * step, step), step)
        upper = dot_nn(r.second_all[...].reshape(others, width), r.up_w[:, piece])
        active, slope = gelu_pair(upper + r.up_shift[:, piece])
        grad = dot_nt(r.cot_all[...].reshape(others, width), r.down_w[piece]) * slope
        down = dot_nn(r.cot_turned[:, :count], r.active_low[:, piece])
        down = down + dot_nn(r.cot_turned[:, count:], active.astype(BF16))
        up = dot_nn(r.second_turned[:, :count], r.upper_low[:, piece])
        up = up + dot_nn(r.second_turned[:, count:], grad.astype(BF16))
        for k in range(4):
            cut = slice(k * owners, (k + 1) * owners)
            both = jnp.concatenate([down[cut], up[cut]], axis=0).astype(BF16)
            r.wide_a[t, k] = both[:, :part]
            r.wide_b[t, k] = both[:, part:]
        started(wide_first(t))
        return carry

    lax.fori_loop(0, 3, wide_piece, 0)

    finish(small_copies)
    small_sum = r.small_own[...]
    for k in range(3):
        small_sum = small_sum + r.small_plane[k]
    same_image = r.small_own[8:9] + r.small_plane[1, 8:9]
    other_image = r.small_plane[0, 8:9] + r.small_plane[2, 8:9]
    r.small_z[...] = small_sum
    r.small_z[8:9] = same_image
    r.small_z[9:10] = other_image
    r.small_z[11:12] = r.small_own[9:10]
    r.small_z[12:13] = r.small_plane[0, 9:10]
    ring = (near, far, third)
    ring_copies = started([remote(30 + k, r.small_z, r.small_ring.at[k], ring[k]) for k in range(3)])

    def wide_second(t):
        return [
            remote(52 + 2 * t, r.wide_a_sum.at[t], r.wide_a_last.at[t], far),
            remote(53 + 2 * t, r.wide_b_sum.at[t], r.wide_b_last.at[t], near),
        ]

    def joined(left, right):
        return left.astype(F32) + right.astype(F32)

    for t in range(3):
        finish(wide_first(t))
        r.wide_a_sum[t] = joined(r.wide_a[t, far_z], r.wide_a_in[t, 1]).astype(BF16)
        r.wide_b_sum[t] = joined(r.wide_b[t, near_z], r.wide_b_in[t, 1]).astype(BF16)
        started(wide_second(t))

    tokens4 = 4 * count
    finish(first_copies)
    finish(resid_copies)
    finish(attended_copies)
    finish(query_copies)
    narrow = dot_nn(r.resid_all[...], r.attended_all[...].reshape(tokens4, local))
    for k in range(4):
        r.narrow_a[k, :, :local] = narrow[k * owners : (k + 1) * owners].astype(BF16)
    narrow = dot_nn(r.first_all[...], r.query_all[...].reshape(tokens4, local))
    for k in range(4):
        r.narrow_a[k, :, local:] = narrow[k * owners : (k + 1) * owners].astype(BF16)
    narrow_a = started(
        [
            remote(58, r.narrow_a.at[near_z], r.narrow_a_in.at[0], near),
            remote(59, r.narrow_a.at[3 - near_z], r.narrow_a_in.at[1], near),
        ]
    )
    finish(pair_copies)
    narrow = dot_nn(r.first_all[...], r.pair_all[...].reshape(tokens4, 2 * local))
    for k in range(4):
        r.narrow_b[k] = narrow[k * owners : (k + 1) * owners].astype(BF16)
    narrow_b = started(
        [
            remote(60, r.narrow_b.at[far_z], r.narrow_b_in.at[0], far),
            remote(61, r.narrow_b.at[far_z + 1 - 2 * (far_z % 2)], r.narrow_b_in.at[1], far),
        ]
    )

    finish(ring_copies)
    small_sum = r.small_z[...]
    for k in range(3):
        small_sum = small_sum + r.small_ring[k]
    r.small_sums[...] = small_sum
    time_lines = [r.small_z[11:13]] + [r.small_ring[k, 11:13] for k in range(3)]
    time_lines = jnp.concatenate(time_lines, axis=0).astype(BF16)
    r.time_turned[...] = dot_nt(select, time_lines)
    time_cut = r.time_turned[pl.ds(pl.multiple_of(z * owners, 8), owners)]
    time_share = jnp.zeros((owners, width), F32)
    for k in range(4):
        source = r.small_z if k == 0 else r.small_ring.at[k - 1]
        for line in range(2):
            column = time_cut[:, 2 * k + line : 2 * k + line + 1]
            time_share = time_share + column * source[8 + line : 9 + line]
    r.time_share[0] = time_share[:, :local]
    r.time_share[1] = time_share[:, local:]

    for t in range(3):
        finish(wide_second(t))
        left = joined(r.wide_a[t, z], r.wide_a_in[t, 0]) + r.wide_a_last[t].astype(F32)
        right = joined(r.wide_b[t, z], r.wide_b_in[t, 0]) + r.wide_b_last[t].astype(F32)
        for at, total in ((t * step, left), (t * step + part, right)):
            r.down_share[:, at : at + part] = total[:owners]
            r.up_share[:, at : at + part] = total[owners:]

    finish(narrow_a)
    r.narrow_a_sum[...] = joined(r.narrow_a[far_z], r.narrow_a_in[1]).astype(BF16)
    last_a = started([remote(62, r.narrow_a_sum, r.narrow_a_last, far)])
    finish(narrow_b)
    r.narrow_b_sum[...] = joined(r.narrow_b[near_z], r.narrow_b_in[1]).astype(BF16)
    last_b = started([remote(63, r.narrow_b_sum, r.narrow_b_last, near)])
    finish(last_a)
    total = joined(r.narrow_a[z], r.narrow_a_in[0]) + r.narrow_a_last[...].astype(F32)
    r.out_share[...] = total[:, :local]
    r.in_share[0] = total[:, local:]
    finish(last_b)
    total = joined(r.narrow_b[z], r.narrow_b_in[0]) + r.narrow_b_last[...].astype(F32)
    r.in_share[1] = total[:, :local]
    r.in_share[2] = total[:, local:]


def layer_call(meshed, inputs, smalls, weights):
    count, width = inputs["tokens"].shape
    local = weights["out_hbm"].shape[0]
    hidden = weights["up_hbm"].shape[1]
    heads = smalls["bias_table"].shape[0]
    tokens4, rows4 = 4 * count, width // 4
    owners, part = rows4 // 4, hidden // 6
    outs = {"output": ((count, width), BF16), "tokens_grad": ((count, width), F32)}
    kept = {
        "first_low": ((count, width), BF16),
        "second_low": ((count, width), BF16),
        "active_low": ((count, hidden), BF16),
        "upper_low": ((count, hidden), BF16),
        "resid_low": ((count, width), BF16),
        "small_own": ((16, width), F32),
    }
    scratch = {
        "time_w": ((2 * local, width), BF16),
        "in_w": ((3 * local, width), BF16),
        "out_w": ((local, width), BF16),
        "up_w": ((width, hidden), BF16),
        "down_w": ((hidden, width), BF16),
        "halo_tokens": ((HALO, width), BF16),
        "rows_low": ((count + HALO, width), BF16),
        "query": ((count, local), BF16),
        "keys": ((KEYS, local), BF16),
        "values": ((KEYS, local), BF16),
        "prob": ((heads, count, KEYS), F32),
        "key_grad": ((KEYS, local), F32),
        "value_grad": ((KEYS, local), F32),
        "attended_grad": ((count, local), BF16),
        "query_grad": ((count, local), F32),
        "attended": ((count, local), F32),
        "resid": ((count, width), F32),
        "part_own": ((count, width), F32),
        "part_other": ((count, width), F32),
        "halo_own": ((HALO, 2 * local), BF16),
        "halo_other": ((HALO, 2 * local), BF16),
        "bias_tiles": ((heads, COLS, 128), F32),
    }
    for name in ("down", "second", "first"):
        scratch[name + "_own"] = ((count, width), BF16)
        scratch[name + "_other"] = ((count, width), BF16)
    if meshed:
        outs |= {
            "small_sums": ((16, width), F32),
            "in_share": ((3, owners, local), F32),
            "time_share": ((2, owners, local), F32),
            "out_share": ((owners, local), F32),
            "up_share": ((owners, hidden), F32),
            "down_share": ((owners, hidden), F32),
        }
        scratch |= kept
        scratch |= {
            "cot_all": ((3, count, width), BF16),
            "second_all": ((3, count, width), BF16),
            "attended_all": ((4, count, local), BF16),
            "query_all": ((4, count, local), BF16),
            "pair_all": ((4, count, 2 * local), BF16),
            "perm": ((width, width), BF16),
            "first_turned": ((width, count), BF16),
            "resid_turned": ((width, count), BF16),
            "first_all": ((rows4, tokens4), BF16),
            "resid_all": ((rows4, tokens4), BF16),
            "cot_turned": ((rows4, tokens4), BF16),
            "second_turned": ((rows4, tokens4), BF16),
            "small_plane": ((3, 16, width), F32),
            "small_z": ((16, width), F32),
            "small_ring": ((3, 16, width), F32),
            "time_turned": ((rows4, 8), F32),
        }
        for name in ("wide_a", "wide_b"):
            scratch[name] = ((3, 4, 2 * owners, part), BF16)
            scratch[name + "_in"] = ((3, 2, 2 * owners, part), BF16)
            scratch[name + "_sum"] = ((3, 2 * owners, part), BF16)
            scratch[name + "_last"] = ((3, 2 * owners, part), BF16)
        for name in ("narrow_a", "narrow_b"):
            scratch[name] = ((4, owners, 2 * local), BF16)
            scratch[name + "_in"] = ((2, owners, 2 * local), BF16)
            scratch[name + "_sum"] = ((owners, 2 * local), BF16)
            scratch[name + "_last"] = ((owners, 2 * local), BF16)
    else:
        outs |= kept
        outs |= {
            "attended_low": ((count, local), BF16),
            "query_low": ((count, local), BF16),
            "pair_low": ((count, 2 * local), BF16),
        }
    links = 64 if meshed else 6
    sems = {"weight_sems": 5, "send_sems": links, "recv_sems": links}
    vmem = pl.BlockSpec(memory_space=pltpu.VMEM)
    smem = pl.BlockSpec(memory_space=pltpu.SMEM)
    anywhere = pl.BlockSpec(memory_space=pl.ANY)
    names = [*inputs, *smalls, *weights, *outs, *scratch, *sems]
    results = pl.pallas_call(
        functools.partial(layer_kernel, names, meshed),
        out_shape=[jax.ShapeDtypeStruct(*shape) for shape in outs.values()],
        in_specs=[vmem] * len(inputs) + [smem] * len(smalls) + [anywhere] * len(weights),
        out_specs=[vmem] * len(outs),
        scratch_shapes=[pltpu.VMEM(*shape) for shape in scratch.values()]
        + [pltpu.SemaphoreType.DMA((number,)) for number in sems.values()],
        name="layer",
        compiler_params=pltpu.CompilerParams(
            collective_id=0, has_side_effects=True, vmem_limit_bytes=61 * 1024 * 1024
        ),
    )(*inputs.values(), *smalls.values(), *weights.values())
    return types.SimpleNamespace(**dict(zip(outs, results, strict=True)))


def time_features(timesteps, width):
    half = width // 2
    freqs = jnp.exp(jnp.arange(half, dtype=F32) * (-math.log(10000.0) / half))
    angles = timesteps.astype(F32)[:, None] * freqs[None, :]
    return jnp.concatenate([jnp.cos(angles), jnp.sin(angles)], axis=1)


def on_device(
    tokens,
    timesteps,
    first_gain,
    first_shift,
    project_in,
    time_weight,
    bias_table,
    bias_index,
    project_out,
    out_shift,
    second_gain,
    second_shift,
    up_weight,
    up_shift,
    down_weight,
    down_shift,
    cotangent,
):
    batch, band_rows, columns, width = tokens.shape
    local = project_in.shape[2]
    count = batch * band_rows * columns
    assert batch == 1 and columns == COLS
    meshed = lax.axis_size("img") == 8 and lax.axis_size("band") == 2
    cot = cotangent.reshape(count, width)
    inputs = {
        "tokens": tokens.reshape(count, width),
        "cotangent": cot,
        "time_low": time_features(timesteps, width).astype(BF16),
        "first_gain": first_gain[None],
        "first_shift": first_shift[None],
        "out_shift": out_shift[None],
        "second_gain": second_gain[None],
        "second_shift": second_shift[None],
        "up_shift": up_shift[None],
        "down_shift": down_shift[None],
    }
    smalls = {"bias_table": bias_table, "bias_index": bias_index}
    weights = {
        "time_hbm": jnp.transpose(time_weight, (1, 2, 0)).reshape(2 * local, width),
        "in_hbm": jnp.transpose(project_in, (1, 2, 0)).reshape(3 * local, width),
        "out_hbm": project_out,
        "up_hbm": up_weight,
        "down_hbm": down_weight,
    }
    r = layer_call(meshed, inputs, smalls, weights)
    if meshed:
        in_share = jnp.transpose(r.in_share, (1, 0, 2))
        time_share = jnp.transpose(r.time_share, (1, 0, 2))
        out_share, up_share, down_share = r.out_share, r.up_share, r.down_share
        small = r.small_sums
    else:
        axes = ("img", "band")
        grads = (
            dot_tn(r.first_low, jnp.concatenate([r.query_low, r.pair_low], axis=1)),
            dot_tn(r.resid_low, r.attended_low),
            dot_tn(r.second_low, r.upper_low),
            dot_tn(cot, r.active_low),
        )
        in_share, out_share, up_share, down_share = [
            lax.psum_scatter(g.astype(BF16), axes, scatter_dimension=0, tiled=True).astype(F32)
            for g in grads
        ]
        rows = in_share.shape[0]
        in_share = in_share.reshape(rows, 3, local)
        times = lax.all_gather(r.small_own[8:10], axes, axis=0)
        here = lax.axis_index(axes) * rows
        time_cut = lax.dynamic_slice_in_dim(times[:, 1], here, rows, axis=1)
        time_share = jnp.einsum("nd,nk->dk", time_cut, times[:, 0], precision=HIGHEST)
        time_share = time_share.reshape(rows, 2, local)
        small = lax.psum(r.small_own, axes)
    heads = bias_table.shape[0]
    return (
        r.output.reshape(tokens.shape),
        r.tokens_grad.reshape(tokens.shape),
        small[0],
        small[1],
        in_share,
        time_share,
        small[10, : heads * 128].reshape(heads, 128)[:, :TAPS],
        jnp.transpose(out_share),
        small[2],
        small[3],
        small[4],
        up_share,
        small[6:8].reshape(-1)[: up_shift.shape[0]],
        jnp.transpose(down_share),
        small[5],
    )


def solution(mesh):
    return jax.shard_map(
        on_device,
        mesh=mesh,
        in_specs=(
            P("img", "band", None, None),
            P("img"),
            P(),
            P(),
            P(None, None, "head"),
            P(None, None, "head"),
            P("head", None),
            P(),
            P("head", None),
            P(),
            P(),
            P(),
            P(None, "head"),
            P("head"),
            P("head", None),
            P(),
            P("img", "band", None, None),
        ),
        out_specs=(
            P("img", "band", None, None),
            P("img", "band", None, None),
            P(),
            P(),
            P(("img", "band"), None, "head"),
            P(("img", "band"), None, "head"),
            P("head", None),
            P("head", ("img", "band")),
            P(),
            P(),
            P(),
            P(("img", "band"), "head"),
            P("head"),
            P("head", ("img", "band")),
            P(),
        ),
        check_vma=False,
    )
```

time: 615 us -> 165 us (0.27)
  waiting for transfers between devices: 407 us -> 0 us
  blocking collectives: 114 us -> 0 us
  Pallas kernels: 32.1 us -> 135 us
  matrix products: 15.6 us -> 0 us
  between operations: 14.6 us -> 1.35 us
    reduce_scatter x2 -> x0, waiting for transfers between devices: 262 us -> none  [on_device(): lax.psum_scatter(g.astype(BF16), axes, scatter_dimension=0, tiled=True)]
    unnamed x6 -> x0, waiting for transfers between devices: 145 us -> none
    pallas_call x1, Pallas kernels: 32.1 us -> 135 us  [layer_call(): pl.pallas_call(functools.partial(layer_kernel, names, meshed), out_shape=...]
    psum x1 -> x0, blocking collectives: 77 us -> none  [on_device(): sums = lax.psum((small_sums[:8], bias_grad), axes)]
    all_gather x1 -> x0, blocking collectives: 36.5 us -> none  [on_device(): times = lax.all_gather(small_sums[8:10], axes, axis=0)]
    dot_general x5 -> x0, matrix products: 15.6 us -> none  [the longest x4 15.1 us: dot_tn(): lax.dot_general(a, b, (((0,), (0,)), ((), ())), preferred_element_type=F32)]
    unnamed x25 -> x11, local copies, waits for them, and re-layouts: 15.5 us -> 10.7 us
  transfers between devices with their start and end apart: 4 -> 0, of which waited for: 3 -> 0; matrix products, arithmetic and copies ran while one was open for 5% -> 0% of each run, Pallas kernels for 0% -> 0%
where the time goes in v2:
time: 165 us; the launch traced here: 162 us
  Pallas kernels  135 us (82%)
  local copies, waits for them, and re-layouts  24.4 us (15%)
    pallas_call x1, Pallas kernels, layer_call(): pl.pallas_call(functools.partial(layer_kernel, names, meshed), out_shape=...  135 us
    unnamed x11, local copies, waits for them, and re-layouts  10.7 us

profile of v2, /device:TPU:0, one launch (start us, length us, event | category | flops | bytes accessed | tf_op | source)
XLA Modules:
  0.0 161.8 jit_solution(15237308776173351154)
XLA Ops:
  1.3 0.1 sine_convert_fusion
  1.4 0.7 pad_maximum_fusion.refs_2_
  2.0 1.3 broadcast_in_dim.23.refs_3_
  3.3 1.3 broadcast_in_dim.24.refs_4_
  4.6 1.3 broadcast_in_dim.25.refs_5_
  5.9 1.3 broadcast_in_dim.26.refs_6_
  7.2 1.3 broadcast_in_dim.27.refs_7_
  8.5 1.3 broadcast_in_dim.29.refs_9_
  9.8 1.3 broadcast_in_dim.28.refs_8_
  11.1 135.3 %layer.1 = (bf16[128,1152]{1,0:T(8,128)(2,1)}, f32[128,1152]{1,0:T(8,128)}, f32[16,1152]{1,0:T(8,128)}, f32[3,72,576]{2,1,0:T(8,128)}, f32[2,72,576]{2,1,0:T(8,1...) custom-call(bf16[128,1152]{1,0:T(8,128)(2,1)} %bitcast.24, bf16[128,1152]{1,0:T(8,128)(2,1)} %bitcast.25, ...), custom_call_target="tpu_custom_call" | custom-call | tf_op jit(solution)/shard_map/layer/pallas_call | solution.py:618
  146.4 0.0 copy-start.1
  146.5 0.0 copy-start
  146.5 1.5 slice.29
  147.9 0.8 slice.34
  148.7 1.8 %slice_reduce_fusion = (f32[1152]{0:T(1024)}, f32[1152]{0:T(1024)}, f32[1152]{0:T(1024)}, f32[1152]{0:T(1024)}, f32[1152]{0:T(1024)}, /*index=5*/f32[1152]{0:T(1024)}) fusion(f32[16,1152]{1,0:T(8,128)} %get-tuple-element.25), kind=kLoop, calls=%fused_computation.1 | loop fusion | bytes 55296 | tf_op jit(solution)/shard_map/slice | solution.py:727
  150.5 0.6 reshape.93
  151.1 1.9 %copy.32 = f32[72,2,576]{2,1,0:T(2,128)} copy(f32[72,2,576]{2,0,1:T(8,128)} %bitcast.22) | data formatting | bytes 663552
  153.0 1.7 %copy.40 = bf16[1,8,16,1152]{3,2,1,0:T(8,128)(2,1)} copy(bf16[1,8,16,1152]{3,2,1,0:T(8,128)(2,1)} %bitcast.23) | data formatting | bytes 589824
  154.7 1.9 %copy.41 = f32[1,8,16,1152]{3,2,1,0:T(8,128)} copy(f32[1,8,16,1152]{3,2,1,0:T(8,128)} %bitcast.20) | data formatting | bytes 1179648
  156.6 1.9 %copy.42 = f32[72,3,576]{2,0,1:T(8,128)} copy(f32[72,3,576]{2,0,1:T(8,128)} %bitcast.21) | data formatting | bytes 995328
  158.5 1.6 copy.43
  160.1 0.0 copy-done.1
  160.1 0.8 copy.44
  160.9 0.0 copy-done
  160.9 0.8 copy.45
  (2 shorter events, 0.0 us)
Async XLA Ops:
  146.4 13.7 %copy-start.1 = (f32[72,2304]{1,0:T(8,128)S(1)}, f32[72,2304]{1,0:T(8,128)}, u32[]{:S(2)}) copy-start(f32[72,2304]{1,0:T(8,128)} %get-tuple-element.80) | copy-start | bytes 1990660
  146.5 14.5 %copy-start = (f32[72,2304]{1,0:T(8,128)S(1)}, f32[72,2304]{1,0:T(8,128)}, u32[]{:S(2)}) copy-start(f32[72,2304]{1,0:T(8,128)} %get-tuple-element.30) | copy-start | bytes 1990660

commit v3 on v2

v3 whole, which is shorter than its diff:
```python
import functools
import math
import types

import jax
import jax.numpy as jnp
from jax import lax
from jax.experimental import pallas as pl
from jax.experimental.pallas import tpu as pltpu
from jax.sharding import PartitionSpec as P

HD = 72
ROWS = 16
COLS = 16
WIN = 5
REACH = WIN // 2
TAPS = WIN * WIN
HALO = REACH * COLS
KEYS = 256

EPSILON = 1e-05
MASKED = -1000000000.0
HIGHEST = lax.Precision.HIGHEST
MESH = pl.DeviceIdType.MESH
BF16 = jnp.bfloat16
F32 = jnp.float32
GELU_A = math.sqrt(2.0 / math.pi)
GELU_B = 0.044715


def dot_nn(a, b):
    return lax.dot_general(a, b, (((1,), (0,)), ((), ())), preferred_element_type=F32)


def dot_nt(a, b):
    return lax.dot_general(a, b, (((1,), (1,)), ((), ())), preferred_element_type=F32)


def dot_tn(a, b):
    return lax.dot_general(a, b, (((0,), (0,)), ((), ())), preferred_element_type=F32)


def normed(values):
    center = values - jnp.mean(values, axis=-1, keepdims=True)
    inv = lax.rsqrt(jnp.mean(center * center, axis=-1, keepdims=True) + EPSILON)
    return center * inv, inv


def normed_back(unit, inv, gain, grad):
    unit_grad = grad * gain
    return inv * (
        unit_grad
        - jnp.mean(unit_grad, axis=-1, keepdims=True)
        - unit * jnp.mean(unit_grad * unit, axis=-1, keepdims=True)
    )


def gelu_pair(u):
    square = u * u
    t = jnp.tanh(GELU_A * u * (1.0 + GELU_B * square))
    half = 0.5 * (1.0 + t)
    slope = half + (0.5 * GELU_A) * u * (1.0 - t * t) * (1.0 + (3.0 * GELU_B) * square)
    return u * half, slope


def column_sum(values):
    return jnp.sum(values, axis=0, keepdims=True)


def line_of(vector, piece=slice(None)):
    return vector[piece][None, :]


def head_window(head, width):
    first = head * HD // 128 * 128
    last = min(-(-(head + 1) * HD // 128) * 128, width)
    return first, last


def layer_kernel(names, meshed, *refs):
    r = types.SimpleNamespace(**dict(zip(names, refs, strict=True)))
    count, width = r.tokens.shape
    local = r.query.shape[1]
    heads = r.bias_table.shape[0]
    hidden = r.up_shift.shape[0]
    scale = HD ** (-0.5)
    image = lax.axis_index("img")
    band = lax.axis_index("band")
    half = lax.axis_index("head")
    sibling = (image, band, 1 - half)
    beside = (image, 1 - band, half)
    peers = [sibling, beside]
    if meshed:
        x, z = image % 2, image // 2
        across = z * 2 + 1 - x
        plane = [(across, band, half), beside, (across, 1 - band, half)]
        spot = 2 * x + band
        spots = [2 * (1 - x) + band, 2 * x + 1 - band, 2 * (1 - x) + 1 - band]
        heights = [z + 1 - 2 * (z % 2), 3 - z, (z + 2) % 4]
        column = [(at * 2 + x, band, half) for at in heights]
        peers = [sibling, *plane, *column]

    weight_copies = [
        pltpu.make_async_copy(source, target, r.weight_sems.at[i])
        for i, (source, target) in enumerate(
            (
                (r.time_hbm, r.time_w),
                (r.in_hbm, r.in_w),
                (r.out_hbm, r.out_w),
                (r.up_hbm, r.up_w),
                (r.down_hbm, r.down_w),
            )
        )
    ]
    for copy in weight_copies:
        copy.start()

    barrier = pltpu.get_barrier_semaphore()
    for other in peers:
        pl.semaphore_signal(barrier, inc=1, device_id=other, device_id_type=MESH)

    used = [0]

    def links(number):
        used[0] += number
        return used[0] - number

    def remote(index, source, target, device):
        return pltpu.make_async_remote_copy(
            src_ref=source,
            dst_ref=target,
            send_sem=r.send_sems.at[index],
            recv_sem=r.recv_sems.at[index],
            device_id=device,
            device_id_type=MESH,
        )

    def started(copies):
        for copy in copies:
            copy.start()
        return copies

    def sent(source, target, device):
        return started([remote(links(1), source, target, device)])

    def finish(copies):
        for copy in copies:
            copy.wait()

    def spread(source, slots, group):
        base = links(3)
        return started([remote(base + k, source, slots.at[k], group[k]) for k in range(3)])

    def deal(source, lanes):
        base = links(3)
        return started(
            [
                remote(
                    base + k,
                    source.at[:, pl.ds(pl.multiple_of(spots[k] * 128, 128), 128)],
                    r.mixed_all.at[k + 1, :, pl.ds(lanes, 128)],
                    plane[k],
                )
                for k in range(3)
            ]
        )

    def column_first(name):
        part, arrived = getattr(r, name + "_part"), getattr(r, name + "_in")
        base = links(2)
        return started(
            [remote(base + k, part.at[heights[k]], arrived.at[k], column[0]) for k in range(2)]
        )

    def column_second(name):
        part, arrived = getattr(r, name + "_part"), getattr(r, name + "_in")
        summed = getattr(r, name + "_sum")
        summed[...] = joined(part[heights[2]], arrived[1]).astype(BF16)
        return sent(summed, getattr(r, name + "_last"), column[2])

    def column_total(name):
        part, arrived = getattr(r, name + "_part"), getattr(r, name + "_in")
        return joined(part[z], arrived[0]) + getattr(r, name + "_last")[...].astype(F32)

    def joined(left, right):
        return left.astype(F32) + right.astype(F32)

    def keep_part(name, values):
        part = getattr(r, name + "_part")
        part[...] = values.astype(BF16).reshape(part.shape)

    def hand_out(stage, slots):
        base = links(3)
        return started(
            [remote(base + k, stage.at[spots[k]], slots.at[spot], plane[k]) for k in range(3)]
        )

    if meshed:
        mine = pl.ds(pl.multiple_of(half * (count // 2), count // 2), count // 2)
        full = local // 128 * 128
        own_lanes = pl.ds(pl.multiple_of(spot * 128, 128), 128)

    def spread_half(source, slots, group):
        base = links(3)
        return started(
            [remote(base + k, source.at[mine], slots.at[k, mine], group[k]) for k in range(3)]
        )

    def pass_half(slots):
        return sent(slots.at[:, mine], slots.at[:, mine], sibling)

    unit, _ = normed(r.tokens[...].astype(F32))
    own_low = (unit * line_of(r.first_gain) + line_of(r.first_shift)).astype(BF16)
    r.first_low[...] = own_low

    pl.semaphore_wait(barrier, len(peers))
    edge = pl.multiple_of((1 - band) * (count - HALO), HALO)
    token_copy = sent(r.tokens.at[pl.ds(edge, HALO)], r.halo_tokens, beside)
    if meshed:
        cot_copies = spread_half(r.cotangent, r.cot_all, column)
        r.first_all[0] = own_low
        first_copies = spread_half(r.first_low, r.first_all.at[pl.ds(1, 3)], plane)
        rows4 = width // 4
        owners = rows4 // 4
        place = lax.broadcasted_iota(jnp.int32, (rows4, width), 1)
        place = place - lax.broadcasted_iota(jnp.int32, (rows4, width), 0)
        r.select[...] = (place == rows4 * z).astype(F32).astype(BF16)
    weight_copies[0].wait()
    time_rows = jnp.broadcast_to(r.time_low[...], (8, width))
    time_proj = dot_nt(time_rows, r.time_w[...])[0:1]
    halo_at = pl.multiple_of((1 - band) * (count + HALO), HALO)
    blank_at = pl.multiple_of(band * (count + HALO), HALO)
    tail = KEYS - count - 2 * HALO
    weight_copies[1].wait()
    r.query[...] = (dot_nt(own_low, r.in_w[0:local]) + time_proj[:, :local]).astype(BF16)
    r.keys[pl.ds(HALO, count)] = dot_nt(own_low, r.in_w[local : 2 * local]).astype(BF16)
    projected = dot_nt(own_low, r.in_w[2 * local : 3 * local]) + time_proj[:, local:]
    r.values[pl.ds(HALO, count)] = projected.astype(BF16)
    for kept in (r.keys, r.values):
        kept[pl.ds(blank_at, HALO)] = jnp.zeros((HALO, local), BF16)
        kept[pl.ds(count + 2 * HALO, tail)] = jnp.zeros((tail, local), BF16)
    finish(token_copy)
    unit, _ = normed(r.halo_tokens[...].astype(F32))
    halo_low = (unit * line_of(r.first_gain) + line_of(r.first_shift)).astype(BF16)
    r.keys[pl.ds(halo_at, HALO)] = dot_nt(halo_low, r.in_w[local : 2 * local]).astype(BF16)
    projected = dot_nt(halo_low, r.in_w[2 * local : 3 * local]) + time_proj[:, local:]
    r.values[pl.ds(halo_at, HALO)] = projected.astype(BF16)

    lane = lax.broadcasted_iota(jnp.int32, (COLS, 128), 1)
    row = lax.broadcasted_iota(jnp.int32, (COLS, 128), 0)
    col_step = lane % COLS - row
    row_step = lane // COLS
    inside = (col_step >= -REACH) & (col_step <= REACH) & (row_step < WIN)
    tap_of = jnp.where(inside, row_step * WIN + col_step + REACH, -1)
    key_lane = lax.broadcasted_iota(jnp.int32, (1, KEYS), 1)
    absent = jnp.where(key_lane < HALO, 1 - band, 0) + jnp.where(
        (key_lane >= count + HALO) & (key_lane < count + 2 * HALO), band, 0
    )
    absent = absent.astype(F32) * MASKED
    masked_half = jnp.full((COLS, 128), MASKED, F32)
    bands_here = count // COLS
    nothing = jnp.zeros((), BF16)

    def in_head(head, shape):
        first, _ = head_window(head, local)
        at = lax.broadcasted_iota(jnp.int32, shape, 1) + first
        return (at >= head * HD) & (at < (head + 1) * HD)

    r.attended[...] = jnp.zeros(r.attended.shape, F32)
    for head in range(heads):
        first, last = head_window(head, local)
        own = in_head(head, (count, last - first))
        tile = jnp.full((COLS, 128), MASKED, F32)
        for tap in range(TAPS):
            tile = jnp.where(tap_of == tap, r.bias_table[head, r.bias_index[tap]], tile)
        tile = jnp.concatenate([tile, masked_half], axis=1)
        bias = jnp.concatenate(
            [tile] + [pltpu.roll(tile, COLS * k, 1) for k in range(1, bands_here)], axis=0
        )
        queries = jnp.where(own, r.query[:, first:last], nothing)
        scores = dot_nt(queries, r.keys[:, first:last]) * scale + (bias + absent)
        top = jnp.max(scores, axis=-1, keepdims=True)
        weights = jnp.exp(scores - top)
        weights = weights * (1.0 / jnp.sum(weights, axis=-1, keepdims=True))
        r.prob[head] = weights
        mixed = dot_nn(weights.astype(BF16), r.values[:, first:last])
        r.attended[:, first:last] += jnp.where(own, mixed, 0.0)

    r.attended_low[...] = r.attended[...].astype(BF16)
    weight_copies[2].wait()
    r.part_own[...] = dot_nn(r.attended_low[...], r.out_w[...])
    part_copy = sent(r.part_own, r.part_other, sibling)
    if meshed:
        r.attended_all[0] = r.attended_low[...]
        attended_copies = spread(r.attended_low, r.attended_all.at[pl.ds(1, 3)], plane)
        r.rest[...] = jnp.zeros(r.rest.shape, BF16)
        r.back_stage[...] = jnp.zeros(r.back_stage.shape, BF16)
        r.small_half[6:8] = jnp.zeros((2, width), F32)
    finish(part_copy)
    after = r.tokens[...].astype(F32) + (r.part_own[...] + r.part_other[...]) + line_of(r.out_shift)
    r.resid[...] = after
    unit, _ = normed(after)
    r.second_low[...] = (unit * line_of(r.second_gain) + line_of(r.second_shift)).astype(BF16)
    if meshed:
        second_copies = spread_half(r.second_low, r.second_all, column)

    if meshed:
        finish(first_copies)
        first_copies = pass_half(r.first_all.at[pl.ds(1, 3)])
    weight_copies[3].wait()
    weight_copies[4].wait()
    step = hidden // 3
    down_sum = None
    second_sum = None
    for at in range(0, hidden, step):
        piece = slice(at, at + step)
        upper = dot_nn(r.second_low[...], r.up_w[:, piece]) + line_of(r.up_shift, piece)
        active, slope = gelu_pair(upper)
        active = active.astype(BF16)
        r.active_low[:, piece] = active
        term = dot_nn(active, r.down_w[piece])
        down_sum = term if down_sum is None else down_sum + term
        grad = dot_nt(r.cotangent[...], r.down_w[piece]) * slope
        sums = column_sum(grad)
        for line in range(-(-hidden // width)):
            low_at, high_at = max(at, line * width), min(at + step, (line + 1) * width)
            if low_at < high_at:
                r.small_own[6 + line : 7 + line, low_at - line * width : high_at - line * width] = (
                    sums[:, low_at - at : high_at - at]
                )
        grad = grad.astype(BF16)
        r.upper_low[:, piece] = grad
        term = dot_nt(grad, r.up_w[:, piece])
        second_sum = term if second_sum is None else second_sum + term
    r.second_own[...] = second_sum.astype(BF16)
    second_copy = sent(r.second_own, r.second_other, sibling)
    r.down_own[...] = down_sum.astype(BF16)
    down_copy = sent(r.down_own, r.down_other, sibling)
    if meshed:
        finish(cot_copies)
        cot_copies = pass_half(r.cot_all)
        finish(first_copies)
        r.first_flat[...] = jnp.transpose(r.first_all[...].reshape(4 * count, width))
    cot = r.cotangent[...].astype(F32)
    r.small_own[5:6] = column_sum(cot)
    finish(second_copy)
    back = r.second_own[...].astype(F32) + r.second_other[...].astype(F32)
    unit, inv = normed(r.resid[...])
    r.small_own[3:4] = column_sum(back * unit)
    r.small_own[4:5] = column_sum(back)
    grad = cot + normed_back(unit, inv, line_of(r.second_gain), back)
    r.tokens_grad[...] = grad
    r.small_own[2:3] = column_sum(grad)
    r.resid_low[...] = grad.astype(BF16)
    r.attended_grad[...] = dot_nt(r.resid_low[...], r.out_w[...]).astype(BF16)
    if meshed:
        r.resid_turned[...] = jnp.transpose(grad)
        for k, at in enumerate([spot] + spots):
            lines = [
                r.resid_turned[pl.ds(pl.multiple_of(line * rows4 + owners * at, 8), owners)]
                for line in range(4)
            ]
            r.resid_stage[k] = jnp.concatenate(lines, axis=0).astype(BF16)
        r.resid_all[:, 0:count] = r.resid_stage[0]
        base = links(3)
        resid_copies = started(
            [
                remote(
                    base + k,
                    r.resid_stage.at[k + 1],
                    r.resid_all.at[:, pl.ds((k + 1) * count, count)],
                    plane[k],
                )
                for k in range(3)
            ]
        )
    r.query_grad[...] = jnp.zeros(r.query_grad.shape, F32)
    r.key_grad[...] = jnp.zeros(r.key_grad.shape, F32)
    r.value_grad[...] = jnp.zeros(r.value_grad.shape, F32)
    for head in range(heads):
        first, last = head_window(head, local)
        own = in_head(head, (count, last - first))
        queries = jnp.where(own, r.query[:, first:last], nothing)
        grads = jnp.where(own, r.attended_grad[:, first:last], nothing)
        weights = r.prob[head]
        prob_grad = dot_nt(grads, r.values[:, first:last])
        r.value_grad[:, first:last] += dot_tn(weights.astype(BF16), grads)
        product = weights * prob_grad
        score_grad = product - weights * jnp.sum(product, axis=-1, keepdims=True)
        tile = score_grad[0:COLS]
        for k in range(1, bands_here):
            tile = tile + pltpu.roll(score_grad[k * COLS : (k + 1) * COLS], KEYS - COLS * k, 1)
        r.bias_tiles[head] = tile[:, :128]
        low = (score_grad * scale).astype(BF16)
        r.query_grad[:, first:last] += jnp.where(own, dot_nn(low, r.keys[:, first:last]), 0.0)
        r.key_grad[:, first:last] += dot_tn(low, queries)

    r.halo_own[:, :local] = r.key_grad[pl.ds(halo_at, HALO)].astype(BF16)
    r.halo_own[:, local:] = r.value_grad[pl.ds(halo_at, HALO)].astype(BF16)
    halo_copy = sent(r.halo_own, r.halo_other, beside)
    low = r.query_grad[...].astype(BF16)
    r.query_low[...] = low
    if meshed:
        r.mixed_all[0, :, 128:256] = r.query_low[:, own_lanes]
        query_copies = deal(r.query_low, 128)
        r.rest[1, :, : local - full] = low[:, full:]
    r.small_own[8:9, :local] = column_sum(low.astype(F32))
    out_lane = lax.broadcasted_iota(jnp.int32, (heads, 128), 1)
    table_grad = jnp.zeros((heads, 128), F32)
    for dc in range(WIN):
        diagonal = inside & (col_step == dc - REACH)
        sums = jnp.sum(jnp.where(diagonal[None], r.bias_tiles[...], 0.0), axis=1)
        for dr in range(WIN):
            group = (out_lane >= dr * COLS) & (out_lane < (dr + 1) * COLS)
            total = jnp.sum(jnp.where(group, sums, 0.0), axis=-1, keepdims=True)
            table_grad = jnp.where(out_lane == r.bias_index[dr * WIN + dc], total, table_grad)
    r.small_own[9:10] = r.time_low[...].astype(F32)
    r.small_own[10:16] = jnp.zeros((6, width), F32)
    for head in range(heads):
        r.small_own[10:11, head * 128 : (head + 1) * 128] = table_grad[head : head + 1]
    finish(down_copy)
    lowered = r.down_own[...].astype(F32) + r.down_other[...].astype(F32)
    r.output[...] = (r.resid[...] + lowered + line_of(r.down_shift)).astype(BF16)

    others = 3 * count
    if meshed:
        finish(cot_copies)
        cot_others = r.cot_all[...].reshape(others, width)
        r.cot_turned[:, :count] = dot_nt(r.select[...], r.cotangent[...]).astype(BF16)
        r.cot_turned[:, count:] = dot_nt(r.select[...], cot_others).astype(BF16)
    first_sum = dot_nn(r.query_low[...], r.in_w[0:local])
    unit, inv = normed(r.tokens[...].astype(F32))
    tokens4 = 4 * count
    if meshed:
        finish(attended_copies)
        finish(resid_copies)
        keep_part(
            "attended", dot_nn(r.resid_all[...], r.attended_all[...].reshape(tokens4, local))
        )
        attended_copies = column_first("attended")
    finish(halo_copy)
    edge_at = pl.multiple_of(HALO + edge, HALO)
    arrived = r.halo_other[...].astype(F32)
    r.key_grad[pl.ds(edge_at, HALO)] += arrived[:, :local]
    r.value_grad[pl.ds(edge_at, HALO)] += arrived[:, local:]
    low = r.key_grad[pl.ds(HALO, count)].astype(BF16)
    r.key_low[...] = low
    if meshed:
        r.mixed_all[0, :, 256:384] = r.key_low[:, own_lanes]
        key_copies = deal(r.key_low, 256)
        r.rest[2, :, : local - full] = low[:, full:]
    low = r.value_grad[pl.ds(HALO, count)].astype(BF16)
    r.value_low[...] = low
    if meshed:
        r.mixed_all[0, :, 384:512] = r.value_low[:, own_lanes]
        value_copies = deal(r.value_low, 384)
        r.rest[3, :, : local - full] = low[:, full:]
        r.mixed_all[0, :, 512:640] = r.rest[spot]
        base = links(3)
        rest_copies = started(
            [
                remote(
                    base + k,
                    r.rest.at[spots[k]],
                    r.mixed_all.at[k + 1, :, pl.ds(512, 128)],
                    plane[k],
                )
                for k in range(3)
            ]
        )
    r.small_own[8:9, local:] = column_sum(low.astype(F32))

    if meshed:
        finish(second_copies)
        second_copies = pass_half(r.second_all)
    first_sum = first_sum + dot_nn(r.key_low[...], r.in_w[local : 2 * local])
    first_sum = first_sum + dot_nn(r.value_low[...], r.in_w[2 * local :])
    r.first_own[...] = first_sum.astype(BF16)
    first_copy = sent(r.first_own, r.first_other, sibling)

    def mixed(start, stop):
        return r.mixed_all[:, :, start:stop].reshape(tokens4, stop - start)

    if meshed:
        finish(query_copies)
        keep_part("query", dot_nn(r.first_flat[...], mixed(128, 256)))
        query_copies = column_first("query")
    finish(first_copy)
    back = r.first_own[...].astype(F32) + r.first_other[...].astype(F32)
    r.small_own[0:1] = column_sum(back * unit)
    r.small_own[1:2] = column_sum(back)
    r.tokens_grad[...] += normed_back(unit, inv, line_of(r.first_gain), back)
    if not meshed:
        return

    r.small_send[0:3] = jnp.where(half == 0, r.small_own[0:3], r.small_own[3:6])
    r.small_send[3:5] = r.small_own[6:8]
    r.small_send[5:6] = r.small_own[10:11]
    r.small_send[6:8] = r.small_own[8:10]
    small_copies = spread(r.small_send, r.small_plane, plane)
    finish(second_copies)
    second_others = r.second_all[...].reshape(others, width)
    r.second_turned[:, :count] = dot_nt(r.select[...], r.second_low[...]).astype(BF16)
    r.second_turned[:, count:] = dot_nt(r.select[...], second_others).astype(BF16)

    finish(key_copies)
    finish(value_copies)
    keep_part("pair", dot_nn(r.first_flat[...], mixed(256, 512)))
    pair_copies = column_first("pair")

    part = step // 2
    near, far = plane[:2]

    def wide_first(t):
        base = links(4)
        return started(
            [
                remote(base, r.wide_a.at[t, spots[0]], r.wide_a_in.at[t, 0], near),
                remote(base + 1, r.wide_a.at[t, spots[2]], r.wide_a_in.at[t, 1], near),
                remote(base + 2, r.wide_b.at[t, spots[1]], r.wide_b_in.at[t, 0], far),
                remote(base + 3, r.wide_b.at[t, spots[2]], r.wide_b_in.at[t, 1], far),
            ]
        )

    def wide_piece(t):
        piece = slice(t * step, (t + 1) * step)
        upper = dot_nn(r.second_all[...].reshape(others, width), r.up_w[:, piece])
        active, slope = gelu_pair(upper + line_of(r.up_shift, piece))
        grad = dot_nt(r.cot_all[...].reshape(others, width), r.down_w[piece]) * slope
        down = dot_nn(r.cot_turned[:, :count], r.active_low[:, piece])
        down = down + dot_nn(r.cot_turned[:, count:], active.astype(BF16))
        up = dot_nn(r.second_turned[:, :count], r.upper_low[:, piece])
        up = up + dot_nn(r.second_turned[:, count:], grad.astype(BF16))
        for k in range(4):
            rows_here = slice(k * owners, (k + 1) * owners)
            both = jnp.concatenate([down[rows_here], up[rows_here]], axis=0).astype(BF16)
            r.wide_a[t, k] = both[:, :part]
            r.wide_b[t, k] = both[:, part:]
        return wide_first(t)

    def wide_second(t):
        finish(wide_copies[t])
        r.wide_a_sum[t] = joined(r.wide_a[t, spots[1]], r.wide_a_in[t, 1]).astype(BF16)
        r.wide_b_sum[t] = joined(r.wide_b[t, spots[0]], r.wide_b_in[t, 1]).astype(BF16)
        return sent(r.wide_a_sum.at[t], r.wide_a_last.at[t], far) + sent(
            r.wide_b_sum.at[t], r.wide_b_last.at[t], near
        )

    wide_copies = [wide_piece(0)]
    finish(rest_copies)
    term = dot_nn(r.first_flat[...], mixed(512, 640))
    for k in range(4):
        upper_half = term[k * rows4 : k * rows4 + rows4 // 2, : local - full]
        lower_half = term[k * rows4 + rows4 // 2 : (k + 1) * rows4, : local - full]
        r.rest_part[k] = jnp.concatenate([upper_half, lower_half], axis=1).astype(BF16)
    rest_copies = column_first("rest")
    finish(attended_copies)
    attended_copies = column_second("attended")
    finish(query_copies)
    query_copies = column_second("query")
    wide_copies.append(wide_piece(1))
    finish(small_copies)
    small_sum = r.small_send[0:6]
    for k in range(3):
        small_sum = small_sum + r.small_plane[k, 0:6]
    r.small_z[0:6] = small_sum
    r.small_z[6:7] = r.small_send[6:7] + r.small_plane[1, 6:7]
    r.small_z[7:8] = r.small_plane[0, 6:7] + r.small_plane[2, 6:7]
    r.small_z[8:9] = r.small_send[7:8]
    r.small_z[9:10] = r.small_plane[0, 7:8]
    column_copies = spread(r.small_z, r.small_column, column)
    wide_copies.append(wide_piece(2))
    finish(pair_copies)
    pair_copies = column_second("pair")
    finish(rest_copies)
    rest_copies = column_second("rest")
    last_copies = [wide_second(0)]
    last_copies.append(wide_second(1))
    finish(attended_copies)
    r.out_share[...] = column_total("attended")
    finish(query_copies)
    total = column_total("query")
    for k in range(4):
        r.back_stage[k, :, :128] = total[k * owners : (k + 1) * owners].astype(BF16)
    last_copies.append(wide_second(2))
    finish(pair_copies)
    total = column_total("pair")
    for k in range(4):
        r.back_stage[k, :, 128:384] = total[k * owners : (k + 1) * owners].astype(BF16)
    finish(rest_copies)
    total = column_total("rest")
    for k in range(4):
        lanes = slice(k // 2 * (local - full), (k // 2 + 1) * (local - full))
        rows_here = slice(k % 2 * owners, (k % 2 + 1) * owners)
        r.back_stage[k, :, 384 : 384 + local - full] = total[rows_here, lanes].astype(BF16)
    r.back_done[spot] = r.back_stage[spot]
    back_copies = hand_out(r.back_stage, r.back_done)
    finish(column_copies)
    small_sum = r.small_z[0:6]
    for k in range(3):
        small_sum = small_sum + r.small_column[k, 0:6]
    r.small_half[0:6] = small_sum
    small_copies = sent(r.small_half, r.small_other, sibling)
    time_lines = [r.small_z[8:10]] + [r.small_column[k, 8:10] for k in range(3)]
    time_lines = jnp.concatenate(time_lines, axis=0).astype(BF16)
    r.time_turned[...] = dot_nt(r.select[...], time_lines)
    time_cut = r.time_turned[pl.ds(pl.multiple_of(spot * owners, 8), owners)]
    time_share = jnp.zeros((owners, width), F32)
    for k in range(4):
        source = r.small_z if k == 0 else r.small_column.at[k - 1]
        for line in range(2):
            factor = time_cut[:, 2 * k + line : 2 * k + line + 1]
            time_share = time_share + factor * source[6 + line : 7 + line]
    r.time_share[0] = time_share[:, :local]
    r.time_share[1] = time_share[:, local:]

    def wide_total(t):
        finish(last_copies[t])
        left = joined(r.wide_a[t, spot], r.wide_a_in[t, 0]) + r.wide_a_last[t].astype(F32)
        right = joined(r.wide_b[t, spot], r.wide_b_in[t, 0]) + r.wide_b_last[t].astype(F32)
        for at, total in ((t * step, left), (t * step + part, right)):
            r.down_share[:, at : at + part] = total[:owners]
            r.up_share[:, at : at + part] = total[owners:]

    wide_total(0)
    wide_total(1)
    finish(small_copies)
    low_half, high_half = r.small_half[0:3], r.small_other[0:3]
    r.small_sums[0:3] = jnp.where(half == 0, low_half, high_half)
    r.small_sums[3:6] = jnp.where(half == 0, high_half, low_half)
    r.small_sums[6:8] = r.small_half[3:5]
    r.small_sums[8:16] = jnp.broadcast_to(r.small_half[5:6], (8, width))
    finish(back_copies)
    for k in range(4):
        piece = slice(k * 128, (k + 1) * 128)
        for line in range(3):
            lanes = slice(line * 128, (line + 1) * 128)
            r.in_share[line, :, piece] = r.back_done[k, :, lanes].astype(F32)
        if k > 0:
            rest = r.back_done[k, :, 384 : 384 + local - full].astype(F32)
            r.in_share[k - 1, :, full:] = rest
    wide_total(2)


def final_kernel(heads, names, *refs):
    r = types.SimpleNamespace(**dict(zip(names, refs, strict=True)))
    copies = [
        pltpu.make_async_copy(source, target, r.sems.at[i])
        for i, (source, target) in enumerate(
            (
                (r.output, r.output_done),
                (r.tokens_grad, r.tokens_done),
                (r.in_share, r.in_done),
                (r.out_share, r.out_done),
                (r.up_share, r.up_done),
                (r.down_share, r.down_done),
            )
        )
    ]
    for copy in copies:
        copy.start()
    width = r.small_sums.shape[1]
    for line, target in enumerate(
        (
            r.first_gain_done,
            r.first_shift_done,
            r.out_shift_done,
            r.second_gain_done,
            r.second_shift_done,
            r.down_shift_done,
        )
    ):
        target[...] = r.small_sums[line]
    for line in range(r.up_shift_done.shape[0] // width):
        r.up_shift_done[line * width : (line + 1) * width] = r.small_sums[6 + line]
    for head in range(heads):
        r.bias_done[head : head + 1] = r.small_sums[8:9, head * 128 : head * 128 + TAPS]
    local = r.time_share.shape[2]
    for k in range(2):
        r.time_done[:, k, :] = r.time_share[k]
    for copy in copies:
        copy.wait()


def final_call(results, heads, hidden):
    inputs = dict(
        output=results.output,
        tokens_grad=results.tokens_grad,
        in_share=results.in_share,
        out_share=results.out_share,
        up_share=results.up_share,
        down_share=results.down_share,
        small_sums=results.small_sums,
        time_share=results.time_share,
    )
    width = results.small_sums.shape[1]
    _, owners, local = results.time_share.shape
    struct = jax.ShapeDtypeStruct
    line = struct((width,), F32)
    outs = dict(
        output_done=struct(results.output.shape, BF16),
        tokens_done=struct(results.tokens_grad.shape, F32),
        in_done=struct(results.in_share.shape, F32),
        out_done=struct(results.out_share.shape, F32),
        up_done=struct(results.up_share.shape, F32),
        down_done=struct(results.down_share.shape, F32),
        first_gain_done=line,
        first_shift_done=line,
        out_shift_done=line,
        second_gain_done=line,
        second_shift_done=line,
        down_shift_done=line,
        up_shift_done=struct((hidden,), F32),
        bias_done=struct((heads, TAPS), F32),
        time_done=struct((owners, 2, local), F32),
    )
    vmem = pl.BlockSpec(memory_space=pltpu.VMEM)
    hbm = pl.BlockSpec(memory_space=pltpu.HBM)
    done = pl.pallas_call(
        functools.partial(final_kernel, heads, [*inputs, *outs, "sems"]),
        out_shape=list(outs.values()),
        in_specs=[vmem] * 8,
        out_specs=[hbm] * 6 + [vmem] * (len(outs) - 6),
        scratch_shapes=[pltpu.SemaphoreType.DMA((6,))],
        name="final",
        compiler_params=pltpu.CompilerParams(vmem_limit_bytes=61 * 1024 * 1024),
    )(*inputs.values())
    return types.SimpleNamespace(**dict(zip(outs, done, strict=True)))


def layer_call(meshed, inputs, smalls, weights):
    count, width = inputs["tokens"].shape
    local = weights["out_hbm"].shape[0]
    hidden = weights["up_hbm"].shape[1]
    heads = smalls["bias_table"].shape[0]
    tokens4, rows4 = 4 * count, width // 4
    owners, part = rows4 // 4, hidden // 6
    outs = dict(output=((count, width), BF16), tokens_grad=((count, width), F32))
    kept = dict(
        first_low=((count, width), BF16),
        second_low=((count, width), BF16),
        active_low=((count, hidden), BF16),
        upper_low=((count, hidden), BF16),
        resid_low=((count, width), BF16),
        attended_low=((count, local), BF16),
        query_low=((count, local), BF16),
        key_low=((count, local), BF16),
        value_low=((count, local), BF16),
        small_own=((16, width), F32),
    )
    scratch = dict(
        time_w=((2 * local, width), BF16),
        in_w=((3 * local, width), BF16),
        out_w=((local, width), BF16),
        up_w=((width, hidden), BF16),
        down_w=((hidden, width), BF16),
        halo_tokens=((HALO, width), BF16),
        query=((count, local), BF16),
        keys=((KEYS, local), BF16),
        values=((KEYS, local), BF16),
        prob=((heads, count, KEYS), F32),
        key_grad=((KEYS, local), F32),
        value_grad=((KEYS, local), F32),
        attended_grad=((count, local), BF16),
        query_grad=((count, local), F32),
        attended=((count, local), F32),
        resid=((count, width), F32),
        part_own=((count, width), F32),
        part_other=((count, width), F32),
        halo_own=((HALO, 2 * local), BF16),
        halo_other=((HALO, 2 * local), BF16),
        bias_tiles=((heads, COLS, 128), F32),
    )
    scratch |= dict(
        down_own=((count, width), BF16),
        down_other=((count, width), BF16),
        second_own=((count, width), BF16),
        second_other=((count, width), BF16),
        first_own=((count, width), BF16),
        first_other=((count, width), BF16),
    )
    if meshed:
        outs |= dict(
            small_sums=((16, width), F32),
            in_share=((3, owners, local), F32),
            time_share=((2, owners, local), F32),
            out_share=((owners, local), F32),
            up_share=((owners, hidden), F32),
            down_share=((owners, hidden), F32),
        )
        scratch |= kept
        scratch |= dict(
            cot_all=((3, count, width), BF16),
            second_all=((3, count, width), BF16),
            first_all=((4, count, width), BF16),
            first_flat=((width, tokens4), BF16),
            attended_all=((4, count, local), BF16),
            resid_turned=((width, count), F32),
            resid_stage=((4, rows4, count), BF16),
            resid_all=((rows4, tokens4), BF16),
            select=((rows4, width), BF16),
            cot_turned=((rows4, tokens4), BF16),
            second_turned=((rows4, tokens4), BF16),
            small_send=((8, width), F32),
            small_plane=((3, 8, width), F32),
            small_z=((10, width), F32),
            small_column=((3, 10, width), F32),
            small_half=((8, width), F32),
            small_other=((8, width), F32),
            time_turned=((rows4, 8), F32),
            mixed_all=((4, count, 640), BF16),
            rest=((4, count, 128), BF16),
            back_stage=((4, owners, 512), BF16),
            back_done=((4, owners, 512), BF16),
        )
        for name, rows, wide in (
            ("attended", owners, local),
            ("query", rows4, 128),
            ("pair", rows4, 256),
            ("rest", rows4 // 2, 128),
        ):
            scratch[name + "_part"] = ((4, rows, wide), BF16)
            scratch[name + "_in"] = ((2, rows, wide), BF16)
            scratch[name + "_sum"] = ((rows, wide), BF16)
            scratch[name + "_last"] = ((rows, wide), BF16)
        for name in ("wide_a", "wide_b"):
            scratch[name] = ((3, 4, 2 * owners, part), BF16)
            scratch[name + "_in"] = ((3, 2, 2 * owners, part), BF16)
            scratch[name + "_sum"] = ((3, 2 * owners, part), BF16)
            scratch[name + "_last"] = ((3, 2 * owners, part), BF16)
    else:
        outs |= kept
    links = 80 if meshed else 6
    sems = dict(weight_sems=5, send_sems=links, recv_sems=links)
    vmem = pl.BlockSpec(memory_space=pltpu.VMEM)
    smem = pl.BlockSpec(memory_space=pltpu.SMEM)
    anywhere = pl.BlockSpec(memory_space=pl.ANY)
    names = [*inputs, *smalls, *weights, *outs, *scratch, *sems]
    results = pl.pallas_call(
        functools.partial(layer_kernel, names, meshed),
        out_shape=[jax.ShapeDtypeStruct(*shape) for shape in outs.values()],
        in_specs=[vmem] * len(inputs) + [smem] * len(smalls) + [anywhere] * len(weights),
        out_specs=[vmem] * len(outs),
        scratch_shapes=[pltpu.VMEM(*shape) for shape in scratch.values()]
        + [pltpu.SemaphoreType.DMA((number,)) for number in sems.values()],
        name="layer",
        compiler_params=pltpu.CompilerParams(
            collective_id=0, has_side_effects=True, vmem_limit_bytes=61 * 1024 * 1024
        ),
    )(*inputs.values(), *smalls.values(), *weights.values())
    return types.SimpleNamespace(**dict(zip(outs, results, strict=True)))


def time_features(timesteps, width):
    half = width // 2
    freqs = jnp.exp(jnp.arange(half, dtype=F32) * (-math.log(10000.0) / half))
    angles = timesteps.astype(F32)[:, None] * freqs[None, :]
    return jnp.concatenate([jnp.cos(angles), jnp.sin(angles)], axis=1)


def on_device(
    tokens,
    timesteps,
    first_gain,
    first_shift,
    project_in,
    time_weight,
    bias_table,
    bias_index,
    project_out,
    out_shift,
    second_gain,
    second_shift,
    up_weight,
    up_shift,
    down_weight,
    down_shift,
    cotangent,
):
    batch, band_rows, columns, width = tokens.shape
    local = project_in.shape[2]
    count = batch * band_rows * columns
    assert batch == 1 and columns == COLS
    meshed = lax.axis_size("img") == 8 and lax.axis_size("band") == 2
    cot = cotangent.reshape(count, width)
    inputs = dict(
        tokens=tokens.reshape(count, width),
        cotangent=cot,
        time_low=time_features(timesteps, width).astype(BF16),
        first_gain=first_gain,
        first_shift=first_shift,
        out_shift=out_shift,
        second_gain=second_gain,
        second_shift=second_shift,
        up_shift=up_shift,
        down_shift=down_shift,
    )
    smalls = dict(bias_table=bias_table, bias_index=bias_index)
    weights = dict(
        time_hbm=jnp.transpose(time_weight, (1, 2, 0)).reshape(2 * local, width),
        in_hbm=jnp.transpose(project_in, (1, 2, 0)).reshape(3 * local, width),
        out_hbm=project_out,
        up_hbm=up_weight,
        down_hbm=down_weight,
    )
    r = layer_call(meshed, inputs, smalls, weights)
    heads = bias_table.shape[0]
    if meshed:
        f = final_call(r, heads, up_shift.shape[0])
        return (
            f.output_done.reshape(tokens.shape),
            f.tokens_done.reshape(tokens.shape),
            f.first_gain_done,
            f.first_shift_done,
            jnp.transpose(f.in_done, (1, 0, 2)),
            f.time_done,
            f.bias_done,
            jnp.transpose(f.out_done),
            f.out_shift_done,
            f.second_gain_done,
            f.second_shift_done,
            f.up_done,
            f.up_shift_done,
            jnp.transpose(f.down_done),
            f.down_shift_done,
        )
    axes = ("img", "band")
    grads = (
        dot_tn(r.first_low, jnp.concatenate([r.query_low, r.key_low, r.value_low], axis=1)),
        dot_tn(r.resid_low, r.attended_low),
        dot_tn(r.second_low, r.upper_low),
        dot_tn(cot, r.active_low),
    )
    in_share, out_share, up_share, down_share = [
        lax.psum_scatter(g.astype(BF16), axes, scatter_dimension=0, tiled=True).astype(F32)
        for g in grads
    ]
    rows = in_share.shape[0]
    in_share = in_share.reshape(rows, 3, local)
    times = lax.all_gather(r.small_own[8:10], axes, axis=0)
    here = lax.axis_index(axes) * rows
    time_cut = lax.dynamic_slice_in_dim(times[:, 1], here, rows, axis=1)
    time_share = jnp.einsum("nd,nk->dk", time_cut, times[:, 0], precision=HIGHEST)
    time_share = time_share.reshape(rows, 2, local)
    small = lax.psum(r.small_own, axes)
    return (
        r.output.reshape(tokens.shape),
        r.tokens_grad.reshape(tokens.shape),
        small[0],
        small[1],
        in_share,
        time_share,
        small[10, : heads * 128].reshape(heads, 128)[:, :TAPS],
        jnp.transpose(out_share),
        small[2],
        small[3],
        small[4],
        up_share,
        small[6:8].reshape(-1)[: up_shift.shape[0]],
        jnp.transpose(down_share),
        small[5],
    )


def solution(mesh):
    return jax.shard_map(
        on_device,
        mesh=mesh,
        in_specs=(
            P("img", "band", None, None),
            P("img"),
            P(),
            P(),
            P(None, None, "head"),
            P(None, None, "head"),
            P("head", None),
            P(),
            P("head", None),
            P(),
            P(),
            P(),
            P(None, "head"),
            P("head"),
            P("head", None),
            P(),
            P("img", "band", None, None),
        ),
        out_specs=(
            P("img", "band", None, None),
            P("img", "band", None, None),
            P(),
            P(),
            P(("img", "band"), None, "head"),
            P(("img", "band"), None, "head"),
            P("head", None),
            P("head", ("img", "band")),
            P(),
            P(),
            P(),
            P(("img", "band"), "head"),
            P("head"),
            P("head", ("img", "band")),
            P(),
        ),
        check_vma=False,
    )
```

time: 165 us -> 81.1 us (0.49); the launches traced: 162 us -> 80.9 us
  Pallas kernels: 135 us -> 78.7 us
  local copies, waits for them, and re-layouts: 24.4 us -> 0.01 us
    pallas_call x1, Pallas kernels: 135 us -> 74.4 us  [layer_call(): pl.pallas_call(functools.partial(layer_kernel, names, meshed), out_shape=...]
    unnamed x11 -> x0, local copies, waits for them, and re-layouts: 10.7 us -> none
    broadcast_in_dim x7 -> x0, local copies, waits for them, and re-layouts: 9.06 us -> none  [the longest x1 1.31 us: on_device(): up_shift[None]]
    pallas_call x0 -> x1, Pallas kernels: none -> 4.33 us  [final_call(): pl.pallas_call(functools.partial(final_kernel, heads, [*inputs, *outs, 's...]
    slice x3 -> x0, local copies, waits for them, and re-layouts: 3.99 us -> none  [the longest x1 1.76 us: on_device(): small[5]]
where the time goes in v3:
time: 81.1 us; the launch traced here: 80.9 us
  Pallas kernels  78.7 us (97%)
  between operations  1.48 us (2%)
    pallas_call x1, Pallas kernels, layer_call(): pl.pallas_call(functools.partial(layer_kernel, names, meshed), out_shape=...  74.4 us
    pallas_call x1, Pallas kernels, final_call(): pl.pallas_call(functools.partial(final_kernel, heads, [*inputs, *outs, 's...  4.33 us

profile of v3, /device:TPU:0, one launch (start us, length us, event | category | flops | bytes accessed | tf_op | source)
XLA Modules:
  0.0 80.9 jit_solution(10305326838674722340)
XLA Ops:
  1.3 0.1 sine_convert_fusion
  1.4 0.7 pad_maximum_fusion.refs_2_
  2.0 74.4 %layer.1 = (bf16[128,1152]{1,0:T(8,128)(2,1)}, f32[128,1152]{1,0:T(8,128)}, f32[16,1152]{1,0:T(8,128)}, f32[3,72,576]{2,1,0:T(8,128)}, f32[2,72,576]{2,1,0:T(8,1...) custom-call(bf16[128,1152]{1,0:T(8,128)(2,1)} %bitcast.16, bf16[128,1152]{1,0:T(8,128)(2,1)} %bitcast.17, ...), custom_call_target="tpu_custom_call" | custom-call | tf_op jit(solution)/shard_map/layer/pallas_call | solution.py:839
  76.4 4.3 %final.1 = (bf16[128,1152]{1,0:T(8,128)(2,1)}, f32[128,1152]{1,0:T(8,128)}, f32[3,72,576]{2,1,0:T(8,128)}, f32[72,576]{1,0:T(8,128)}, f32[72,2304]{1,0:T(8,128)}...) custom-call(bf16[128,1152]{1,0:T(8,128)(2,1)} %get-tuple-element.38., ...), custom_call_target="tpu_custom_call" | custom-call | tf_op jit(solution)/shard_map/final/pallas_call | solution.py:719
  (2 shorter events, 0.0 us)

commit v4 on v3

--- a/solution.py
+++ b/solution.py
@@ -4,6 +4,7 @@
 
 import jax
 import jax.numpy as jnp
+import numpy as np
 from jax import lax
 from jax.experimental import pallas as pl
 from jax.experimental.pallas import tpu as pltpu
@@ -26,6 +27,7 @@
 F32 = jnp.float32
 GELU_A = math.sqrt(2.0 / math.pi)
 GELU_B = 0.044715
+TURN = (6.28125, 0.0019350051879882812, 3.019916e-07)
 
 
 def dot_nn(a, b):
@@ -67,6 +69,18 @@
     return jnp.sum(values, axis=0, keepdims=True)
 
 
+def cos_sin(angle):
+    turns = jnp.floor(angle * (0.5 / math.pi) + 0.5)
+    rest = ((angle - turns * TURN[0]) - turns * TURN[1]) - turns * TURN[2]
+    square = rest * rest
+    cosine = jnp.full(angle.shape, 1.0 / math.factorial(18), F32)
+    sine = jnp.full(angle.shape, 1.0 / math.factorial(19), F32)
+    for power in range(16, -1, -2):
+        cosine = 1.0 / math.factorial(power) - cosine * square
+        sine = 1.0 / math.factorial(power + 1) - sine * square
+    return cosine, sine * rest
+
+
 def line_of(vector, piece=slice(None)):
     return vector[piece][None, :]
 
@@ -77,7 +91,7 @@
     return first, last
 
 
-def layer_kernel(names, meshed, *refs):
+def layer_kernel(names, inputs, small_names, weight_names, meshed, *refs):
     r = types.SimpleNamespace(**dict(zip(names, refs, strict=True)))
     count, width = r.tokens.shape
     local = r.query.shape[1]
@@ -100,20 +114,15 @@
         column = [(at * 2 + x, band, half) for at in heights]
         peers = [sibling, *plane, *column]
 
-    weight_copies = [
-        pltpu.make_async_copy(source, target, r.weight_sems.at[i])
-        for i, (source, target) in enumerate(
-            (
-                (r.time_hbm, r.time_w),
-                (r.in_hbm, r.in_w),
-                (r.out_hbm, r.out_w),
-                (r.up_hbm, r.up_w),
-                (r.down_hbm, r.down_w),
-            )
-        )
-    ]
-    for copy in weight_copies:
-        copy.start()
+    loads = {}
+    for name in (*inputs[:4], *small_names, *weight_names[:2], *inputs[4:], *weight_names[2:]):
+        source, target = getattr(r, name + "_hbm"), getattr(r, name)
+        loads[name] = pltpu.make_async_copy(source, target, r.load_sems.at[len(loads)])
+        loads[name].start()
+
+    def loaded(*wanted):
+        for name in wanted:
+            loads.pop(name).wait()
 
     barrier = pltpu.get_barrier_semaphore()
     for other in peers:
@@ -123,6 +132,7 @@
 
     def links(number):
         used[0] += number
+        assert used[0] <= r.send_sems.shape[0]
         return used[0] - number
 
     def remote(index, source, target, device):
@@ -206,16 +216,24 @@
             [remote(base + k, source.at[mine], slots.at[k, mine], group[k]) for k in range(3)]
         )
 
-    def pass_half(slots):
-        return sent(slots.at[:, mine], slots.at[:, mine], sibling)
-
+    def pass_half(slots, slot, number):
+        part = slots.at[pl.ds(slot, number), mine]
+        return sent(part, part, sibling)
+
+    loaded(*inputs[:3])
     unit, _ = normed(r.tokens[...].astype(F32))
     own_low = (unit * line_of(r.first_gain) + line_of(r.first_shift)).astype(BF16)
     r.first_low[...] = own_low
 
+    loaded(inputs[3])
+    angle = r.step_index[0].astype(F32) * line_of(r.frequencies)
+    cosine, sine = cos_sin(angle)
+    r.time_low[:, : width // 2] = cosine.astype(BF16)
+    r.time_low[:, width // 2 :] = sine.astype(BF16)
     pl.semaphore_wait(barrier, len(peers))
     edge = pl.multiple_of((1 - band) * (count - HALO), HALO)
     token_copy = sent(r.tokens.at[pl.ds(edge, HALO)], r.halo_tokens, beside)
+    loaded(inputs[4])
     if meshed:
         cot_copies = spread_half(r.cotangent, r.cot_all, column)
         r.first_all[0] = own_low
@@ -225,13 +243,13 @@
         place = lax.broadcasted_iota(jnp.int32, (rows4, width), 1)
         place = place - lax.broadcasted_iota(jnp.int32, (rows4, width), 0)
         r.select[...] = (place == rows4 * z).astype(F32).astype(BF16)
-    weight_copies[0].wait()
+    loaded(weight_names[0])
     time_rows = jnp.broadcast_to(r.time_low[...], (8, width))
     time_proj = dot_nt(time_rows, r.time_w[...])[0:1]
     halo_at = pl.multiple_of((1 - band) * (count + HALO), HALO)
     blank_at = pl.multiple_of(band * (count + HALO), HALO)
     tail = KEYS - count - 2 * HALO
-    weight_copies[1].wait()
+    loaded(weight_names[1])
     r.query[...] = (dot_nt(own_low, r.in_w[0:local]) + time_proj[:, :local]).astype(BF16)
     r.keys[pl.ds(HALO, count)] = dot_nt(own_low, r.in_w[local : 2 * local]).astype(BF16)
     projected = dot_nt(own_low, r.in_w[2 * local : 3 * local]) + time_proj[:, local:]
@@ -246,6 +264,7 @@
     projected = dot_nt(halo_low, r.in_w[2 * local : 3 * local]) + time_proj[:, local:]
     r.values[pl.ds(halo_at, HALO)] = projected.astype(BF16)
 
+    loaded(*small_names)
     lane = lax.broadcasted_iota(jnp.int32, (COLS, 128), 1)
     row = lax.broadcasted_iota(jnp.int32, (COLS, 128), 0)
     col_step = lane % COLS - row
@@ -287,7 +306,7 @@
         r.attended[:, first:last] += jnp.where(own, mixed, 0.0)
 
     r.attended_low[...] = r.attended[...].astype(BF16)
-    weight_copies[2].wait()
+    loaded(weight_names[2], *inputs[5:8])
     r.part_own[...] = dot_nn(r.attended_low[...], r.out_w[...])
     part_copy = sent(r.part_own, r.part_other, sibling)
     if meshed:
@@ -296,6 +315,8 @@
         r.rest[...] = jnp.zeros(r.rest.shape, BF16)
         r.back_stage[...] = jnp.zeros(r.back_stage.shape, BF16)
         r.small_half[6:8] = jnp.zeros((2, width), F32)
+    loaded(*weight_names[3:], *inputs[8:])
+    r.active_grad[...] = dot_nt(r.cotangent[...], r.down_w[...])
     finish(part_copy)
     after = r.tokens[...].astype(F32) + (r.part_own[...] + r.part_other[...]) + line_of(r.out_shift)
     r.resid[...] = after
@@ -306,21 +327,16 @@
 
     if meshed:
         finish(first_copies)
-        first_copies = pass_half(r.first_all.at[pl.ds(1, 3)])
-    weight_copies[3].wait()
-    weight_copies[4].wait()
+        first_copies = pass_half(r.first_all, 1, 3)
     step = hidden // 3
-    down_sum = None
     second_sum = None
     for at in range(0, hidden, step):
         piece = slice(at, at + step)
         upper = dot_nn(r.second_low[...], r.up_w[:, piece]) + line_of(r.up_shift, piece)
         active, slope = gelu_pair(upper)
         active = active.astype(BF16)
-        r.active_low[:, piece] = active
-        term = dot_nn(active, r.down_w[piece])
-        down_sum = term if down_sum is None else down_sum + term
-        grad = dot_nt(r.cotangent[...], r.down_w[piece]) * slope
+        r.active_low[0:count, piece] = active
+        grad = r.active_grad[:, piece] * slope
         sums = column_sum(grad)
         for line in range(-(-hidden // width)):
             low_at, high_at = max(at, line * width), min(at + step, (line + 1) * width)
@@ -329,16 +345,14 @@
                     sums[:, low_at - at : high_at - at]
                 )
         grad = grad.astype(BF16)
-        r.upper_low[:, piece] = grad
+        r.upper_low[0:count, piece] = grad
         term = dot_nt(grad, r.up_w[:, piece])
         second_sum = term if second_sum is None else second_sum + term
     r.second_own[...] = second_sum.astype(BF16)
     second_copy = sent(r.second_own, r.second_other, sibling)
-    r.down_own[...] = down_sum.astype(BF16)
+    r.down_own[...] = dot_nn(r.active_low[0:count], r.down_w[...]).astype(BF16)
     down_copy = sent(r.down_own, r.down_other, sibling)
     if meshed:
-        finish(cot_copies)
-        cot_copies = pass_half(r.cot_all)
         finish(first_copies)
         r.first_flat[...] = jnp.transpose(r.first_all[...].reshape(4 * count, width))
     cot = r.cotangent[...].astype(F32)
@@ -353,27 +367,6 @@
     r.small_own[2:3] = column_sum(grad)
     r.resid_low[...] = grad.astype(BF16)
     r.attended_grad[...] = dot_nt(r.resid_low[...], r.out_w[...]).astype(BF16)
-    if meshed:
-        r.resid_turned[...] = jnp.transpose(grad)
-        for k, at in enumerate([spot] + spots):
-            lines = [
-                r.resid_turned[pl.ds(pl.multiple_of(line * rows4 + owners * at, 8), owners)]
-                for line in range(4)
-            ]
-            r.resid_stage[k] = jnp.concatenate(lines, axis=0).astype(BF16)
-        r.resid_all[:, 0:count] = r.resid_stage[0]
-        base = links(3)
-        resid_copies = started(
-            [
-                remote(
-                    base + k,
-                    r.resid_stage.at[k + 1],
-                    r.resid_all.at[:, pl.ds((k + 1) * count, count)],
-                    plane[k],
-                )
-                for k in range(3)
-            ]
-        )
     r.query_grad[...] = jnp.zeros(r.query_grad.shape, F32)
     r.key_grad[...] = jnp.zeros(r.key_grad.shape, F32)
     r.value_grad[...] = jnp.zeros(r.value_grad.shape, F32)
@@ -395,6 +388,9 @@
         r.query_grad[:, first:last] += jnp.where(own, dot_nn(low, r.keys[:, first:last]), 0.0)
         r.key_grad[:, first:last] += dot_tn(low, queries)
 
+    if meshed:
+        finish(cot_copies[:1] + second_copies[:1])
+        near_copies = pass_half(r.cot_all, 0, 1) + pass_half(r.second_all, 0, 1)
     r.halo_own[:, :local] = r.key_grad[pl.ds(halo_at, HALO)].astype(BF16)
     r.halo_own[:, local:] = r.value_grad[pl.ds(halo_at, HALO)].astype(BF16)
     halo_copy = sent(r.halo_own, r.halo_other, beside)
@@ -422,23 +418,47 @@
     lowered = r.down_own[...].astype(F32) + r.down_other[...].astype(F32)
     r.output[...] = (r.resid[...] + lowered + line_of(r.down_shift)).astype(BF16)
 
-    others = 3 * count
-    if meshed:
-        finish(cot_copies)
-        cot_others = r.cot_all[...].reshape(others, width)
-        r.cot_turned[:, :count] = dot_nt(r.select[...], r.cotangent[...]).astype(BF16)
-        r.cot_turned[:, count:] = dot_nt(r.select[...], cot_others).astype(BF16)
+    if meshed:
+        r.resid_turned[...] = jnp.transpose(r.tokens_grad[...])
+        for k, at in enumerate([spot] + spots):
+            lines = [
+                r.resid_turned[pl.ds(pl.multiple_of(line * rows4 + owners * at, 8), owners)]
+                for line in range(4)
+            ]
+            r.resid_stage[k] = jnp.concatenate(lines, axis=0).astype(BF16)
+        r.resid_all[:, 0:count] = r.resid_stage[0]
+        base = links(3)
+        resid_copies = started(
+            [
+                remote(
+                    base + k,
+                    r.resid_stage.at[k + 1],
+                    r.resid_all.at[:, pl.ds((k + 1) * count, count)],
+                    plane[k],
+                )
+                for k in range(3)
+            ]
+        )
     first_sum = dot_nn(r.query_low[...], r.in_w[0:local])
     unit, inv = normed(r.tokens[...].astype(F32))
     tokens4 = 4 * count
     if meshed:
-        finish(attended_copies)
-        finish(resid_copies)
-        keep_part(
-            "attended", dot_nn(r.resid_all[...], r.attended_all[...].reshape(tokens4, local))
-        )
-        attended_copies = column_first("attended")
+        finish(near_copies)
+
+        def near_piece(t):
+            piece = slice(t * step, (t + 1) * step)
+            upper = dot_nn(r.second_all[0], r.up_w[:, piece]) + line_of(r.up_shift, piece)
+            active, slope = gelu_pair(upper)
+            r.active_low[count:, piece] = active.astype(BF16)
+            grad = dot_nt(r.cot_all[0], r.down_w[piece]) * slope
+            r.upper_low[count:, piece] = grad.astype(BF16)
+
+        near_piece(0)
+        near_piece(1)
     finish(halo_copy)
+    if meshed:
+        finish(cot_copies[1:])
+        cot_copies = pass_half(r.cot_all, 1, 2)
     edge_at = pl.multiple_of(HALO + edge, HALO)
     arrived = r.halo_other[...].astype(F32)
     r.key_grad[pl.ds(edge_at, HALO)] += arrived[:, :local]
@@ -470,9 +490,6 @@
         )
     r.small_own[8:9, local:] = column_sum(low.astype(F32))
 
-    if meshed:
-        finish(second_copies)
-        second_copies = pass_half(r.second_all)
     first_sum = first_sum + dot_nn(r.key_low[...], r.in_w[local : 2 * local])
     first_sum = first_sum + dot_nn(r.value_low[...], r.in_w[2 * local :])
     r.first_own[...] = first_sum.astype(BF16)
@@ -485,6 +502,9 @@
         finish(query_copies)
         keep_part("query", dot_nn(r.first_flat[...], mixed(128, 256)))
         query_copies = column_first("query")
+    if meshed:
+        finish(second_copies[1:])
+        far_copies = pass_half(r.second_all, 1, 2)
     finish(first_copy)
     back = r.first_own[...].astype(F32) + r.first_other[...].astype(F32)
     r.small_own[0:1] = column_sum(back * unit)
@@ -492,21 +512,6 @@
     r.tokens_grad[...] += normed_back(unit, inv, line_of(r.first_gain), back)
     if not meshed:
         return
-
-    r.small_send[0:3] = jnp.where(half == 0, r.small_own[0:3], r.small_own[3:6])
-    r.small_send[3:5] = r.small_own[6:8]
-    r.small_send[5:6] = r.small_own[10:11]
-    r.small_send[6:8] = r.small_own[8:10]
-    small_copies = spread(r.small_send, r.small_plane, plane)
-    finish(second_copies)
-    second_others = r.second_all[...].reshape(others, width)
-    r.second_turned[:, :count] = dot_nt(r.select[...], r.second_low[...]).astype(BF16)
-    r.second_turned[:, count:] = dot_nt(r.select[...], second_others).astype(BF16)
-
-    finish(key_copies)
-    finish(value_copies)
-    keep_part("pair", dot_nn(r.first_flat[...], mixed(256, 512)))
-    pair_copies = column_first("pair")
 
     part = step // 2
     near, far = plane[:2]
@@ -524,13 +529,13 @@
 
     def wide_piece(t):
         piece = slice(t * step, (t + 1) * step)
-        upper = dot_nn(r.second_all[...].reshape(others, width), r.up_w[:, piece])
+        upper = dot_nn(r.second_all[1:].reshape(2 * count, width), r.up_w[:, piece])
         active, slope = gelu_pair(upper + line_of(r.up_shift, piece))
-        grad = dot_nt(r.cot_all[...].reshape(others, width), r.down_w[piece]) * slope
-        down = dot_nn(r.cot_turned[:, :count], r.active_low[:, piece])
-        down = down + dot_nn(r.cot_turned[:, count:], active.astype(BF16))
-        up = dot_nn(r.second_turned[:, :count], r.upper_low[:, piece])
-        up = up + dot_nn(r.second_turned[:, count:], grad.astype(BF16))
+        grad = dot_nt(r.cot_all[1:].reshape(2 * count, width), r.down_w[piece]) * slope
+        down = dot_nn(r.cot_turned[:, : 2 * count], r.active_low[:, piece])
+        down = down + dot_nn(r.cot_turned[:, 2 * count :], active.astype(BF16))
+        up = dot_nn(r.second_turned[:, : 2 * count], r.upper_low[:, piece])
+        up = up + dot_nn(r.second_turned[:, 2 * count :], grad.astype(BF16))
         for k in range(4):
             rows_here = slice(k * owners, (k + 1) * owners)
             both = jnp.concatenate([down[rows_here], up[rows_here]], axis=0).astype(BF16)
@@ -546,19 +551,51 @@
             r.wide_b_sum.at[t], r.wide_b_last.at[t], near
         )
 
+    def wide_total(t):
+        finish(last_copies[t])
+        left = joined(r.wide_a[t, spot], r.wide_a_in[t, 0]) + r.wide_a_last[t].astype(F32)
+        right = joined(r.wide_b[t, spot], r.wide_b_in[t, 0]) + r.wide_b_last[t].astype(F32)
+        for at, total in ((t * step, left), (t * step + part, right)):
+            r.down_share[:, at : at + part] = total[:owners]
+            r.up_share[:, at : at + part] = total[owners:]
+
+    r.small_send[0:3] = jnp.where(half == 0, r.small_own[0:3], r.small_own[3:6])
+    r.small_send[3:5] = r.small_own[6:8]
+    r.small_send[5:6] = r.small_own[10:11]
+    r.small_send[6:8] = r.small_own[8:10]
+    small_copies = spread(r.small_send, r.small_plane, plane)
+    finish(cot_copies)
+    others = 3 * count
+    cot_others = r.cot_all[...].reshape(others, width)
+    r.cot_turned[:, :count] = dot_nt(r.select[...], r.cotangent[...]).astype(BF16)
+    r.cot_turned[:, count:] = dot_nt(r.select[...], cot_others).astype(BF16)
+    near_piece(2)
+    finish(key_copies)
+    keep_part("key", dot_nn(r.first_flat[...], mixed(256, 384)))
+    key_copies = column_first("key")
+    finish(query_copies)
+    query_copies = column_second("query")
+    finish(far_copies)
+    second_others = r.second_all[...].reshape(others, width)
+    r.second_turned[:, :count] = dot_nt(r.select[...], r.second_low[...]).astype(BF16)
+    r.second_turned[:, count:] = dot_nt(r.select[...], second_others).astype(BF16)
     wide_copies = [wide_piece(0)]
+    finish(value_copies)
+    keep_part("value", dot_nn(r.first_flat[...], mixed(384, 512)))
+    value_copies = column_first("value")
+    wide_copies.append(wide_piece(1))
     finish(rest_copies)
     term = dot_nn(r.first_flat[...], mixed(512, 640))
     for k in range(4):
         upper_half = term[k * rows4 : k * rows4 + rows4 // 2, : local - full]
         lower_half = term[k * rows4 + rows4 // 2 : (k + 1) * rows4, : local - full]
         r.rest_part[k] = jnp.concatenate([upper_half, lower_half], axis=1).astype(BF16)
-    rest_copies = column_first("rest")
-    finish(attended_copies)
-    attended_copies = column_second("attended")
-    finish(query_copies)
-    query_copies = column_second("query")
-    wide_copies.append(wide_piece(1))
+    base = links(3)
+    rest_copies = started(
+        [remote(base + k, r.rest_part.at[heights[k]], r.rest_in.at[k], column[k]) for k in range(3)]
+    )
+    finish(key_copies)
+    key_copies = column_second("key")
     finish(small_copies)
     small_sum = r.small_send[0:6]
     for k in range(3):
@@ -570,31 +607,39 @@
     r.small_z[9:10] = r.small_plane[0, 7:8]
     column_copies = spread(r.small_z, r.small_column, column)
     wide_copies.append(wide_piece(2))
-    finish(pair_copies)
-    pair_copies = column_second("pair")
-    finish(rest_copies)
-    rest_copies = column_second("rest")
+    finish(value_copies)
+    value_copies = column_second("value")
+    finish(attended_copies)
+    finish(resid_copies)
+    keep_part("attended", dot_nn(r.resid_all[...], r.attended_all[...].reshape(tokens4, local)))
+    attended_copies = column_first("attended")
     last_copies = [wide_second(0)]
-    last_copies.append(wide_second(1))
-    finish(attended_copies)
-    r.out_share[...] = column_total("attended")
     finish(query_copies)
     total = column_total("query")
     for k in range(4):
-        r.back_stage[k, :, :128] = total[k * owners : (k + 1) * owners].astype(BF16)
-    last_copies.append(wide_second(2))
-    finish(pair_copies)
-    total = column_total("pair")
-    for k in range(4):
-        r.back_stage[k, :, 128:384] = total[k * owners : (k + 1) * owners].astype(BF16)
+        r.front_stage[k] = total[k * owners : (k + 1) * owners].astype(BF16)
+    r.front_done[spot] = r.front_stage[spot]
+    front_copies = hand_out(r.front_stage, r.front_done)
     finish(rest_copies)
-    total = column_total("rest")
+    total = joined(r.rest_part[z], r.rest_in[0]) + joined(r.rest_in[1], r.rest_in[2])
     for k in range(4):
         lanes = slice(k // 2 * (local - full), (k // 2 + 1) * (local - full))
         rows_here = slice(k % 2 * owners, (k % 2 + 1) * owners)
-        r.back_stage[k, :, 384 : 384 + local - full] = total[rows_here, lanes].astype(BF16)
+        r.back_stage[k, :, 256 : 256 + local - full] = total[rows_here, lanes].astype(BF16)
+    last_copies.append(wide_second(1))
+    finish(key_copies)
+    total = column_total("key")
+    for k in range(4):
+        r.back_stage[k, :, :128] = total[k * owners : (k + 1) * owners].astype(BF16)
+    last_copies.append(wide_second(2))
+    finish(value_copies)
+    total = column_total("value")
+    for k in range(4):
+        r.back_stage[k, :, 128:256] = total[k * owners : (k + 1) * owners].astype(BF16)
     r.back_done[spot] = r.back_stage[spot]
     back_copies = hand_out(r.back_stage, r.back_done)
+    finish(attended_copies)
+    attended_copies = column_second("attended")
     finish(column_copies)
     small_sum = r.small_z[0:6]
     for k in range(3):
@@ -613,15 +658,6 @@
             time_share = time_share + factor * source[6 + line : 7 + line]
     r.time_share[0] = time_share[:, :local]
     r.time_share[1] = time_share[:, local:]
-
-    def wide_total(t):
-        finish(last_copies[t])
-        left = joined(r.wide_a[t, spot], r.wide_a_in[t, 0]) + r.wide_a_last[t].astype(F32)
-        right = joined(r.wide_b[t, spot], r.wide_b_in[t, 0]) + r.wide_b_last[t].astype(F32)
-        for at, total in ((t * step, left), (t * step + part, right)):
-            r.down_share[:, at : at + part] = total[:owners]
-            r.up_share[:, at : at + part] = total[owners:]
-
     wide_total(0)
     wide_total(1)
     finish(small_copies)
@@ -630,16 +666,21 @@
     r.small_sums[3:6] = jnp.where(half == 0, high_half, low_half)
     r.small_sums[6:8] = r.small_half[3:5]
     r.small_sums[8:16] = jnp.broadcast_to(r.small_half[5:6], (8, width))
+    finish(front_copies)
+    for k in range(4):
+        r.in_share[0, :, k * 128 : (k + 1) * 128] = r.front_done[k].astype(F32)
+    finish(attended_copies)
+    r.out_share[...] = column_total("attended")
+    wide_total(2)
     finish(back_copies)
     for k in range(4):
-        piece = slice(k * 128, (k + 1) * 128)
-        for line in range(3):
+        for line in range(2):
             lanes = slice(line * 128, (line + 1) * 128)
-            r.in_share[line, :, piece] = r.back_done[k, :, lanes].astype(F32)
+            share = r.back_done[k, :, lanes].astype(F32)
+            r.in_share[1 + line, :, k * 128 : (k + 1) * 128] = share
         if k > 0:
-            rest = r.back_done[k, :, 384 : 384 + local - full].astype(F32)
+            rest = r.back_done[k, :, 256 : 256 + local - full].astype(F32)
             r.in_share[k - 1, :, full:] = rest
-    wide_total(2)
 
 
 def final_kernel(heads, names, *refs):
@@ -723,24 +764,25 @@
         out_specs=[hbm] * 6 + [vmem] * (len(outs) - 6),
         scratch_shapes=[pltpu.SemaphoreType.DMA((6,))],
         name="final",
-        compiler_params=pltpu.CompilerParams(vmem_limit_bytes=61 * 1024 * 1024),
+        compiler_params=pltpu.CompilerParams(vmem_limit_bytes=8 * 1024 * 1024),
     )(*inputs.values())
     return types.SimpleNamespace(**dict(zip(outs, done, strict=True)))
 
 
-def layer_call(meshed, inputs, smalls, weights):
+def layer_call(meshed, timesteps, inputs, smalls, weights):
     count, width = inputs["tokens"].shape
-    local = weights["out_hbm"].shape[0]
-    hidden = weights["up_hbm"].shape[1]
+    local = weights["out_w"].shape[0]
+    hidden = weights["up_w"].shape[1]
     heads = smalls["bias_table"].shape[0]
     tokens4, rows4 = 4 * count, width // 4
     owners, part = rows4 // 4, hidden // 6
     outs = dict(output=((count, width), BF16), tokens_grad=((count, width), F32))
+    feed_rows = 2 * count if meshed else count
     kept = dict(
         first_low=((count, width), BF16),
         second_low=((count, width), BF16),
-        active_low=((count, hidden), BF16),
-        upper_low=((count, hidden), BF16),
+        active_low=((feed_rows, hidden), BF16),
+        upper_low=((feed_rows, hidden), BF16),
         resid_low=((count, width), BF16),
         attended_low=((count, local), BF16),
         query_low=((count, local), BF16),
@@ -748,12 +790,10 @@
         value_low=((count, local), BF16),
         small_own=((16, width), F32),
     )
-    scratch = dict(
-        time_w=((2 * local, width), BF16),
-        in_w=((3 * local, width), BF16),
-        out_w=((local, width), BF16),
-        up_w=((width, hidden), BF16),
-        down_w=((hidden, width), BF16),
+    loads = inputs | weights
+    scratch = {name: (array.shape, array.dtype) for name, array in loads.items()}
+    scratch |= dict(
+        time_low=((1, width), BF16),
         halo_tokens=((HALO, width), BF16),
         query=((count, local), BF16),
         keys=((KEYS, local), BF16),
@@ -764,6 +804,7 @@
         attended_grad=((count, local), BF16),
         query_grad=((count, local), F32),
         attended=((count, local), F32),
+        active_grad=((count, hidden), F32),
         resid=((count, width), F32),
         part_own=((count, width), F32),
         part_other=((count, width), F32),
@@ -810,14 +851,18 @@
             time_turned=((rows4, 8), F32),
             mixed_all=((4, count, 640), BF16),
             rest=((4, count, 128), BF16),
-            back_stage=((4, owners, 512), BF16),
-            back_done=((4, owners, 512), BF16),
+            rest_part=((4, rows4 // 2, 128), BF16),
+            rest_in=((3, rows4 // 2, 128), BF16),
+            front_stage=((4, owners, 128), BF16),
+            front_done=((4, owners, 128), BF16),
+            back_stage=((4, owners, 384), BF16),
+            back_done=((4, owners, 384), BF16),
         )
         for name, rows, wide in (
             ("attended", owners, local),
             ("query", rows4, 128),
-            ("pair", rows4, 256),
-            ("rest", rows4 // 2, 128),
+            ("key", rows4, 128),
+            ("value", rows4, 128),
         ):
             scratch[name + "_part"] = ((4, rows, wide), BF16)
             scratch[name + "_in"] = ((2, rows, wide), BF16)
@@ -830,32 +875,33 @@
             scratch[name + "_last"] = ((3, 2 * owners, part), BF16)
     else:
         outs |= kept
-    links = 80 if meshed else 6
-    sems = dict(weight_sems=5, send_sems=links, recv_sems=links)
+    links = 96 if meshed else 6
+    sems = dict(load_sems=len(loads | smalls), send_sems=links, recv_sems=links)
     vmem = pl.BlockSpec(memory_space=pltpu.VMEM)
     smem = pl.BlockSpec(memory_space=pltpu.SMEM)
-    anywhere = pl.BlockSpec(memory_space=pl.ANY)
-    names = [*inputs, *smalls, *weights, *outs, *scratch, *sems]
+    hbm = pl.BlockSpec(memory_space=pltpu.HBM)
+    names = [name + "_hbm" for name in (*loads, *smalls)]
+    names = ["step_index", *names, *outs, *smalls, *scratch, *sems]
     results = pl.pallas_call(
-        functools.partial(layer_kernel, names, meshed),
+        functools.partial(layer_kernel, names, [*inputs], [*smalls], [*weights], meshed),
         out_shape=[jax.ShapeDtypeStruct(*shape) for shape in outs.values()],
-        in_specs=[vmem] * len(inputs) + [smem] * len(smalls) + [anywhere] * len(weights),
+        in_specs=[smem] + [hbm] * len(loads | smalls),
         out_specs=[vmem] * len(outs),
-        scratch_shapes=[pltpu.VMEM(*shape) for shape in scratch.values()]
+        scratch_shapes=[pltpu.SMEM(array.shape, array.dtype) for array in smalls.values()]
+        + [pltpu.VMEM(*shape) for shape in scratch.values()]
         + [pltpu.SemaphoreType.DMA((number,)) for number in sems.values()],
         name="layer",
         compiler_params=pltpu.CompilerParams(
-            collective_id=0, has_side_effects=True, vmem_limit_bytes=61 * 1024 * 1024
+            collective_id=0, has_side_effects=True, vmem_limit_bytes=50 * 1024 * 1024
         ),
-    )(*inputs.values(), *smalls.values(), *weights.values())
+    )(
+        timesteps,
+        *[
+            pltpu.with_memory_space_constraint(array, pltpu.HBM)
+            for array in (loads | smalls).values()
+        ],
+    )
     return types.SimpleNamespace(**dict(zip(outs, results, strict=True)))
-
-
-def time_features(timesteps, width):
-    half = width // 2
-    freqs = jnp.exp(jnp.arange(half, dtype=F32) * (-math.log(10000.0) / half))
-    angles = timesteps.astype(F32)[:, None] * freqs[None, :]
-    return jnp.concatenate([jnp.cos(angles), jnp.sin(angles)], axis=1)
 
 
 def on_device(
@@ -881,14 +927,16 @@
     local = project_in.shape[2]
     count = batch * band_rows * columns
     assert batch == 1 and columns == COLS
+    half = width // 2
+    frequencies = np.exp(np.arange(half) * (-math.log(10000.0) / half)).astype(np.float32)
     meshed = lax.axis_size("img") == 8 and lax.axis_size("band") == 2
     cot = cotangent.reshape(count, width)
     inputs = dict(
         tokens=tokens.reshape(count, width),
-        cotangent=cot,
-        time_low=time_features(timesteps, width).astype(BF16),
         first_gain=first_gain,
         first_shift=first_shift,
+        frequencies=jnp.asarray(frequencies),
+        cotangent=cot,
         out_shift=out_shift,
         second_gain=second_gain,
         second_shift=second_shift,
@@ -897,13 +945,13 @@
     )
     smalls = dict(bias_table=bias_table, bias_index=bias_index)
     weights = dict(
-        time_hbm=jnp.transpose(time_weight, (1, 2, 0)).reshape(2 * local, width),
-        in_hbm=jnp.transpose(project_in, (1, 2, 0)).reshape(3 * local, width),
-        out_hbm=project_out,
-        up_hbm=up_weight,
-        down_hbm=down_weight,
-    )
-    r = layer_call(meshed, inputs, smalls, weights)
+        time_w=jnp.transpose(time_weight, (1, 2, 0)).reshape(2 * local, width),
+        in_w=jnp.transpose(project_in, (1, 2, 0)).reshape(3 * local, width),
+        out_w=project_out,
+        up_w=up_weight,
+        down_w=down_weight,
+    )
+    r = layer_call(meshed, timesteps, inputs, smalls, weights)
     heads = bias_table.shape[0]
     if meshed:
         f = final_call(r, heads, up_shift.shape[0])

time: 81.1 us -> 73 us (0.900)
  Pallas kernels: 78.7 us -> 71.4 us
    pallas_call x1, Pallas kernels: 74.4 us -> 69 us  [layer_call(): pl.pallas_call(functools.partial(layer_kernel, names, [*inputs], [*smalls...]
    pallas_call x1, Pallas kernels: 4.33 us -> 2.43 us  [final_call(): pl.pallas_call(functools.partial(final_kernel, heads, [*inputs, *outs, 's...]
where the time goes in v4:
time: 73 us; the launch traced here: 72.9 us
  Pallas kernels  71.4 us (98%)
  between operations  1.47 us (2%)
    pallas_call x1, Pallas kernels, layer_call(): pl.pallas_call(functools.partial(layer_kernel, names, [*inputs], [*smalls...  69 us
    pallas_call x1, Pallas kernels, final_call(): pl.pallas_call(functools.partial(final_kernel, heads, [*inputs, *outs, 's...  2.43 us

profile of v4, /device:TPU:0, one launch (start us, length us, event | category | flops | bytes accessed | tf_op | source)
XLA Modules:
  0.0 72.9 jit_solution(1731678197579152484)
XLA Ops:
  1.3 69.0 %layer.1 = (bf16[128,1152]{1,0:T(8,128)(2,1)S(1)}, f32[128,1152]{1,0:T(8,128)S(1)}, f32[16,1152]{1,0:T(8,128)S(1)}, f32[3,72,576]{2,1,0:T(8,128)S(1)}, f32[2,72,...) custom-call(s32[1]{0:T(128)S(6)} %copy.33.refs_0_, ...), custom_call_target="tpu_custom_call" | custom-call | tf_op jit(solution)/shard_map/layer/pallas_call | solution.py:885
  70.3 2.4 %final.1 = (bf16[128,1152]{1,0:T(8,128)(2,1)}, f32[128,1152]{1,0:T(8,128)}, f32[3,72,576]{2,1,0:T(8,128)}, f32[72,576]{1,0:T(8,128)}, f32[72,2304]{1,0:T(8,128)}...) custom-call(bf16[128,1152]{1,0:T(8,128)(2,1)S(1)} %get-tuple-element, ...), custom_call_target="tpu_custom_call" | custom-call | tf_op jit(solution)/shard_map/final/pallas_call | solution.py:760

commit v5 on v4

--- a/solution.py
+++ b/solution.py
@@ -27,6 +27,8 @@
 F32 = jnp.float32
 GELU_A = math.sqrt(2.0 / math.pi)
 GELU_B = 0.044715
+MARK = 100
+WIDE_TILES = (256, 512, 768, 512, 256)
 TURN = (6.28125, 0.0019350051879882812, 3.019916e-07)
 
 
@@ -240,9 +242,9 @@
         first_copies = spread_half(r.first_low, r.first_all.at[pl.ds(1, 3)], plane)
         rows4 = width // 4
         owners = rows4 // 4
-        place = lax.broadcasted_iota(jnp.int32, (rows4, width), 1)
-        place = place - lax.broadcasted_iota(jnp.int32, (rows4, width), 0)
-        r.select[...] = (place == rows4 * z).astype(F32).astype(BF16)
+        cot_flat = r.time_w.at[:, pl.ds(0, 4 * count)]
+        second_flat = r.time_w.at[:, pl.ds(4 * count, 4 * count)]
+        own_rows = pl.ds(pl.multiple_of(z * rows4, 32), rows4)
     loaded(weight_names[0])
     time_rows = jnp.broadcast_to(r.time_low[...], (8, width))
     time_proj = dot_nt(time_rows, r.time_w[...])[0:1]
@@ -317,6 +319,8 @@
         r.small_half[6:8] = jnp.zeros((2, width), F32)
     loaded(*weight_names[3:], *inputs[8:])
     r.active_grad[...] = dot_nt(r.cotangent[...], r.down_w[...])
+    if meshed:
+        cot_flat[:, :count] = jnp.transpose(r.cotangent[...])
     finish(part_copy)
     after = r.tokens[...].astype(F32) + (r.part_own[...] + r.part_other[...]) + line_of(r.out_shift)
     r.resid[...] = after
@@ -329,6 +333,7 @@
         finish(first_copies)
         first_copies = pass_half(r.first_all, 1, 3)
     step = hidden // 3
+    tiles = WIDE_TILES
     second_sum = None
     for at in range(0, hidden, step):
         piece = slice(at, at + step)
@@ -355,6 +360,7 @@
     if meshed:
         finish(first_copies)
         r.first_flat[...] = jnp.transpose(r.first_all[...].reshape(4 * count, width))
+        second_flat[:, :count] = jnp.transpose(r.second_low[...])
     cot = r.cotangent[...].astype(F32)
     r.small_own[5:6] = column_sum(cot)
     finish(second_copy)
@@ -414,6 +420,10 @@
     r.small_own[10:16] = jnp.zeros((6, width), F32)
     for head in range(heads):
         r.small_own[10:11, head * 128 : (head + 1) * 128] = table_grad[head : head + 1]
+    if meshed:
+        mark = lax.broadcasted_iota(jnp.int32, (1, width), 1) == image * 128 + MARK
+        stamp = jnp.where(band == 0, r.step_index[0], 0).astype(F32)
+        r.small_own[10:11] += jnp.where(mark, stamp, 0.0)
     finish(down_copy)
     lowered = r.down_own[...].astype(F32) + r.down_other[...].astype(F32)
     r.output[...] = (r.resid[...] + lowered + line_of(r.down_shift)).astype(BF16)
@@ -444,6 +454,8 @@
     tokens4 = 4 * count
     if meshed:
         finish(near_copies)
+        cot_flat[:, count : 2 * count] = jnp.transpose(r.cot_all[0])
+        second_flat[:, count : 2 * count] = jnp.transpose(r.second_all[0])
 
         def near_piece(t):
             piece = slice(t * step, (t + 1) * step)
@@ -490,100 +502,118 @@
         )
     r.small_own[8:9, local:] = column_sum(low.astype(F32))
 
-    first_sum = first_sum + dot_nn(r.key_low[...], r.in_w[local : 2 * local])
-    first_sum = first_sum + dot_nn(r.value_low[...], r.in_w[2 * local :])
-    r.first_own[...] = first_sum.astype(BF16)
-    first_copy = sent(r.first_own, r.first_other, sibling)
+    def first_back():
+        total = first_sum + dot_nn(r.key_low[...], r.in_w[local : 2 * local])
+        total = total + dot_nn(r.value_low[...], r.in_w[2 * local :])
+        r.first_own[...] = total.astype(BF16)
+        return sent(r.first_own, r.first_other, sibling)
+
+    def first_norm_back():
+        back = r.first_own[...].astype(F32) + r.first_other[...].astype(F32)
+        r.small_own[0:1] = column_sum(back * unit)
+        r.small_own[1:2] = column_sum(back)
+        r.tokens_grad[...] += normed_back(unit, inv, line_of(r.first_gain), back)
+
+    if not meshed:
+        finish(first_back())
+        first_norm_back()
+        return
 
     def mixed(start, stop):
         return r.mixed_all[:, :, start:stop].reshape(tokens4, stop - start)
 
-    if meshed:
-        finish(query_copies)
-        keep_part("query", dot_nn(r.first_flat[...], mixed(128, 256)))
-        query_copies = column_first("query")
-    if meshed:
-        finish(second_copies[1:])
-        far_copies = pass_half(r.second_all, 1, 2)
-    finish(first_copy)
-    back = r.first_own[...].astype(F32) + r.first_other[...].astype(F32)
-    r.small_own[0:1] = column_sum(back * unit)
-    r.small_own[1:2] = column_sum(back)
-    r.tokens_grad[...] += normed_back(unit, inv, line_of(r.first_gain), back)
-    if not meshed:
-        return
-
-    part = step // 2
     near, far = plane[:2]
+    starts = [sum(tiles[:t]) for t in range(len(tiles))]
+
+    def wide_lanes(t):
+        return pl.ds(starts[t] // 2, tiles[t] // 2)
 
     def wide_first(t):
-        base = links(4)
+        base, lanes = links(4), wide_lanes(t)
         return started(
             [
-                remote(base, r.wide_a.at[t, spots[0]], r.wide_a_in.at[t, 0], near),
-                remote(base + 1, r.wide_a.at[t, spots[2]], r.wide_a_in.at[t, 1], near),
-                remote(base + 2, r.wide_b.at[t, spots[1]], r.wide_b_in.at[t, 0], far),
-                remote(base + 3, r.wide_b.at[t, spots[2]], r.wide_b_in.at[t, 1], far),
+                remote(
+                    base + k,
+                    part.at[target, :, lanes],
+                    arrived.at[k % 2, :, lanes],
+                    near if k < 2 else far,
+                )
+                for k, (part, arrived, target) in enumerate(
+                    (
+                        (r.wide_a, r.wide_a_in, spots[0]),
+                        (r.wide_a, r.wide_a_in, spots[2]),
+                        (r.wide_b, r.wide_b_in, spots[1]),
+                        (r.wide_b, r.wide_b_in, spots[2]),
+                    )
+                )
             ]
         )
 
     def wide_piece(t):
-        piece = slice(t * step, (t + 1) * step)
+        piece, lanes = slice(starts[t], starts[t] + tiles[t]), wide_lanes(t)
         upper = dot_nn(r.second_all[1:].reshape(2 * count, width), r.up_w[:, piece])
         active, slope = gelu_pair(upper + line_of(r.up_shift, piece))
         grad = dot_nt(r.cot_all[1:].reshape(2 * count, width), r.down_w[piece]) * slope
-        down = dot_nn(r.cot_turned[:, : 2 * count], r.active_low[:, piece])
-        down = down + dot_nn(r.cot_turned[:, 2 * count :], active.astype(BF16))
-        up = dot_nn(r.second_turned[:, : 2 * count], r.upper_low[:, piece])
-        up = up + dot_nn(r.second_turned[:, 2 * count :], grad.astype(BF16))
+        down = dot_nn(cot_flat[own_rows, : 2 * count], r.active_low[:, piece])
+        down = down + dot_nn(cot_flat[own_rows, 2 * count :], active.astype(BF16))
+        up = dot_nn(second_flat[own_rows, : 2 * count], r.upper_low[:, piece])
+        up = up + dot_nn(second_flat[own_rows, 2 * count :], grad.astype(BF16))
+        part = tiles[t] // 2
         for k in range(4):
             rows_here = slice(k * owners, (k + 1) * owners)
             both = jnp.concatenate([down[rows_here], up[rows_here]], axis=0).astype(BF16)
-            r.wide_a[t, k] = both[:, :part]
-            r.wide_b[t, k] = both[:, part:]
+            r.wide_a[k, :, lanes] = both[:, :part]
+            r.wide_b[k, :, lanes] = both[:, part:]
         return wide_first(t)
 
     def wide_second(t):
+        lanes = wide_lanes(t)
         finish(wide_copies[t])
-        r.wide_a_sum[t] = joined(r.wide_a[t, spots[1]], r.wide_a_in[t, 1]).astype(BF16)
-        r.wide_b_sum[t] = joined(r.wide_b[t, spots[0]], r.wide_b_in[t, 1]).astype(BF16)
-        return sent(r.wide_a_sum.at[t], r.wide_a_last.at[t], far) + sent(
-            r.wide_b_sum.at[t], r.wide_b_last.at[t], near
+        total = joined(r.wide_a[spots[1], :, lanes], r.wide_a_in[1, :, lanes])
+        r.wide_a_sum[:, lanes] = total.astype(BF16)
+        total = joined(r.wide_b[spots[0], :, lanes], r.wide_b_in[1, :, lanes])
+        r.wide_b_sum[:, lanes] = total.astype(BF16)
+        return sent(r.wide_a_sum.at[:, lanes], r.wide_a_last.at[:, lanes], far) + sent(
+            r.wide_b_sum.at[:, lanes], r.wide_b_last.at[:, lanes], near
         )
 
     def wide_total(t):
         finish(last_copies[t])
-        left = joined(r.wide_a[t, spot], r.wide_a_in[t, 0]) + r.wide_a_last[t].astype(F32)
-        right = joined(r.wide_b[t, spot], r.wide_b_in[t, 0]) + r.wide_b_last[t].astype(F32)
-        for at, total in ((t * step, left), (t * step + part, right)):
-            r.down_share[:, at : at + part] = total[:owners]
-            r.up_share[:, at : at + part] = total[owners:]
-
-    r.small_send[0:3] = jnp.where(half == 0, r.small_own[0:3], r.small_own[3:6])
-    r.small_send[3:5] = r.small_own[6:8]
-    r.small_send[5:6] = r.small_own[10:11]
-    r.small_send[6:8] = r.small_own[8:10]
-    small_copies = spread(r.small_send, r.small_plane, plane)
+        lanes, at = wide_lanes(t), starts[t]
+        for part, arrived, last in (
+            (r.wide_a, r.wide_a_in, r.wide_a_last),
+            (r.wide_b, r.wide_b_in, r.wide_b_last),
+        ):
+            total = joined(part[spot, :, lanes], arrived[0, :, lanes])
+            total = total + last[:, lanes].astype(F32)
+            r.down_share[:, at : at + tiles[t] // 2] = total[:owners]
+            r.up_share[:, at : at + tiles[t] // 2] = total[owners:]
+            at += tiles[t] // 2
+
+    finish(query_copies)
+    keep_part("query", dot_nn(r.first_flat[...], mixed(128, 256)))
+    query_copies = column_first("query")
+    finish(second_copies[1:])
+    far_copies = pass_half(r.second_all, 1, 2)
     finish(cot_copies)
-    others = 3 * count
-    cot_others = r.cot_all[...].reshape(others, width)
-    r.cot_turned[:, :count] = dot_nt(r.select[...], r.cotangent[...]).astype(BF16)
-    r.cot_turned[:, count:] = dot_nt(r.select[...], cot_others).astype(BF16)
+    cot_flat[:, 2 * count :] = jnp.transpose(r.cot_all[1:].reshape(2 * count, width))
     near_piece(2)
     finish(key_copies)
     keep_part("key", dot_nn(r.first_flat[...], mixed(256, 384)))
     key_copies = column_first("key")
+    finish(far_copies)
+    second_flat[:, 2 * count :] = jnp.transpose(r.second_all[1:].reshape(2 * count, width))
+    wide_copies = [wide_piece(0)]
     finish(query_copies)
     query_copies = column_second("query")
-    finish(far_copies)
-    second_others = r.second_all[...].reshape(others, width)
-    r.second_turned[:, :count] = dot_nt(r.select[...], r.second_low[...]).astype(BF16)
-    r.second_turned[:, count:] = dot_nt(r.select[...], second_others).astype(BF16)
-    wide_copies = [wide_piece(0)]
+    wide_copies.append(wide_piece(1))
     finish(value_copies)
     keep_part("value", dot_nn(r.first_flat[...], mixed(384, 512)))
     value_copies = column_first("value")
-    wide_copies.append(wide_piece(1))
+    wide_copies.append(wide_piece(2))
+    first_copy = first_back()
+    finish(key_copies)
+    key_copies = column_second("key")
     finish(rest_copies)
     term = dot_nn(r.first_flat[...], mixed(512, 640))
     for k in range(4):
@@ -594,26 +624,23 @@
     rest_copies = started(
         [remote(base + k, r.rest_part.at[heights[k]], r.rest_in.at[k], column[k]) for k in range(3)]
     )
-    finish(key_copies)
-    key_copies = column_second("key")
-    finish(small_copies)
-    small_sum = r.small_send[0:6]
-    for k in range(3):
-        small_sum = small_sum + r.small_plane[k, 0:6]
-    r.small_z[0:6] = small_sum
-    r.small_z[6:7] = r.small_send[6:7] + r.small_plane[1, 6:7]
-    r.small_z[7:8] = r.small_plane[0, 6:7] + r.small_plane[2, 6:7]
-    r.small_z[8:9] = r.small_send[7:8]
-    r.small_z[9:10] = r.small_plane[0, 7:8]
-    column_copies = spread(r.small_z, r.small_column, column)
-    wide_copies.append(wide_piece(2))
+    wide_copies.append(wide_piece(3))
     finish(value_copies)
     value_copies = column_second("value")
+    wide_copies.append(wide_piece(4))
+    finish(first_copy)
+    first_norm_back()
+    r.small_send[0:3] = jnp.where(half == 0, r.small_own[0:3], r.small_own[3:6])
+    r.small_send[3:5] = r.small_own[6:8]
+    r.small_send[5:6] = r.small_own[10:11]
+    r.small_send[6:8] = jnp.broadcast_to(r.small_own[8:9], (2, width))
+    small_copies = spread(r.small_send, r.small_plane, plane)
+    last_copies = [wide_second(0)]
+    last_copies.append(wide_second(1))
     finish(attended_copies)
     finish(resid_copies)
     keep_part("attended", dot_nn(r.resid_all[...], r.attended_all[...].reshape(tokens4, local)))
     attended_copies = column_first("attended")
-    last_copies = [wide_second(0)]
     finish(query_copies)
     total = column_total("query")
     for k in range(4):
@@ -626,40 +653,54 @@
         lanes = slice(k // 2 * (local - full), (k // 2 + 1) * (local - full))
         rows_here = slice(k % 2 * owners, (k % 2 + 1) * owners)
         r.back_stage[k, :, 256 : 256 + local - full] = total[rows_here, lanes].astype(BF16)
-    last_copies.append(wide_second(1))
+    last_copies.append(wide_second(2))
     finish(key_copies)
     total = column_total("key")
     for k in range(4):
         r.back_stage[k, :, :128] = total[k * owners : (k + 1) * owners].astype(BF16)
-    last_copies.append(wide_second(2))
+    last_copies.append(wide_second(3))
     finish(value_copies)
     total = column_total("value")
     for k in range(4):
         r.back_stage[k, :, 128:256] = total[k * owners : (k + 1) * owners].astype(BF16)
     r.back_done[spot] = r.back_stage[spot]
     back_copies = hand_out(r.back_stage, r.back_done)
+    last_copies.append(wide_second(4))
+    finish(small_copies)
+    small_sum = r.small_send[0:6]
+    for k in range(3):
+        small_sum = small_sum + r.small_plane[k, 0:6]
+    r.small_z[0:6] = small_sum
+    r.small_z[6:7] = r.small_send[6:7] + r.small_plane[1, 6:7]
+    r.small_z[7:8] = r.small_plane[0, 6:7] + r.small_plane[2, 6:7]
+    column_copies = spread(r.small_z, r.small_column, column)
     finish(attended_copies)
     attended_copies = column_second("attended")
+    wide_total(0)
+    wide_total(1)
     finish(column_copies)
     small_sum = r.small_z[0:6]
     for k in range(3):
         small_sum = small_sum + r.small_column[k, 0:6]
     r.small_half[0:6] = small_sum
     small_copies = sent(r.small_half, r.small_other, sibling)
-    time_lines = [r.small_z[8:10]] + [r.small_column[k, 8:10] for k in range(3)]
-    time_lines = jnp.concatenate(time_lines, axis=0).astype(BF16)
-    r.time_turned[...] = dot_nt(r.select[...], time_lines)
-    time_cut = r.time_turned[pl.ds(pl.multiple_of(spot * owners, 8), owners)]
+    steps = [small_sum[5:6, k * 128 + MARK : k * 128 + MARK + 1] for k in range(8)]
+    cosine, sine = cos_sin(jnp.concatenate(steps, axis=0) * line_of(r.frequencies))
+    r.time_lines[:, : width // 2] = cosine.astype(BF16).astype(F32)
+    r.time_lines[:, width // 2 :] = sine.astype(BF16).astype(F32)
+    r.time_flat[...] = jnp.transpose(r.time_lines[...])
+    time_cut = r.time_flat[pl.ds(pl.multiple_of(z * rows4 + spot * owners, 8), owners)]
     time_share = jnp.zeros((owners, width), F32)
     for k in range(4):
         source = r.small_z if k == 0 else r.small_column.at[k - 1]
-        for line in range(2):
-            factor = time_cut[:, 2 * k + line : 2 * k + line + 1]
-            time_share = time_share + factor * source[6 + line : 7 + line]
+        at = z if k == 0 else heights[k - 1]
+        r.time_sums[pl.ds(2 * at + x, 1)] = source[6:7]
+        r.time_sums[pl.ds(2 * at + 1 - x, 1)] = source[7:8]
+    for k in range(8):
+        time_share = time_share + time_cut[:, k : k + 1] * r.time_sums[k : k + 1]
     r.time_share[0] = time_share[:, :local]
     r.time_share[1] = time_share[:, local:]
-    wide_total(0)
-    wide_total(1)
+    wide_total(2)
     finish(small_copies)
     low_half, high_half = r.small_half[0:3], r.small_other[0:3]
     r.small_sums[0:3] = jnp.where(half == 0, low_half, high_half)
@@ -671,7 +712,7 @@
         r.in_share[0, :, k * 128 : (k + 1) * 128] = r.front_done[k].astype(F32)
     finish(attended_copies)
     r.out_share[...] = column_total("attended")
-    wide_total(2)
+    wide_total(3)
     finish(back_copies)
     for k in range(4):
         for line in range(2):
@@ -681,6 +722,7 @@
         if k > 0:
             rest = r.back_done[k, :, 256 : 256 + local - full].astype(F32)
             r.in_share[k - 1, :, full:] = rest
+    wide_total(4)
 
 
 def final_kernel(heads, names, *refs):
@@ -775,7 +817,7 @@
     hidden = weights["up_w"].shape[1]
     heads = smalls["bias_table"].shape[0]
     tokens4, rows4 = 4 * count, width // 4
-    owners, part = rows4 // 4, hidden // 6
+    owners = rows4 // 4
     outs = dict(output=((count, width), BF16), tokens_grad=((count, width), F32))
     feed_rows = 2 * count if meshed else count
     kept = dict(
@@ -839,16 +881,15 @@
             resid_turned=((width, count), F32),
             resid_stage=((4, rows4, count), BF16),
             resid_all=((rows4, tokens4), BF16),
-            select=((rows4, width), BF16),
-            cot_turned=((rows4, tokens4), BF16),
-            second_turned=((rows4, tokens4), BF16),
             small_send=((8, width), F32),
             small_plane=((3, 8, width), F32),
-            small_z=((10, width), F32),
-            small_column=((3, 10, width), F32),
+            small_z=((8, width), F32),
+            small_column=((3, 8, width), F32),
+            time_sums=((8, width), F32),
+            time_lines=((8, width), F32),
             small_half=((8, width), F32),
             small_other=((8, width), F32),
-            time_turned=((rows4, 8), F32),
+            time_flat=((width, 8), F32),
             mixed_all=((4, count, 640), BF16),
             rest=((4, count, 128), BF16),
             rest_part=((4, rows4 // 2, 128), BF16),
@@ -869,13 +910,13 @@
             scratch[name + "_sum"] = ((rows, wide), BF16)
             scratch[name + "_last"] = ((rows, wide), BF16)
         for name in ("wide_a", "wide_b"):
-            scratch[name] = ((3, 4, 2 * owners, part), BF16)
-            scratch[name + "_in"] = ((3, 2, 2 * owners, part), BF16)
-            scratch[name + "_sum"] = ((3, 2 * owners, part), BF16)
-            scratch[name + "_last"] = ((3, 2 * owners, part), BF16)
+            scratch[name] = ((4, 2 * owners, hidden // 2), BF16)
+            scratch[name + "_in"] = ((2, 2 * owners, hidden // 2), BF16)
+            scratch[name + "_sum"] = ((2 * owners, hidden // 2), BF16)
+            scratch[name + "_last"] = ((2 * owners, hidden // 2), BF16)
     else:
         outs |= kept
-    links = 96 if meshed else 6
+    links = 112 if meshed else 6
     sems = dict(load_sems=len(loads | smalls), send_sems=links, recv_sems=links)
     vmem = pl.BlockSpec(memory_space=pltpu.VMEM)
     smem = pl.BlockSpec(memory_space=pltpu.SMEM)

time: 73 us -> 71.8 us (0.984)
  Pallas kernels: 71.4 us -> 70.2 us
    pallas_call x1, Pallas kernels: 69 us -> 67.8 us  [layer_call(): pl.pallas_call(functools.partial(layer_kernel, names, [*inputs], [*smalls...]
where the time goes in v5:
time: 71.8 us; the launch traced here: 71.7 us
  Pallas kernels  70.2 us (98%)
  between operations  1.47 us (2%)
    pallas_call x1, Pallas kernels, layer_call(): pl.pallas_call(functools.partial(layer_kernel, names, [*inputs], [*smalls...  67.8 us
    pallas_call x1, Pallas kernels, final_call(): pl.pallas_call(functools.partial(final_kernel, heads, [*inputs, *outs, 's...  2.43 us

profile of v5, /device:TPU:0, one launch (start us, length us, event | category | flops | bytes accessed | tf_op | source)
XLA Modules:
  0.0 71.7 jit_solution(3519916781070812355)
XLA Ops:
  1.3 67.8 %layer.1 = (bf16[128,1152]{1,0:T(8,128)(2,1)S(1)}, f32[128,1152]{1,0:T(8,128)S(1)}, f32[16,1152]{1,0:T(8,128)S(1)}, f32[3,72,576]{2,1,0:T(8,128)S(1)}, f32[2,72,...) custom-call(s32[1]{0:T(128)S(6)} %copy.33.refs_0_, ...), custom_call_target="tpu_custom_call" | custom-call | tf_op jit(solution)/shard_map/layer/pallas_call | solution.py:926
  69.1 2.4 %final.1 = (bf16[128,1152]{1,0:T(8,128)(2,1)}, f32[128,1152]{1,0:T(8,128)}, f32[3,72,576]{2,1,0:T(8,128)}, f32[72,576]{1,0:T(8,128)}, f32[72,2304]{1,0:T(8,128)}...) custom-call(bf16[128,1152]{1,0:T(8,128)(2,1)S(1)} %get-tuple-element, ...), custom_call_target="tpu_custom_call" | custom-call | tf_op jit(solution)/shard_map/final/pallas_call | solution.py:802

commit v6 on v5

--- a/solution.py
+++ b/solution.py
@@ -117,7 +117,7 @@
         peers = [sibling, *plane, *column]
 
     loads = {}
-    for name in (*inputs[:4], *small_names, *weight_names[:2], *inputs[4:], *weight_names[2:]):
+    for name in (*inputs[:4], *weight_names[:2], *small_names, *inputs[4:], *weight_names[2:]):
         source, target = getattr(r, name + "_hbm"), getattr(r, name)
         loads[name] = pltpu.make_async_copy(source, target, r.load_sems.at[len(loads)])
         loads[name].start()
@@ -437,18 +437,21 @@
             ]
             r.resid_stage[k] = jnp.concatenate(lines, axis=0).astype(BF16)
         r.resid_all[:, 0:count] = r.resid_stage[0]
-        base = links(3)
-        resid_copies = started(
-            [
-                remote(
-                    base + k,
-                    r.resid_stage.at[k + 1],
-                    r.resid_all.at[:, pl.ds((k + 1) * count, count)],
-                    plane[k],
-                )
-                for k in range(3)
-            ]
-        )
+
+        def resid_send():
+            base = links(3)
+            return started(
+                [
+                    remote(
+                        base + k,
+                        r.resid_stage.at[k + 1],
+                        r.resid_all.at[:, pl.ds((k + 1) * count, count)],
+                        plane[k],
+                    )
+                    for k in range(3)
+                ]
+            )
+
     first_sum = dot_nn(r.query_low[...], r.in_w[0:local])
     unit, inv = normed(r.tokens[...].astype(F32))
     tokens4 = 4 * count
@@ -466,6 +469,7 @@
             r.upper_low[count:, piece] = grad.astype(BF16)
 
         near_piece(0)
+        resid_copies = resid_send()
         near_piece(1)
     finish(halo_copy)
     if meshed:
@@ -698,15 +702,21 @@
         r.time_sums[pl.ds(2 * at + 1 - x, 1)] = source[7:8]
     for k in range(8):
         time_share = time_share + time_cut[:, k : k + 1] * r.time_sums[k : k + 1]
-    r.time_share[0] = time_share[:, :local]
-    r.time_share[1] = time_share[:, local:]
+    for k in range(2):
+        r.time_share[:, k, :] = time_share[:, k * local : (k + 1) * local]
     wide_total(2)
     finish(small_copies)
     low_half, high_half = r.small_half[0:3], r.small_other[0:3]
-    r.small_sums[0:3] = jnp.where(half == 0, low_half, high_half)
-    r.small_sums[3:6] = jnp.where(half == 0, high_half, low_half)
-    r.small_sums[6:8] = r.small_half[3:5]
-    r.small_sums[8:16] = jnp.broadcast_to(r.small_half[5:6], (8, width))
+    mixed_low = jnp.where(half == 0, low_half, high_half)
+    mixed_high = jnp.where(half == 0, high_half, low_half)
+    for line, target in enumerate((r.first_gain_grad, r.first_shift_grad, r.out_shift_grad)):
+        target[...] = mixed_low[line]
+    for line, target in enumerate((r.second_gain_grad, r.second_shift_grad, r.down_shift_grad)):
+        target[...] = mixed_high[line]
+    for line in range(hidden // width):
+        r.up_shift_grad[line * width : (line + 1) * width] = r.small_half[3 + line]
+    for head in range(heads):
+        r.bias_grad[head : head + 1] = r.small_half[5:6, head * 128 : head * 128 + TAPS]
     finish(front_copies)
     for k in range(4):
         r.in_share[0, :, k * 128 : (k + 1) * 128] = r.front_done[k].astype(F32)
@@ -725,90 +735,30 @@
     wide_total(4)
 
 
-def final_kernel(heads, names, *refs):
-    r = types.SimpleNamespace(**dict(zip(names, refs, strict=True)))
+def final_kernel(*refs):
+    sems = refs[-1]
+    number = (len(refs) - 1) // 2
     copies = [
-        pltpu.make_async_copy(source, target, r.sems.at[i])
-        for i, (source, target) in enumerate(
-            (
-                (r.output, r.output_done),
-                (r.tokens_grad, r.tokens_done),
-                (r.in_share, r.in_done),
-                (r.out_share, r.out_done),
-                (r.up_share, r.up_done),
-                (r.down_share, r.down_done),
-            )
-        )
+        pltpu.make_async_copy(refs[k], refs[number + k], sems.at[k]) for k in range(number)
     ]
     for copy in copies:
         copy.start()
-    width = r.small_sums.shape[1]
-    for line, target in enumerate(
-        (
-            r.first_gain_done,
-            r.first_shift_done,
-            r.out_shift_done,
-            r.second_gain_done,
-            r.second_shift_done,
-            r.down_shift_done,
-        )
-    ):
-        target[...] = r.small_sums[line]
-    for line in range(r.up_shift_done.shape[0] // width):
-        r.up_shift_done[line * width : (line + 1) * width] = r.small_sums[6 + line]
-    for head in range(heads):
-        r.bias_done[head : head + 1] = r.small_sums[8:9, head * 128 : head * 128 + TAPS]
-    local = r.time_share.shape[2]
-    for k in range(2):
-        r.time_done[:, k, :] = r.time_share[k]
     for copy in copies:
         copy.wait()
 
 
-def final_call(results, heads, hidden):
-    inputs = dict(
-        output=results.output,
-        tokens_grad=results.tokens_grad,
-        in_share=results.in_share,
-        out_share=results.out_share,
-        up_share=results.up_share,
-        down_share=results.down_share,
-        small_sums=results.small_sums,
-        time_share=results.time_share,
-    )
-    width = results.small_sums.shape[1]
-    _, owners, local = results.time_share.shape
-    struct = jax.ShapeDtypeStruct
-    line = struct((width,), F32)
-    outs = dict(
-        output_done=struct(results.output.shape, BF16),
-        tokens_done=struct(results.tokens_grad.shape, F32),
-        in_done=struct(results.in_share.shape, F32),
-        out_done=struct(results.out_share.shape, F32),
-        up_done=struct(results.up_share.shape, F32),
-        down_done=struct(results.down_share.shape, F32),
-        first_gain_done=line,
-        first_shift_done=line,
-        out_shift_done=line,
-        second_gain_done=line,
-        second_shift_done=line,
-        down_shift_done=line,
-        up_shift_done=struct((hidden,), F32),
-        bias_done=struct((heads, TAPS), F32),
-        time_done=struct((owners, 2, local), F32),
-    )
-    vmem = pl.BlockSpec(memory_space=pltpu.VMEM)
-    hbm = pl.BlockSpec(memory_space=pltpu.HBM)
+def final_call(results):
+    arrays = list(vars(results).values())
     done = pl.pallas_call(
-        functools.partial(final_kernel, heads, [*inputs, *outs, "sems"]),
-        out_shape=list(outs.values()),
-        in_specs=[vmem] * 8,
-        out_specs=[hbm] * 6 + [vmem] * (len(outs) - 6),
-        scratch_shapes=[pltpu.SemaphoreType.DMA((6,))],
+        final_kernel,
+        out_shape=[jax.ShapeDtypeStruct(array.shape, array.dtype) for array in arrays],
+        in_specs=[pl.BlockSpec(memory_space=pltpu.VMEM)] * len(arrays),
+        out_specs=[pl.BlockSpec(memory_space=pltpu.HBM)] * len(arrays),
+        scratch_shapes=[pltpu.SemaphoreType.DMA((len(arrays),))],
         name="final",
         compiler_params=pltpu.CompilerParams(vmem_limit_bytes=8 * 1024 * 1024),
-    )(*inputs.values())
-    return types.SimpleNamespace(**dict(zip(outs, done, strict=True)))
+    )(*arrays)
+    return types.SimpleNamespace(**dict(zip(vars(results), done, strict=True)))
 
 
 def layer_call(meshed, timesteps, inputs, smalls, weights):
@@ -864,9 +814,16 @@
     )
     if meshed:
         outs |= dict(
-            small_sums=((16, width), F32),
+            first_gain_grad=((width,), F32),
+            first_shift_grad=((width,), F32),
+            out_shift_grad=((width,), F32),
+            second_gain_grad=((width,), F32),
+            second_shift_grad=((width,), F32),
+            down_shift_grad=((width,), F32),
+            up_shift_grad=((hidden,), F32),
+            bias_grad=((heads, TAPS), F32),
             in_share=((3, owners, local), F32),
-            time_share=((2, owners, local), F32),
+            time_share=((owners, 2, local), F32),
             out_share=((owners, local), F32),
             up_share=((owners, hidden), F32),
             down_share=((owners, hidden), F32),
@@ -995,23 +952,23 @@
     r = layer_call(meshed, timesteps, inputs, smalls, weights)
     heads = bias_table.shape[0]
     if meshed:
-        f = final_call(r, heads, up_shift.shape[0])
+        f = final_call(r)
         return (
-            f.output_done.reshape(tokens.shape),
-            f.tokens_done.reshape(tokens.shape),
-            f.first_gain_done,
-            f.first_shift_done,
-            jnp.transpose(f.in_done, (1, 0, 2)),
-            f.time_done,
-            f.bias_done,
-            jnp.transpose(f.out_done),
-            f.out_shift_done,
-            f.second_gain_done,
-            f.second_shift_done,
-            f.up_done,
-            f.up_shift_done,
-            jnp.transpose(f.down_done),
-            f.down_shift_done,
+            f.output.reshape(tokens.shape),
+            f.tokens_grad.reshape(tokens.shape),
+            f.first_gain_grad,
+            f.first_shift_grad,
+            jnp.transpose(f.in_share, (1, 0, 2)),
+            f.time_share,
+            f.bias_grad,
+            jnp.transpose(f.out_share),
+            f.out_shift_grad,
+            f.second_gain_grad,
+            f.second_shift_grad,
+            f.up_share,
+            f.up_shift_grad,
+            jnp.transpose(f.down_share),
+            f.down_shift_grad,
         )
     axes = ("img", "band")
     grads = (

time: 71.8 us -> 70.9 us (0.987)
  Pallas kernels: 70.2 us -> 69.2 us
where the time goes in v6:
time: 70.9 us; the launch traced here: 70.7 us
  Pallas kernels  69.2 us (98%)
  between operations  1.47 us (2%)
    pallas_call x1, Pallas kernels, layer_call(): pl.pallas_call(functools.partial(layer_kernel, names, [*inputs], [*smalls...  67.3 us
    pallas_call x1, Pallas kernels, final_call(): pl.pallas_call(final_kernel, out_shape=[jax.ShapeDtypeStruct(array.shape,...  1.9 us

profile of v6, /device:TPU:0, one launch (start us, length us, event | category | flops | bytes accessed | tf_op | source)
XLA Modules:
  0.0 70.7 jit_solution(11336671254792209860)
XLA Ops:
  1.3 67.3 %layer.1 = (bf16[128,1152]{1,0:T(8,128)(2,1)S(1)}, f32[128,1152]{1,0:T(8,128)S(1)}, f32[1152]{0:T(1024)S(1)}, f32[1152]{0:T(1024)S(1)}, f32[1152]{0:T(1024)S(1)}...) custom-call(s32[1]{0:T(128)S(6)} %copy.33.refs_0_, ...), custom_call_target="tpu_custom_call" | custom-call | tf_op jit(solution)/shard_map/layer/pallas_call | solution.py:883
  68.7 1.9 %final.1 = (bf16[128,1152]{1,0:T(8,128)(2,1)}, f32[128,1152]{1,0:T(8,128)}, f32[1152]{0:T(1024)}, f32[1152]{0:T(1024)}, f32[1152]{0:T(1024)}, /*index=5*/f32[115...) custom-call(bf16[128,1152]{1,0:T(8,128)(2,1)S(1)} %get-tuple-element, ...), custom_call_target="tpu_custom_call" | custom-call | tf_op jit(solution)/shard_map/final/pallas_call | solution.py:752

commit v7 on v6

--- a/solution.py
+++ b/solution.py
@@ -597,11 +597,11 @@
     finish(query_copies)
     keep_part("query", dot_nn(r.first_flat[...], mixed(128, 256)))
     query_copies = column_first("query")
+    near_piece(2)
     finish(second_copies[1:])
     far_copies = pass_half(r.second_all, 1, 2)
     finish(cot_copies)
     cot_flat[:, 2 * count :] = jnp.transpose(r.cot_all[1:].reshape(2 * count, width))
-    near_piece(2)
     finish(key_copies)
     keep_part("key", dot_nn(r.first_flat[...], mixed(256, 384)))
     key_copies = column_first("key")
@@ -631,7 +631,6 @@
     wide_copies.append(wide_piece(3))
     finish(value_copies)
     value_copies = column_second("value")
-    wide_copies.append(wide_piece(4))
     finish(first_copy)
     first_norm_back()
     r.small_send[0:3] = jnp.where(half == 0, r.small_own[0:3], r.small_own[3:6])
@@ -639,6 +638,7 @@
     r.small_send[5:6] = r.small_own[10:11]
     r.small_send[6:8] = jnp.broadcast_to(r.small_own[8:9], (2, width))
     small_copies = spread(r.small_send, r.small_plane, plane)
+    wide_copies.append(wide_piece(4))
     last_copies = [wide_second(0)]
     last_copies.append(wide_second(1))
     finish(attended_copies)
@@ -662,6 +662,14 @@
     total = column_total("key")
     for k in range(4):
         r.back_stage[k, :, :128] = total[k * owners : (k + 1) * owners].astype(BF16)
+    finish(small_copies)
+    small_sum = r.small_send[0:6]
+    for k in range(3):
+        small_sum = small_sum + r.small_plane[k, 0:6]
+    r.small_z[0:6] = small_sum
+    r.small_z[6:7] = r.small_send[6:7] + r.small_plane[1, 6:7]
+    r.small_z[7:8] = r.small_plane[0, 6:7] + r.small_plane[2, 6:7]
+    column_copies = spread(r.small_z, r.small_column, column)
     last_copies.append(wide_second(3))
     finish(value_copies)
     total = column_total("value")
@@ -670,14 +678,6 @@
     r.back_done[spot] = r.back_stage[spot]
     back_copies = hand_out(r.back_stage, r.back_done)
     last_copies.append(wide_second(4))
-    finish(small_copies)
-    small_sum = r.small_send[0:6]
-    for k in range(3):
-        small_sum = small_sum + r.small_plane[k, 0:6]
-    r.small_z[0:6] = small_sum
-    r.small_z[6:7] = r.small_send[6:7] + r.small_plane[1, 6:7]
-    r.small_z[7:8] = r.small_plane[0, 6:7] + r.small_plane[2, 6:7]
-    column_copies = spread(r.small_z, r.small_column, column)
     finish(attended_copies)
     attended_copies = column_second("attended")
     wide_total(0)

time: 70.9 us -> 70.8 us (level)
  no operation moved by 1% of the time
where the time goes in v7:
time: 70.8 us; the launch traced here: 70.6 us
  Pallas kernels  69.2 us (98%)
  between operations  1.47 us (2%)
    pallas_call x1, Pallas kernels, layer_call(): pl.pallas_call(functools.partial(layer_kernel, names, [*inputs], [*smalls...  67.3 us
    pallas_call x1, Pallas kernels, final_call(): pl.pallas_call(final_kernel, out_shape=[jax.ShapeDtypeStruct(array.shape,...  1.9 us

profile of v7, /device:TPU:0, one launch (start us, length us, event | category | flops | bytes accessed | tf_op | source)
XLA Modules:
  0.0 70.6 jit_solution(14007172751961515795)
XLA Ops:
  1.3 67.3 %layer.1 = (bf16[128,1152]{1,0:T(8,128)(2,1)S(1)}, f32[128,1152]{1,0:T(8,128)S(1)}, f32[1152]{0:T(1024)S(1)}, f32[1152]{0:T(1024)S(1)}, f32[1152]{0:T(1024)S(1)}...) custom-call(s32[1]{0:T(128)S(6)} %copy.33.refs_0_, ...), custom_call_target="tpu_custom_call" | custom-call | tf_op jit(solution)/shard_map/layer/pallas_call | solution.py:883
  68.6 1.9 %final.1 = (bf16[128,1152]{1,0:T(8,128)(2,1)}, f32[128,1152]{1,0:T(8,128)}, f32[1152]{0:T(1024)}, f32[1152]{0:T(1024)}, f32[1152]{0:T(1024)}, /*index=5*/f32[115...) custom-call(bf16[128,1152]{1,0:T(8,128)(2,1)S(1)} %get-tuple-element, ...), custom_call_target="tpu_custom_call" | custom-call | tf_op jit(solution)/shard_map/final/pallas_call | solution.py:752
